TPU v7x, 32 devices: a whole 2x2x4 slice. The times are simulated.
32 devices in a mesh: parts: 2 (over y), row: 8 (over z, core), col: 2 (over x), ch: 1.
Axes of the slice: x: 2, y: 2, z: 4, core: 2. Of those that a mesh axis runs over, the one named last changes fastest.
Arguments:
- z_trunk: bfloat16 [128, 64, 128], P(('parts', 'row'), ('col', 'ch')), parts along dimension 0, may hold values from -6 to 6
- single: bfloat16 [128, 384], P('parts'), parts along dimension 0, may hold values from -6 to 6
- atom_coords: float32 [3, 512], P(None, ('parts', 'row', 'col', 'ch')), parts along dimension 1, may hold values from -48 to 48
- atom_single: bfloat16 [512, 128], P(('parts', 'row', 'col', 'ch')), parts along dimension 0, may hold values from -6 to 6
- rep_atom: int32 [128], P('parts'), parts along dimension 0, may hold values from 0 to 255
- atom_token: int32 [512], P(('parts', 'row', 'col', 'ch')), parts along dimension 0, may hold values from 0 to 63
- token_mask: int32 [128], P('parts'), parts along dimension 0, may hold values from 0 to 1, as said below
- chain_id: int32 [128], P('parts'), parts along dimension 0, may hold values from 0 to 5, never falling along the last dimension, each value on 1 to 32 neighbouring positions
- w_left: bfloat16 [384, 128], replicated, may hold values from -0.3125 to 0.3125
- w_right: bfloat16 [384, 128], replicated, may hold values from -0.3125 to 0.3125
- w_dist: bfloat16 [39, 128], replicated, may hold values from -4 to 4
- tri_in: bfloat16 [128, 640], replicated, may hold values from -0.5 to 0.5
- tri_out: bfloat16 [128, 128], replicated, may hold values from -0.5 to 0.5
- pae_w: bfloat16 [128, 64], replicated, may hold values from -30 to 30
- pool_w: bfloat16 [128, 384], replicated, may hold values from -0.5 to 0.5
- plddt_w: bfloat16 [384, 50], replicated, may hold values from -30 to 30
- atom_w: bfloat16 [128, 50], replicated, may hold values from -0.5 to 0.5
Outputs:
- aligned_error: float32 [128, 64], P(('parts', 'row'), ('col', 'ch')), parts along dimension 0
- interface_score: float32 [128], P(('parts', 'row')), parts along dimension 0
- atom_confidence: float32 [512], P(('parts', 'row', 'col', 'ch')), parts along dimension 0
There are 2 independent parts, one for each index of `parts`. A program takes and returns all parts, laid end to end along the dimension named above; an argument that names none is the same for every part. Nothing has to cross between parts.
Inputs may be any that keep to these rules, and one draw needn't show every extreme that they name: `token_mask`: the real tokens form a prefix of 32 tokens or more. `chain_id`: never falls from one token to the next.
All inputs are finite; a program needn't handle non-finite values.
Results may differ from a plain program's by a relative error of at most 0.013.
Values may be sent and summed in bfloat16 or wider, within the bound.
No kernel may reach another device: no remote copies, remote signals or barrier semaphores. Data moves between devices by JAX's collectives and lax.ppermute only.
A program may use at most 64 MiB of HBM per device.

v0:
```python
import jax
import jax.numpy as jnp
from jax import lax
from jax.sharding import PartitionSpec as P

EPSILON = 1e-05


def layer_norm(values):
    center = values - jnp.mean(values, axis=-1, keepdims=True)
    spread = jnp.mean(center * center, axis=-1, keepdims=True)
    return center * lax.rsqrt(spread + EPSILON)


def distance_basis(distance, count):
    step_size = 18.0 / (count - 1)
    centers = 3.375 + step_size * jnp.arange(count, dtype=jnp.float32)
    scaled = (distance[..., None] - centers) / step_size
    return jnp.exp(-scaled * scaled)


def bin_average(logits, centers):
    probability = jax.nn.softmax(logits, axis=-1)
    return jnp.sum(probability * centers, axis=-1)


def per_device(
    z_trunk,
    single,
    atom_coords,
    atom_single,
    rep_atom,
    atom_token,
    token_mask,
    chain_id,
    w_left,
    w_right,
    w_dist,
    tri_in,
    tri_out,
    pae_w,
    pool_w,
    plddt_w,
    atom_w,
):
    tile_rows, tile_cols, pair_width = z_trunk.shape
    tokens = single.shape[0]
    col_index = lax.axis_index("col") * lax.axis_size("ch") + lax.axis_index("ch")
    row_start = lax.axis_index("row") * tile_rows
    col_start = col_index * tile_cols
    wanted = jnp.concatenate(
        [
            lax.dynamic_slice_in_dim(rep_atom, row_start, tile_rows),
            lax.dynamic_slice_in_dim(rep_atom, col_start, tile_cols),
        ]
    )
    shard_piece = lax.all_gather(atom_coords, ("row", "col", "ch"), axis=1, tiled=True)
    places = lax.iota(jnp.int32, shard_piece.shape[1])
    selector = (places[:, None] == wanted[None, :]).astype(jnp.float32)
    coords = jnp.dot(
        shard_piece, selector, precision=lax.Precision.HIGHEST, preferred_element_type=jnp.float32
    )
    offset = coords[:, :tile_rows, None] - coords[:, None, tile_rows:]
    distance = jnp.sqrt(jnp.sum(offset * offset, axis=0))
    basis_count = w_dist.shape[0]
    radial_basis = distance_basis(distance, basis_count).astype(jnp.bfloat16)
    embedded = jnp.dot(
        radial_basis.reshape(-1, basis_count), w_dist, preferred_element_type=jnp.float32
    ).reshape(tile_rows, tile_cols, pair_width)
    row_single = lax.dynamic_slice_in_dim(single, row_start, tile_rows)
    col_single = lax.dynamic_slice_in_dim(single, col_start, tile_cols)
    from_rows = jnp.dot(row_single, w_left, preferred_element_type=jnp.float32)
    from_cols = jnp.dot(col_single, w_right, preferred_element_type=jnp.float32)
    pair_rep = (
        z_trunk.astype(jnp.float32) + from_rows[:, None, :] + from_cols[None, :, :] + embedded
    )
    mask_float = token_mask.astype(jnp.float32)
    row_mask = lax.dynamic_slice_in_dim(mask_float, row_start, tile_rows)
    col_mask = lax.dynamic_slice_in_dim(mask_float, col_start, tile_cols)
    pair_mask = row_mask[:, None] * col_mask[None, :]
    normed = layer_norm(pair_rep).astype(jnp.bfloat16)
    projected = jnp.dot(
        normed.reshape(-1, pair_width), tri_in, preferred_element_type=jnp.float32
    ).reshape(tile_rows, tile_cols, 5 * pair_width)
    left_side = (
        jax.nn.sigmoid(projected[..., 0:pair_width])
        * projected[..., pair_width : 2 * pair_width]
        * pair_mask[..., None]
    ).astype(jnp.bfloat16)
    right_side = (
        jax.nn.sigmoid(projected[..., 2 * pair_width : 3 * pair_width])
        * projected[..., 3 * pair_width : 4 * pair_width]
        * pair_mask[..., None]
    ).astype(jnp.bfloat16)
    gating = jax.nn.sigmoid(projected[..., 4 * pair_width : 5 * pair_width])
    partial_terms = jnp.einsum(
        "ikc,jkc->ijc",
        left_side,
        lax.all_gather(right_side, "row", axis=0, tiled=True),
        preferred_element_type=jnp.float32,
    )
    product_sum = lax.psum_scatter(partial_terms, ("col", "ch"), scatter_dimension=1, tiled=True)
    normed_outer = layer_norm(product_sum).astype(jnp.bfloat16)
    updated = pair_rep + gating * jnp.dot(
        normed_outer.reshape(-1, pair_width), tri_out, preferred_element_type=jnp.float32
    ).reshape(tile_rows, tile_cols, pair_width)
    bins_pae = pae_w.shape[1]
    pae_logits = jnp.dot(
        updated.astype(jnp.bfloat16).reshape(-1, pair_width),
        pae_w,
        preferred_element_type=jnp.float32,
    ).reshape(tile_rows, tile_cols, bins_pae)
    pae_centers = 0.5 * (jnp.arange(bins_pae, dtype=jnp.float32) + 0.5)
    probability = jax.nn.softmax(pae_logits, axis=-1)
    aligned_error = jnp.sum(probability * pae_centers, axis=-1)
    tm_scale = 1.24 * (max(tokens, 19) - 15) ** (1.0 / 3.0) - 1.8
    tm_values = 1.0 / (1.0 + (pae_centers / tm_scale) ** 2)
    tm_pair = jnp.sum(probability * tm_values, axis=-1)
    row_chain = lax.dynamic_slice_in_dim(chain_id, row_start, tile_rows)
    col_chain = lax.dynamic_slice_in_dim(chain_id, col_start, tile_cols)
    interface = pair_mask * (row_chain[:, None] != col_chain[None, :]).astype(jnp.float32)
    numerator_part = jnp.sum(interface * tm_pair, axis=1)
    count_part = jnp.sum(interface, axis=1)
    pooled_part = jnp.sum(col_mask[None, :, None] * updated, axis=1)
    numerator, count_total, pooled = lax.psum(
        (numerator_part, count_part, pooled_part), ("col", "ch")
    )
    interface_score = numerator / jnp.maximum(count_total, 1.0)
    pooled = pooled / jnp.sum(mask_float)
    single_new = row_single.astype(jnp.float32) + jnp.dot(
        pooled.astype(jnp.bfloat16), pool_w, preferred_element_type=jnp.float32
    )
    single_norm = layer_norm(single_new).astype(jnp.bfloat16)
    bins_plddt = plddt_w.shape[1]
    shard_piece = lax.all_gather(single_norm, "row", axis=0, tiled=True)
    places = lax.iota(jnp.int32, shard_piece.shape[0])
    selector = (atom_token[:, None] == places[None, :]).astype(jnp.bfloat16)
    picked = jnp.dot(selector, shard_piece, preferred_element_type=jnp.float32)
    atom_logits = jnp.dot(picked.astype(jnp.bfloat16), plddt_w, preferred_element_type=jnp.float32)
    atom_logits = atom_logits + jnp.dot(atom_single, atom_w, preferred_element_type=jnp.float32)
    plddt_centers = (jnp.arange(bins_plddt, dtype=jnp.float32) + 0.5) / bins_plddt
    atom_confidence = bin_average(atom_logits, plddt_centers)
    return (aligned_error, interface_score, atom_confidence)


def solution(mesh):
    placed = (
        P(("parts", "row"), ("col", "ch"), None),
        P("parts", None),
        P(None, ("parts", "row", "col", "ch")),
        P(("parts", "row", "col", "ch"), None),
        P("parts"),
        P(("parts", "row", "col", "ch")),
        P("parts"),
        P("parts"),
        P(),
        P(),
        P(),
        P(),
        P(),
        P(),
        P(),
        P(),
        P(),
    )
    return jax.shard_map(
        per_device,
        mesh=mesh,
        in_specs=placed,
        out_specs=(
            P(("parts", "row"), ("col", "ch")),
            P(("parts", "row")),
            P(("parts", "row", "col", "ch")),
        ),
        check_vma=False,
    )
```

profile of v0, /device:TPU:0, one launch (start us, length us, event | category | flops | bytes accessed | tf_op | source)
XLA Modules:
  0.0 114.9 jit_solution(4880533692368617881)
XLA Ops:
  7.2 0.0 copy-start
  7.2 0.0 reduce-scatter.2.cloned.1.call-start
  7.2 0.7 dynamic_slice.26
  8.0 0.7 dynamic_slice.27
  8.7 0.7 convert_element_type.44
  9.4 0.1 dynamic_slice.28
  9.4 0.1 dynamic_slice.29
  9.5 34.2 %all-gather = f32[16,16,3]{1,2,0:T(4,128)S(1)} all-gather(f32[1,16,3]{1,2,0:T(4,128)} %bitcast.42), channel_id=1, replica_groups=mesh['parts'=2,'row'=8,'col'=2,'ch'=1] {'row','col','ch'}, dimensions={0}, use_global_device_ids=true | all-gather | bytes 3264 | tf_op jit(solution)/shard_map/all_gather | solution.py:57
  43.7 0.1 reshape.134
  43.8 0.1 pad_add_fusion
  43.9 0.2 convolution_bitcast_fusion.1
  44.0 0.1 slice.22
  44.1 0.1 multiply_reduce_fusion.6
  44.2 1.0 fusion.41
  45.3 1.1 fusion.36
  46.3 1.2 %fusion.52 = (f32[8,32]{1,0:T(8,128)S(1)}, f32[8,32,128]{2,1,0:T(8,128)S(1)}) fusion(bf16[39,128]{1,0:T(8,128)(2,1)} %param.27, f32[39]{0:T(128)S(1)} %multiply_add_fusion, f32[8,32]{1,0:T(8,128)S(1)} %sqrt.7, f32[32,128]{1,0:T(8,128)S(1)} %fusion.36, f32[8,128]{1,0:T(8,128)S(1)} %fusion.41, bf16[8,32,128]{2,1,0:T(8,128)(2,1)} %param.17), kind=kOutput, calls=%fused_computation.93 | convolution fusion | flops 2769408 | bytes 229276 | tf_op jit(solution)/shard_map/dot_general | solution.py:67
  47.5 0.0 copy-start.1
  47.5 0.2 multiply_reduce_fusion.4
  47.7 0.0 copy-done
  47.7 0.3 fusion.8
  48.0 0.1 broadcast_multiply_fusion
  48.1 0.1 fusion.13
  48.2 0.0 copy-done.1
  48.2 14.9 %all_gather.10 = bf16[64,32,128]{2,1,0:T(8,128)(2,1)S(1)} all-gather(bf16[8,32,128]{2,1,0:T(8,128)(2,1)S(1)} %get-tuple-element.11), channel_id=1, replica_groups=mesh['parts'=2,'row'=8,'col'=2,'ch'=1] {'row'}, dimensions={0}, use_global_device_ids=true | all-gather | bytes 589824 | tf_op jit(solution)/shard_map/all_gather | solution.py:99
  63.2 3.0 %copy.51 = bf16[64,32,128]{1,0,2:T(8,128)(2,1)S(1)} copy(bf16[64,32,128]{2,1,0:T(8,128)(2,1)S(1)} %all_gather.10) | data formatting | bytes 1048576 | tf_op jit(solution)/shard_map/all_gather | solution.py:99
  66.2 0.0 copy-start.7
  66.2 0.0 copy-start.8
  66.2 0.0 copy-start.3
  66.2 0.0 copy-start.4
  66.2 0.9 copy.52
  67.1 2.1 %convolution_bitcast_fusion = f32[8,64,128]{1,0,2:T(8,128)S(1)} fusion(bf16[64,32,128]{1,0,2:T(8,128)(2,1)S(1)} %copy.51, bf16[8,32,128]{1,0,2:T(8,128)(2,1)} %copy.52), kind=kOutput, calls=%fused_computation.2 | convolution fusion | flops 4194304 | bytes 851968 | tf_op jit(solution)/shard_map/ikc,jkc->ijc/dot_general | solution.py:96
  69.2 0.9 copy.53
  70.2 0.0 reduce-scatter.2.cloned.1.call-update
  70.2 0.0 copy-done.7
  70.2 0.1 dynamic_slice.30
  70.3 0.1 dynamic_slice.31
  70.4 0.0 copy-done.8
  70.4 0.6 convert_reduce_fusion
  71.0 0.0 copy-done.3
  71.0 0.0 copy-done.4
  71.0 0.1 fusion.63
  71.1 8.4 %reduce-scatter.2.cloned.1.call-done = f32[8,32,128]{2,0,1:T(8,128)} async-done(((f32[8,64,128]{2,0,1:T(8,128)}), f32[8,32,128]{2,0,1:T(8,128)}) %reduce-scatter.2.cloned.1.call-update) | async-done | bytes 131088 | tf_op jit(solution)/shard_map/reduce_scatter | solution.py:102
  79.5 1.0 reduce_sum.147
  80.5 0.1 copy.54
  80.6 0.1 copy.55
  80.7 1.1 multiply_reduce_fusion.3
  81.8 0.1 copy.56
  81.9 0.1 copy.57
  81.9 1.0 multiply_convert_fusion
  83.0 1.1 multiply_reduce_fusion
  84.1 0.0 copy-done.6
  84.1 1.0 multiply_reduce_fusion.1
  85.2 0.2 fusion.45
  85.4 5.0 %all-reduce = (f32[8]{0:T(128)S(1)}, f32[8]{0:T(128)S(1)}, f32[8,128]{1,0:T(8,128)S(1)}) all-reduce(f32[8]{0:T(128)S(1)} %get-tuple-element.6, f32[8]{0:T(128)S(1)} %get-tuple-element.5, f32[8,128]{1,0:T(8,128)S(1)} %get-tuple-element.14), channel_id=1, replica_groups=mesh['parts'=2,'row'=8,'col'=2,'ch'=1] {'col','ch'}, use_global_device_ids=true, to_apply=%region_11.0 | all-reduce | flops 1040 | bytes 8320 | tf_op jit(solution)/shard_map/psum | solution.py:125
  90.4 0.0 copy-done.2
  90.4 1.6 %fusion.53 = (f32[8]{0:T(128)S(1)}, f32[8,384]{1,0:T(8,128)S(1)}) fusion(bf16[128,384]{1,0:T(8,128)(2,1)S(1)} %copy-done.2, f32[8,128]{1,0:T(8,128)S(1)} %get-tuple-element.9, f32[]{:T(128)} %convert_reduce_fusion, bf16[64,384]{1,0:T(8,128)(2,1)} %param.18, s32[]{:T(128)S(6)} %select_n.4), kind=kOutput, calls=%fused_computation.94 | convolution fusion | flops 797688 | bytes 120872 | tf_op jit(solution)/shard_map/dot_general | solution.py:130
  91.9 0.2 multiply_reduce_fusion.5
  92.1 0.1 multiply_convert_fusion.3
  92.2 14.0 %all_gather.11 = bf16[64,384]{1,0:T(8,128)(2,1)S(1)} all-gather(bf16[8,384]{1,0:T(8,128)(2,1)S(1)} %multiply_convert_fusion.3), channel_id=1, replica_groups=mesh['parts'=2,'row'=8,'col'=2,'ch'=1] {'row'}, dimensions={0}, use_global_device_ids=true | all-gather | bytes 55296 | tf_op jit(solution)/shard_map/all_gather | solution.py:135
  106.3 0.0 copy-done.5
  106.3 0.4 fusion.54
  106.7 0.2 fusion.40
  106.9 0.7 multiply_reduce_fusion.7
  107.6 0.5 maximum_divide_fusion
  (16 shorter events, 0.1 us)
Async XLA Ops:
  7.2 40.6 %copy-start = (bf16[128,640]{1,0:T(8,128)(2,1)S(1)}, bf16[128,640]{1,0:T(8,128)(2,1)}, u32[]{:S(2)}) copy-start(bf16[128,640]{1,0:T(8,128)(2,1)} %param.28) | copy-start | bytes 491524
  7.2 72.3 %reduce-scatter.2.cloned.1.call-start = ((), (), s32[]{:S(2)}) async-start(), calls=%async_computation.1 | async-start | bytes 393216 | tf_op jit(solution)/shard_map/reduce_scatter | solution.py:102
  47.5 0.7 copy-start.1
  66.2 4.0 %copy-start.7 = (s32[64]{0:T(128)S(1)}, s32[64]{0:T(128)}, u32[]{:S(2)}) copy-start(s32[64]{0:T(128)} %param.24) | copy-start | bytes 772
  66.2 4.2 %copy-start.8 = (s32[64]{0:T(128)S(1)}, s32[64]{0:T(128)}, u32[]{:S(2)}) copy-start(s32[64]{0:T(128)} %param.23) | copy-start | bytes 772
  66.2 4.8 %copy-start.3 = (bf16[128,50]{0,1:T(8,128)(2,1)S(1)}, bf16[128,50]{0,1:T(8,128)(2,1)}, u32[]{:S(2)}) copy-start(bf16[128,50]{0,1:T(8,128)(2,1)} %param.33) | copy-start | bytes 38404
  66.2 4.8 %copy-start.4 = (bf16[16,128]{1,0:T(8,128)(2,1)S(1)}, bf16[16,128]{1,0:T(8,128)(2,1)}, u32[]{:S(2)}) copy-start(bf16[16,128]{1,0:T(8,128)(2,1)} %param.20) | copy-start | bytes 12292
  67.1 17.0 %copy-start.6 = (bf16[128,64]{0,1:T(8,128)(2,1)S(1)}, bf16[128,64]{0,1:T(8,128)(2,1)}, u32[]{:S(2)}) copy-start(bf16[128,64]{0,1:T(8,128)(2,1)} %param.30) | copy-start | bytes 49156
  69.2 21.2 %copy-start.2 = (bf16[128,384]{1,0:T(8,128)(2,1)S(1)}, bf16[128,384]{1,0:T(8,128)(2,1)}, u32[]{:S(2)}) copy-start(bf16[128,384]{1,0:T(8,128)(2,1)} %param.31) | copy-start | bytes 294916
  69.2 37.1 %copy-start.5 = (bf16[384,50]{0,1:T(8,128)(2,1)S(1)}, bf16[384,50]{0,1:T(8,128)(2,1)}, u32[]{:S(2)}) copy-start(bf16[384,50]{0,1:T(8,128)(2,1)} %param.32) | copy-start | bytes 115204
  69.2 37.1 %copy-start.9 = (s32[16]{0:T(128)S(1)}, s32[16]{0:T(128)}, u32[]{:S(2)}) copy-start(s32[16]{0:T(128)} %param.22) | copy-start | bytes 196
Sparse Core Ops, SparseCore 0:
  70.3 9.1 reduce-scatter.1
where the time goes:
time: 115 us
  blocking collectives  68.2 us (59%)
  between operations  14.2 us (12%)
  matrix products  10.1 us (9%)
  waiting for transfers between devices  8.45 us (7%)
  local copies, waits for them, and re-layouts  7.06 us (6%)
  other arithmetic  6.86 us (6%)
    all_gather x1, blocking collectives, per_device(): lax.all_gather(atom_coords, ('row', 'col', 'ch'), axis=1, tiled=True)  34.2 us
    all_gather x1, blocking collectives, per_device(): lax.all_gather(right_side, 'row', axis=0, tiled=True)  14.9 us
    all_gather x1, blocking collectives, per_device(): shard_piece = lax.all_gather(single_norm, 'row', axis=0, tiled=True)  14 us
    reduce_scatter x1, waiting for transfers between devices, per_device(): lax.psum_scatter(partial_terms, ('col', 'ch'), scatter_dimension=1, tiled...  8.43 us
    psum x1, blocking collectives, per_device(): lax.psum((numerator_part, count_part, pooled_part), ('col', 'ch'))  5 us
    all_gather x1, local copies, waits for them, and re-layouts, per_device(): lax.all_gather(right_side, 'row', axis=0, tiled=True)  2.97 us
  transfers between devices with their start and end apart: 1, of which 1 were waited for; matrix products, arithmetic and copies ran while one was open for 1% of the time, Pallas kernels for 0%

commit v1 on v0

--- a/solution.py
+++ b/solution.py
@@ -1,6 +1,8 @@
 import jax
 import jax.numpy as jnp
 from jax import lax
+from jax.experimental import pallas as pl
+from jax.experimental.pallas import tpu as pltpu
 from jax.sharding import PartitionSpec as P
 
 EPSILON = 1e-05
@@ -143,6 +145,363 @@
     return (aligned_error, interface_score, atom_confidence)
 
 
+WHOLE_PAIR_BYTES = 4 * 1024 * 1024
+VMEM = pl.BlockSpec(memory_space=pltpu.VMEM)
+SMEM = pl.BlockSpec(memory_space=pltpu.SMEM)
+
+
+def sigmoid(values):
+    return 1.0 / (1.0 + jnp.exp(-values))
+
+
+def place_of():
+    row = lax.axis_index("row")
+    return lax.div(row, 2), lax.rem(row, 2), lax.axis_index("col")
+
+
+def token_count(mask_ref):
+    return jnp.sum(mask_ref[...].astype(jnp.float32), axis=1, keepdims=True)
+
+
+def pack_kernel(z_ref, mine_ref, other_ref, out_ref):
+    rows, cols, width = z_ref.shape
+    atoms = mine_ref.shape[1]
+    out_ref[0 : rows * cols, :] = z_ref[...].reshape(rows * cols, width)
+    half = lax.rem(lax.axis_index("row"), 2)
+    for place, ref in ((half, mine_ref), (1 - half, other_ref)):
+        value = ref[...]
+        high = value.astype(jnp.bfloat16).astype(jnp.float32)
+        middle = (value - high).astype(jnp.bfloat16).astype(jnp.float32)
+        low = value - high - middle
+        filler = jnp.zeros((width - 9, atoms), jnp.float32)
+        stacked = jnp.concatenate([high, middle, low, filler], axis=0)
+        start = pl.multiple_of(rows * cols + place * atoms, 16)
+        out_ref[pl.ds(start, atoms), :] = stacked.T.astype(jnp.bfloat16)
+
+
+def edge_kernel(slots, col_count, *refs):
+    packs = refs[: len(slots)]
+    single_ref, rep_ref, mask_ref, w_left_ref, w_right_ref, w_dist_ref, tri_in_ref = refs[
+        len(slots) : len(slots) + 7
+    ]
+    pair_ref, gating_ref, left_ref, right_ref = refs[len(slots) + 7 : len(slots) + 11]
+    xyz_ref, rows_ref, cols_ref, dist_ref = refs[len(slots) + 11 :]
+    _, tile_rows, _, tile_cols, width = pair_ref.shape
+    tokens = single_ref.shape[0]
+    pairs = tile_rows * tile_cols
+    atoms = (packs[0].shape[0] - pairs) // 2
+    basis_count = w_dist_ref.shape[0]
+    chip, half, col = place_of()
+    single = single_ref[...]
+    rows_ref[...] = jnp.dot(single, w_left_ref[...], preferred_element_type=jnp.float32)
+    cols_ref[...] = jnp.dot(single, w_right_ref[...], preferred_element_type=jnp.float32)
+    dist_ref[...] = jnp.zeros_like(dist_ref)
+    dist_ref[0:basis_count, :] = w_dist_ref[...].astype(jnp.float32)
+    w_dist = dist_ref[...].astype(jnp.bfloat16)
+    rep = rep_ref[...]
+    order = lax.broadcasted_iota(jnp.int32, (2 * atoms, tokens), 0)
+    picked = jnp.zeros((tokens, width), jnp.float32)
+    for pack, (chip_step, col_step) in zip(packs, slots):
+        device = 2 * (chip ^ chip_step) * col_count + (col ^ col_step)
+        number = jnp.where(
+            order < atoms, order + device * atoms, order - atoms + (device + col_count) * atoms
+        )
+        chosen = (number == rep).astype(jnp.float32).astype(jnp.bfloat16)
+        picked = picked + lax.dot_general(
+            chosen, pack[pairs:, :], (((0,), (0,)), ((), ())), preferred_element_type=jnp.float32
+        )
+    for axis in range(3):
+        whole = picked[:, axis : axis + 1] + picked[:, axis + 3 : axis + 4]
+        whole = whole + picked[:, axis + 6 : axis + 7]
+        xyz_ref[axis] = jnp.broadcast_to(whole, (tokens, width))
+    count = token_count(mask_ref)
+    step_size = 18.0 / (basis_count - 1)
+    centers = 3.375 + step_size * lax.broadcasted_iota(jnp.int32, (1, 1, width), 2).astype(
+        jnp.float32
+    )
+    row_order = lax.broadcasted_iota(jnp.int32, (tile_rows, tile_cols, width), 0)
+    col_order = lax.broadcasted_iota(jnp.int32, (tile_rows, tile_cols, width), 1)
+    limit = count.astype(jnp.int32).reshape(1, 1, 1)
+    tri_in = tri_in_ref[...]
+    for pack, (chip_step, col_step) in zip(packs, slots):
+        at_chip = chip ^ chip_step
+        at_col = col ^ col_step
+        row_start = pl.multiple_of((2 * at_chip + half) * tile_rows, 8)
+        col_start = pl.multiple_of(at_col * tile_cols, 8)
+        row_slice = pl.ds(row_start, tile_rows)
+        col_slice = pl.ds(col_start, tile_cols)
+        square = jnp.zeros((tile_rows, tile_cols, width), jnp.float32)
+        for axis in range(3):
+            gap = xyz_ref[axis, row_slice, :][:, None, :] - xyz_ref[axis, col_slice, :][None]
+            square = square + gap * gap
+        scaled = (jnp.sqrt(square) - centers) * (1.0 / step_size)
+        basis = jnp.exp(-scaled * scaled).astype(jnp.bfloat16)
+        pair = (
+            pack[0:pairs, :].astype(jnp.float32).reshape(tile_rows, tile_cols, width)
+            + rows_ref[row_slice, :][:, None, :]
+            + cols_ref[col_slice, :][None]
+        )
+        pair = pair.reshape(pairs, width) + jnp.dot(
+            basis.reshape(pairs, width), w_dist, preferred_element_type=jnp.float32
+        )
+        tile = (tile_rows, tile_cols, width)
+        pair_ref[at_chip, :, at_col] = pair.reshape(tile)
+        normed = layer_norm(pair).astype(jnp.bfloat16)
+        projected = jnp.dot(normed, tri_in, preferred_element_type=jnp.float32)
+        real = jnp.where(
+            (row_order + row_start < limit) & (col_order + col_start < limit), 1.0, 0.0
+        )
+        left = sigmoid(projected[:, 0:width]) * projected[:, width : 2 * width]
+        left = (left.reshape(tile) * real).astype(jnp.bfloat16)
+        left_ref[at_chip, :, at_col] = left.astype(jnp.float32)
+        right = sigmoid(projected[:, 2 * width : 3 * width]) * projected[:, 3 * width : 4 * width]
+        right = right.reshape(tile) * real
+        right_ref[at_col, :, at_chip] = jnp.swapaxes(right, 0, 1).astype(jnp.bfloat16)
+        gating_ref[at_chip, :, at_col] = sigmoid(projected[:, 4 * width :]).reshape(tile)
+
+
+def triangle_kernel(
+    tm_scale,
+    left_ref,
+    mine_ref,
+    other_ref,
+    pair_ref,
+    gating_ref,
+    tri_out_ref,
+    pae_w_ref,
+    mask_ref,
+    chain_ref,
+    chain_smem,
+    aligned_ref,
+    interface_ref,
+    pooled_ref,
+    right_ref,
+    updated_ref,
+):
+    chips, tile_rows, col_count, tile_cols, width = pair_ref.shape
+    tokens = col_count * tile_cols
+    chip, half, col = place_of()
+    shape = (tokens, chips, tile_rows, width)
+    right_ref[:, :, half] = mine_ref[...].reshape(shape).astype(jnp.float32)
+    right_ref[:, :, 1 - half] = other_ref[...].reshape(shape).astype(jnp.float32)
+    count = token_count(mask_ref)
+    token_order = lax.broadcasted_iota(jnp.int32, (tokens, width), 0)
+    real = jnp.where(token_order < count.astype(jnp.int32), 1.0, 0.0)
+    tri_out = tri_out_ref[...]
+    block = 4
+    blocks = tile_rows // block
+
+    def rows_of(step, carry):
+        at_chip = lax.div(step, blocks)
+        first = lax.rem(step, blocks) * block
+
+        def add_token(token, sums):
+            key = right_ref[token].reshape(tokens, width)
+            key_col = lax.div(token, tile_cols)
+            key_place = lax.rem(token, tile_cols)
+            return tuple(
+                sums[i] + left_ref[at_chip, first + i, key_col, pl.ds(key_place, 1), :] * key
+                for i in range(block)
+            )
+
+        zero = jnp.zeros((tokens, width), jnp.float32)
+        sums = lax.fori_loop(0, tokens, add_token, (zero,) * block, unroll=8)
+        outer = jnp.concatenate(sums, axis=0)
+        change = jnp.dot(
+            layer_norm(outer).astype(jnp.bfloat16), tri_out, preferred_element_type=jnp.float32
+        )
+        for i in range(block):
+            gating = gating_ref[at_chip, first + i].reshape(tokens, width)
+            updated = pair_ref[at_chip, first + i].reshape(tokens, width) + gating * (
+                change[i * tokens : (i + 1) * tokens]
+            )
+            updated_ref[at_chip, first + i] = updated.astype(jnp.bfloat16)
+            pooled_ref[pl.ds(at_chip * tile_rows + first + i, 1), :] = jnp.sum(
+                updated * real, axis=0, keepdims=True
+            )
+        return carry
+
+    lax.fori_loop(0, chips * blocks, rows_of, 0)
+    bins = pae_w_ref.shape[1]
+    logits = lax.dot_general(
+        pae_w_ref[...],
+        updated_ref[chip].reshape(tile_rows * tokens, width),
+        (((0,), (1,)), ((), ())),
+        preferred_element_type=jnp.float32,
+    )
+    centers = 0.5 * (lax.broadcasted_iota(jnp.int32, (bins, 1), 0).astype(jnp.float32) + 0.5)
+    ratio = centers / tm_scale
+    weight = jnp.exp(logits - jnp.max(logits, axis=0, keepdims=True))
+    total = jnp.sum(weight, axis=0, keepdims=True)
+    error = jnp.sum(weight * centers, axis=0, keepdims=True) / total
+    tm_pair = jnp.sum(weight * (1.0 / (1.0 + ratio * ratio)), axis=0, keepdims=True) / total
+    chains = chain_ref[...]
+    keys = lax.broadcasted_iota(jnp.int32, (1, tokens), 1)
+    limit = count.astype(jnp.int32)
+    places = lax.broadcasted_iota(jnp.int32, (1, tile_rows), 1)
+    scores = jnp.zeros((1, tile_rows), jnp.float32)
+    query = (2 * chip + half) * tile_rows
+    for i in range(tile_rows):
+        span = error[:, i * tokens : (i + 1) * tokens]
+        mine = span[:, 0:tile_cols]
+        for other in range(1, col_count):
+            mine = jnp.where(
+                col == other, span[:, other * tile_cols : (other + 1) * tile_cols], mine
+            )
+        aligned_ref[i : i + 1, :] = mine
+        face = (keys < limit) & (query + i < limit) & (chains != chain_smem[query + i])
+        face = jnp.where(face, 1.0, 0.0)
+        number = jnp.sum(face, axis=1, keepdims=True)
+        score = jnp.sum(face * tm_pair[:, i * tokens : (i + 1) * tokens], axis=1, keepdims=True)
+        scores = jnp.where(places == i, score / jnp.maximum(number, 1.0), scores)
+    interface_ref[...] = scores
+
+
+def atom_kernel(
+    mine_ref,
+    other_ref,
+    single_ref,
+    mask_ref,
+    pool_w_ref,
+    plddt_w_ref,
+    atom_token_ref,
+    atom_single_ref,
+    atom_w_ref,
+    out_ref,
+    pooled_ref,
+):
+    chips, _, tile_rows, width = pooled_ref.shape
+    tokens = single_ref.shape[0]
+    half = lax.rem(lax.axis_index("row"), 2)
+    pooled_ref[:, half] = mine_ref[...].reshape(chips, tile_rows, width)
+    pooled_ref[:, 1 - half] = other_ref[...].reshape(chips, tile_rows, width)
+    pooled = pooled_ref[...].reshape(tokens, width) / token_count(mask_ref)
+    single_new = single_ref[...].astype(jnp.float32) + jnp.dot(
+        pooled.astype(jnp.bfloat16), pool_w_ref[...], preferred_element_type=jnp.float32
+    )
+    single_norm = layer_norm(single_new).astype(jnp.bfloat16)
+    atoms = atom_token_ref.shape[1]
+    order = lax.broadcasted_iota(jnp.int32, (tokens, atoms), 0)
+    chosen = (order == atom_token_ref[...]).astype(jnp.float32).astype(jnp.bfloat16)
+    picked = lax.dot_general(
+        chosen, single_norm, (((0,), (0,)), ((), ())), preferred_element_type=jnp.float32
+    ).astype(jnp.bfloat16)
+    turned = (((0,), (1,)), ((), ()))
+    logits = lax.dot_general(
+        plddt_w_ref[...], picked, turned, preferred_element_type=jnp.float32
+    ) + lax.dot_general(
+        atom_w_ref[...], atom_single_ref[...], turned, preferred_element_type=jnp.float32
+    )
+    bins = logits.shape[0]
+    centers = (lax.broadcasted_iota(jnp.int32, (bins, 1), 0).astype(jnp.float32) + 0.5) / bins
+    weight = jnp.exp(logits - jnp.max(logits, axis=0, keepdims=True))
+    total = jnp.sum(weight, axis=0, keepdims=True)
+    out_ref[...] = jnp.sum(weight * centers, axis=0, keepdims=True) / total
+
+
+def direct(
+    z_trunk,
+    single,
+    atom_coords,
+    atom_single,
+    rep_atom,
+    atom_token,
+    token_mask,
+    chain_id,
+    w_left,
+    w_right,
+    w_dist,
+    tri_in,
+    tri_out,
+    pae_w,
+    pool_w,
+    plddt_w,
+    atom_w,
+):
+    tile_rows, tile_cols, width = z_trunk.shape
+    tokens = single.shape[0]
+    if tokens * tokens * width * 4 > WHOLE_PAIR_BYTES:
+        return per_device(
+            z_trunk, single, atom_coords, atom_single, rep_atom, atom_token, token_mask, chain_id,
+            w_left, w_right, w_dist, tri_in, tri_out, pae_w, pool_w, plddt_w, atom_w,
+        )
+    row_count = lax.axis_size("row")
+    col_count = lax.axis_size("col")
+    chips = row_count // 2
+    atoms = atom_coords.shape[1]
+    float32 = jnp.float32
+
+    def across(values, axis, count, step):
+        return lax.ppermute(values, axis, [(i, i ^ step) for i in range(count)])
+
+    def partner(values):
+        return across(values, "row", row_count, 1)
+
+    packed = pl.pallas_call(
+        pack_kernel,
+        out_shape=jax.ShapeDtypeStruct((tile_rows * tile_cols + 2 * atoms, width), jnp.bfloat16),
+        in_specs=[VMEM] * 3,
+        out_specs=VMEM,
+        name="pack",
+    )(z_trunk, atom_coords, partner(atom_coords))
+    slots = [(i, j) for i in range(chips) for j in range(col_count)]
+    along = [packed] + [across(packed, "row", row_count, 2 * i) for i in range(1, chips)]
+    packs = [along[i] if j == 0 else across(along[i], "col", col_count, j) for i, j in slots]
+    mask_row = token_mask.reshape(1, tokens)
+    tiles = jax.ShapeDtypeStruct((chips, tile_rows, col_count, tile_cols, width), float32)
+    turned = jax.ShapeDtypeStruct((col_count, tile_cols, chips, tile_rows, width), jnp.bfloat16)
+    pair, gating, left, right = pl.pallas_call(
+        lambda *refs: edge_kernel(slots, col_count, *refs),
+        out_shape=(tiles, tiles, tiles, turned),
+        in_specs=[VMEM] * (len(slots) + 7),
+        out_specs=(VMEM,) * 4,
+        scratch_shapes=[
+            pltpu.VMEM((3, tokens, width), float32),
+            pltpu.VMEM((tokens, width), float32),
+            pltpu.VMEM((tokens, width), float32),
+            pltpu.VMEM((width, width), float32),
+        ],
+        name="edges",
+    )(*packs, single, rep_atom.reshape(1, tokens), mask_row, w_left, w_right, w_dist, tri_in)
+    tm_scale = 1.24 * (max(tokens, 19) - 15) ** (1.0 / 3.0) - 1.8
+    aligned_error, interface_score, pooled = pl.pallas_call(
+        lambda *refs: triangle_kernel(tm_scale, *refs),
+        out_shape=(
+            jax.ShapeDtypeStruct((tile_rows, tile_cols), float32),
+            jax.ShapeDtypeStruct((1, tile_rows), float32),
+            jax.ShapeDtypeStruct((chips * tile_rows, width), float32),
+        ),
+        in_specs=[VMEM] * 9 + [SMEM],
+        out_specs=(VMEM,) * 3,
+        scratch_shapes=[
+            pltpu.VMEM((tokens, chips, 2, tile_rows, width), float32),
+            pltpu.VMEM((chips, tile_rows, tokens, width), jnp.bfloat16),
+        ],
+        name="triangle",
+    )(
+        left, right, partner(right), pair, gating, tri_out, pae_w, mask_row,
+        chain_id.reshape(1, tokens), chain_id,
+    )
+    atom_confidence = pl.pallas_call(
+        atom_kernel,
+        out_shape=jax.ShapeDtypeStruct((1, atoms), float32),
+        in_specs=[VMEM] * 9,
+        out_specs=VMEM,
+        scratch_shapes=[pltpu.VMEM((chips, 2, tile_rows, width), float32)],
+        name="atoms",
+    )(
+        pooled, partner(pooled), single, mask_row, pool_w, plddt_w,
+        atom_token.reshape(1, atoms), atom_single, atom_w,
+    )
+    return (aligned_error, interface_score.reshape(tile_rows), atom_confidence.reshape(atoms))
+
+
+def gathers_whole(mesh):
+    row_count, col_count = mesh.shape["row"], mesh.shape["col"]
+    power = all(count & (count - 1) == 0 for count in (row_count, col_count))
+    return power and row_count > 1 and mesh.shape["ch"] == 1
+
+
 def solution(mesh):
     placed = (
         P(("parts", "row"), ("col", "ch"), None),
@@ -164,7 +523,7 @@
         P(),
     )
     return jax.shard_map(
-        per_device,
+        direct if gathers_whole(mesh) else per_device,
         mesh=mesh,
         in_specs=placed,
         out_specs=(

time: 115 us -> 49 us (0.43)
  blocking collectives: 68.2 us -> 0 us
  Pallas kernels: 0 us -> 22.3 us
  between operations: 14.2 us -> 0.71 us
  starting transfers between devices: 0.04 us -> 10.2 us
  matrix products: 10.1 us -> 0 us
  other arithmetic: 6.86 us -> 0 us
  local copies, waits for them, and re-layouts: 7.06 us -> 4.79 us
  waiting for transfers between devices: 8.45 us -> 10.7 us
    all_gather x3 -> x0, blocking collectives: 63.2 us -> none  [the longest x1 34.2 us: per_device(): lax.all_gather(atom_coords, ('row', 'col', 'ch'), axis=1, tiled=True)]
    pallas_call x0 -> x4, Pallas kernels: none -> 22.3 us  [the longest x1 11.2 us: direct(): pl.pallas_call(lambda *refs: triangle_kernel(tm_scale, *refs), out_shape=...]
    ppermute x0 -> x10, waiting for transfers between devices: none -> 10.7 us  [across(): return lax.ppermute(values, axis, [(i, i ^ step) for i in range(count)])]
    ppermute x0 -> x10, starting transfers between devices: none -> 10.2 us  [across(): return lax.ppermute(values, axis, [(i, i ^ step) for i in range(count)])]
    dot_general x10 -> x0, matrix products: 9.07 us -> none  [the longest x1 2.13 us: per_device(): jnp.einsum('ikc,jkc->ijc', left_side, lax.all_gather(right_side, 'row', a...]
    reduce_scatter x1 -> x0, waiting for transfers between devices: 8.43 us -> none  [per_device(): lax.psum_scatter(partial_terms, ('col', 'ch'), scatter_dimension=1, tiled...]
    psum x1 -> x0, blocking collectives: 5 us -> none  [per_device(): lax.psum((numerator_part, count_part, pooled_part), ('col', 'ch'))]
    unnamed x21 -> x29, local copies, waits for them, and re-layouts: 0.14 us -> 4.79 us
  transfers between devices with their start and end apart: 1 -> 10, of which waited for: 1 -> 5; matrix products, arithmetic and copies ran while one was open for 1% -> 5% of each run, Pallas kernels for 0% -> 0%
where the time goes in v1:
time: 49 us; the launch traced here: 48.7 us
  Pallas kernels  22.3 us (46%)
  waiting for transfers between devices  10.7 us (22%)
  starting transfers between devices  10.2 us (21%)
  local copies, waits for them, and re-layouts  4.79 us (10%)
  between operations  0.71 us (1%)
    pallas_call x1, Pallas kernels, direct(): pl.pallas_call(lambda *refs: triangle_kernel(tm_scale, *refs), out_shape=...  11.2 us
    ppermute x10, waiting for transfers between devices, across(): return lax.ppermute(values, axis, [(i, i ^ step) for i in range(count)])  10.7 us
    ppermute x10, starting transfers between devices, across(): return lax.ppermute(values, axis, [(i, i ^ step) for i in range(count)])  10.2 us
    pallas_call x1, Pallas kernels, direct(): pl.pallas_call(lambda *refs: edge_kernel(slots, col_count, *refs), out_sh...  7.4 us
    unnamed x29, local copies, waits for them, and re-layouts  4.79 us
    pallas_call x1, Pallas kernels, direct(): pl.pallas_call(atom_kernel, out_shape=jax.ShapeDtypeStruct((1, atoms), fl...  2.21 us
    pallas_call x1, Pallas kernels, direct(): pl.pallas_call(pack_kernel, out_shape=jax.ShapeDtypeStruct((tile_rows * t...  1.57 us
  transfers between devices with their start and end apart: 10, of which 5 were waited for; matrix products, arithmetic and copies ran while one was open for 5% of the time, Pallas kernels for 0%

profile of v1, /device:TPU:0, one launch (start us, length us, event | category | flops | bytes accessed | tf_op | source)
XLA Modules:
  0.0 48.7 jit_solution(1088264258079969798)
XLA Ops:
  0.6 0.6 %collective-permute-start = (f32[3,16]{1,0:T(4,128)}, f32[3,16]{1,0:T(4,128)S(1)}, u32[]{:S(2)}, u32[]{:S(2)}) collective-permute-start(f32[3,16]{1,0:T(4,128)} %mine_ref.1), channel_id=1, source_target_pairs={{0,2},{2,0},{4,6},{6,4},{8,10},{10,8},{12,14},{14,12},{1,3},{3,1},... | collective-permute-start | bytes 584 | tf_op jit(solution)/shard_map/ppermute | solution.py:435
  1.2 1.0 %collective-permute-done.other_ref = f32[3,16]{1,0:T(4,128)S(1)} collective-permute-done((f32[3,16]{1,0:T(4,128)}, f32[3,16]{1,0:T(4,128)S(1)}, u32[]{:S(2)}, u32[]{:S(2)}) %collective-permute-start) | collective-permute-done | bytes 224 | tf_op jit(solution)/shard_map/ppermute | solution.py:435
  2.2 0.0 copy-start.12
  2.2 0.6 %copy-done.12 = f32[3,16]{1,0:T(4,128)} copy-done((f32[3,16]{1,0:T(4,128)}, f32[3,16]{1,0:T(4,128)S(1)}, u32[]{:S(2)}) %copy-start.12) | copy-done | bytes 216
  2.8 1.6 %pack.1.refs_0_ = bf16[288,128]{1,0:T(8,128)(2,1)} custom-call(bf16[8,32,128]{2,1,0:T(8,128)(2,1)} %z_ref.1, f32[3,16]{1,0:T(4,128)} %mine_ref.1, f32[3,16]{1,0:T(4,128)} %copy-done.12), custom_call_target="tpu_custom_call" | custom-call | tf_op jit(solution)/shard_map/pack/pallas_call | solution.py:440
  4.4 2.9 %collective-permute-start.2 = (bf16[288,128]{1,0:T(8,128)(2,1)}, bf16[288,128]{1,0:T(8,128)(2,1)S(1)}, u32[]{:S(2)}, u32[]{:S(2)}) collective-permute-start(bf16[288,128]{1,0:T(8,128)(2,1)} %pack.1.refs_0_), channel_id=1, source_target_pairs={{0,4},{2,6},{4,0},{6,2},{8,12},{10,14},{12,8},{14,10},{1,5},{3,7},... | collective-permute-start | bytes 221192 | tf_op jit(solution)/shard_map/ppermute | solution.py:435
  7.3 2.6 %collective-permute-start.4 = (bf16[288,128]{1,0:T(8,128)(2,1)}, bf16[288,128]{1,0:T(8,128)(2,1)S(1)}, u32[]{:S(2)}, u32[]{:S(2)}) collective-permute-start(bf16[288,128]{1,0:T(8,128)(2,1)} %pack.1.refs_0_), channel_id=1, source_target_pairs={{0,8},{2,10},{4,12},{6,14},{8,0},{10,2},{12,4},{14,6},{1,9},{3,11}... | collective-permute-start | bytes 221192 | tf_op jit(solution)/shard_map/ppermute | solution.py:435
  9.9 0.0 collective-permute-start.6
  9.9 1.7 %collective-permute-start.1 = (bf16[288,128]{1,0:T(8,128)(2,1)}, bf16[288,128]{1,0:T(8,128)(2,1)S(1)}, u32[]{:S(2)}, u32[]{:S(2)}) collective-permute-start(bf16[288,128]{1,0:T(8,128)(2,1)} %pack.1.refs_0_), channel_id=1, source_target_pairs={{0,1},{1,0},{2,3},{3,2},{4,5},{5,4},{6,7},{7,6},{8,9},{9,8},{10,11... | collective-permute-start | bytes 221192 | tf_op jit(solution)/shard_map/ppermute | solution.py:435
  11.6 0.0 collective-permute-done.2.refs_2_
  11.6 0.0 copy-start.1
  11.6 0.3 collective-permute-start.3
  11.9 4.4 %collective-permute-done.4.refs_4_ = bf16[288,128]{1,0:T(8,128)(2,1)S(1)} collective-permute-done((bf16[288,128]{1,0:T(8,128)(2,1)}, bf16[288,128]{1,0:T(8,128)(2,1)S(1)}, u32[]{:S(2)}, u32[]{:S(2)}) %collective-permute-start.4) | collective-permute-done | bytes 73760 | tf_op jit(solution)/shard_map/ppermute | solution.py:435
  16.3 0.0 copy-start.2
  16.3 1.5 %collective-permute-start.5 = (bf16[288,128]{1,0:T(8,128)(2,1)S(1)}, bf16[288,128]{1,0:T(8,128)(2,1)S(1)}, u32[]{:S(2)}, u32[]{:S(2)}) collective-permute-start(bf16[288,128]{1,0:T(8,128)(2,1)S(1)} %collective-permute-done.4.refs_4_), channel_id=1, source_target_pairs={{0,1},{1,0},{2,3},{3,2},{4,5},{5,4},{6,7},{7,6},{8,9},{9,8},{10,11... | collective-permute-start | bytes 221192 | tf_op jit(solution)/shard_map/ppermute | solution.py:435
  17.8 0.0 collective-permute-done.6.refs_6_
  17.8 0.0 copy-start.3
  17.8 0.5 %collective-permute-start.7 = (bf16[288,128]{1,0:T(8,128)(2,1)S(1)}, bf16[288,128]{1,0:T(8,128)(2,1)S(1)}, u32[]{:S(2)}, u32[]{:S(2)}) collective-permute-start(bf16[288,128]{1,0:T(8,128)(2,1)S(1)} %collective-permute-done.6.refs_6_), channel_id=1, source_target_pairs={{0,1},{1,0},{2,3},{3,2},{4,5},{5,4},{6,7},{7,6},{8,9},{9,8},{10,11... | collective-permute-start | bytes 221192 | tf_op jit(solution)/shard_map/ppermute | solution.py:435
  18.4 0.0 collective-permute-done.1.refs_1_
  18.4 0.0 copy-start.4
  18.4 0.0 collective-permute-done.3.refs_3_
  18.4 0.0 copy-start.5
  18.4 2.3 %collective-permute-done.5.refs_5_ = bf16[288,128]{1,0:T(8,128)(2,1)S(1)} collective-permute-done((bf16[288,128]{1,0:T(8,128)(2,1)S(1)}, bf16[288,128]{1,0:T(8,128)(2,1)S(1)}, u32[]{:S(2)}, u32[]{:S(2)}) %collective-permute-start.5) | collective-permute-done | bytes 73760 | tf_op jit(solution)/shard_map/ppermute | solution.py:435
  20.7 0.0 copy-start.6
  20.7 1.5 %collective-permute-done.7.refs_7_ = bf16[288,128]{1,0:T(8,128)(2,1)S(1)} collective-permute-done((bf16[288,128]{1,0:T(8,128)(2,1)S(1)}, bf16[288,128]{1,0:T(8,128)(2,1)S(1)}, u32[]{:S(2)}, u32[]{:S(2)}) %collective-permute-start.7) | collective-permute-done | bytes 73760 | tf_op jit(solution)/shard_map/ppermute | solution.py:435
  22.2 0.0 copy-start.7
  22.2 0.0 copy-done.1
  22.2 0.0 copy-done.2
  22.2 0.0 copy-done.3
  22.2 0.0 copy-done.4
  22.2 0.0 copy-done.5
  22.2 0.0 copy-done.6
  22.2 0.6 %copy-done.7 = bf16[288,128]{1,0:T(8,128)(2,1)} copy-done((bf16[288,128]{1,0:T(8,128)(2,1)}, bf16[288,128]{1,0:T(8,128)(2,1)S(1)}, u32[]{:S(2)}) %copy-start.7) | copy-done | bytes 73752
  22.8 0.0 copy-start.9
  22.8 7.4 %edges.1 = (f32[4,8,2,32,128]{4,3,2,1,0:T(8,128)}, f32[4,8,2,32,128]{4,3,2,1,0:T(8,128)}, f32[4,8,2,32,128]{4,3,2,1,0:T(8,128)}, bf16[2,32,4,8,128]{4,3,2,1,0:T(8,128)(2,1)}) custom-call(bf16[288,128]{1,0:T(8,128)(2,1)} %pack.1.refs_0_, bf16[288,128]{1,0:T(8,128)(2,1)} %copy-done.4, bf16[288,128]{1,0:T(8,128)(2,1)} %copy-done.1, bf16[288,128]{1,0:T(8,128)(2,1)} %copy-done.5, ...), custom_call_target="tpu_custom_call" | custom-call | tf_op jit(solution)/shard_map/edges/pallas_call | solution.py:453
  30.2 0.0 collective-permute-start.8
  30.2 0.0 copy-done.9
  30.3 0.7 %copy.20.refs_6_ = bf16[128,64]{1,0:T(8,128)(2,1)} copy(bf16[128,64]{0,1:T(8,128)(2,1)S(1)} %copy-done.9) | data formatting | bytes 32768 | tf_op args[13]
  31.0 1.4 %collective-permute-done.8.refs_2_ = bf16[2,32,4,8,128]{4,3,2,1,0:T(8,128)(2,1)S(1)} collective-permute-done((bf16[2,32,4,8,128]{4,3,2,1,0:T(8,128)(2,1)}, bf16[2,32,4,8,128]{4,3,2,1,0:T(8,128)(2,1)S(1)}, u32[]{:S(2)}, u32[]{:S(2)}) %collective-permute-start.8) | collective-permute-done | bytes 524320 | tf_op jit(solution)/shard_map/ppermute | solution.py:435
  32.4 0.0 copy-start
  32.4 0.8 %copy-done = bf16[2,32,4,8,128]{4,3,2,1,0:T(8,128)(2,1)} copy-done((bf16[2,32,4,8,128]{4,3,2,1,0:T(8,128)(2,1)}, bf16[2,32,4,8,128]{4,3,2,1,0:T(8,128)(2,1)S(1)}, u32[]{:S(2)}) %copy-start) | copy-done | bytes 524312
  33.1 0.0 copy-start.8
  33.1 11.2 %triangle.1 = (f32[8,32]{1,0:T(8,128)}, f32[1,8]{1,0:T(1,128)}, f32[32,128]{1,0:T(8,128)}) custom-call(f32[4,8,2,32,128]{4,3,2,1,0:T(8,128)} %get-tuple-element.10.refs_0_, bf16[2,32,4,8,128]{4,3,2,1,0:T(8,128)(2,1)} %get-tuple-element.11.refs_1_, bf16[2,32,4,8,128]{4,3,2,1,0:T(8,128)(2,1)} %copy-done, f32[4,8,2,32,128]{4,3,2,1,0:T(8,128)} %get-tuple-element.12.refs_3_, ...), custom_call_target="tpu_custom_call" | custom-call | tf_op jit(solution)/shard_map/triangle/pallas_call | solution.py:467
  44.3 0.0 copy-start.11
  44.3 0.1 collective-permute-start.9
  44.4 0.0 copy-done.8
  44.4 0.8 %copy.21.plddt_w_ref = bf16[384,50]{1,0:T(8,128)(2,1)} copy(bf16[384,50]{0,1:T(8,128)(2,1)S(1)} %copy-done.8) | data formatting | bytes 76800 | tf_op args[15]
  45.2 0.0 copy-done.11
  45.2 0.7 %copy.22.atom_w_ref = bf16[128,50]{1,0:T(8,128)(2,1)} copy(bf16[128,50]{0,1:T(8,128)(2,1)S(1)} %copy-done.11) | data formatting | bytes 25600 | tf_op args[16]
  45.9 0.0 collective-permute-done.9.other_ref
  45.9 0.0 copy-start.10
  45.9 0.6 %copy-done.10 = f32[32,128]{1,0:T(8,128)} copy-done((f32[32,128]{1,0:T(8,128)}, f32[32,128]{1,0:T(8,128)S(1)}, u32[]{:S(2)}) %copy-start.10) | copy-done | bytes 16408
  46.5 2.2 %atoms.1 = f32[1,16]{1,0:T(1,128)} custom-call(f32[32,128]{1,0:T(8,128)} %get-tuple-element.16.mine_ref, f32[32,128]{1,0:T(8,128)} %copy-done.10, bf16[64,384]{1,0:T(8,128)(2,1)} %single_ref.1, s32[1,64]{1,0:T(1,128)} %bitcast.8, bf16[128,384]{1,0:T(8,128)(2,1)} %pool_w_ref.1, bf16[384,50]{1,0:T(8,128)(2,1)} %copy.21.plddt_w_ref, s32[1,16]{1,0:T(1,128)} %bitcast.11, ...), custom_call_target="tpu_custom_call" | custom-call | tf_op jit(solution)/shard_map/atoms/pallas_call | solution.py:485
Async XLA Ops:
  0.6 1.6 %collective-permute-start = (f32[3,16]{1,0:T(4,128)}, f32[3,16]{1,0:T(4,128)S(1)}, u32[]{:S(2)}, u32[]{:S(2)}) collective-permute-start(f32[3,16]{1,0:T(4,128)} %mine_ref.1), channel_id=1, source_target_pairs={{0,2},{2,0},{4,6},{6,4},{8,10},{10,8},{12,14},{14,12},{1,3},{3,1},... | collective-permute-start | bytes 584 | tf_op jit(solution)/shard_map/ppermute | solution.py:435
  2.2 0.6 %copy-start.12 = (f32[3,16]{1,0:T(4,128)}, f32[3,16]{1,0:T(4,128)S(1)}, u32[]{:S(2)}) copy-start(f32[3,16]{1,0:T(4,128)S(1)} %collective-permute-done.other_ref) | copy-start | bytes 580
  4.4 7.2 %collective-permute-start.2 = (bf16[288,128]{1,0:T(8,128)(2,1)}, bf16[288,128]{1,0:T(8,128)(2,1)S(1)}, u32[]{:S(2)}, u32[]{:S(2)}) collective-permute-start(bf16[288,128]{1,0:T(8,128)(2,1)} %pack.1.refs_0_), channel_id=1, source_target_pairs={{0,4},{2,6},{4,0},{6,2},{8,12},{10,14},{12,8},{14,10},{1,5},{3,7},... | collective-permute-start | bytes 221192 | tf_op jit(solution)/shard_map/ppermute | solution.py:435
  7.3 9.1 %collective-permute-start.4 = (bf16[288,128]{1,0:T(8,128)(2,1)}, bf16[288,128]{1,0:T(8,128)(2,1)S(1)}, u32[]{:S(2)}, u32[]{:S(2)}) collective-permute-start(bf16[288,128]{1,0:T(8,128)(2,1)} %pack.1.refs_0_), channel_id=1, source_target_pairs={{0,8},{2,10},{4,12},{6,14},{8,0},{10,2},{12,4},{14,6},{1,9},{3,11}... | collective-permute-start | bytes 221192 | tf_op jit(solution)/shard_map/ppermute | solution.py:435
  9.9 8.0 %collective-permute-start.6 = (bf16[288,128]{1,0:T(8,128)(2,1)}, bf16[288,128]{1,0:T(8,128)(2,1)S(1)}, u32[]{:S(2)}, u32[]{:S(2)}) collective-permute-start(bf16[288,128]{1,0:T(8,128)(2,1)} %pack.1.refs_0_), channel_id=1, source_target_pairs={{0,12},{2,14},{4,8},{6,10},{8,4},{10,6},{12,0},{14,2},{1,13},{3,15... | collective-permute-start | bytes 221192 | tf_op jit(solution)/shard_map/ppermute | solution.py:435
  9.9 8.5 %collective-permute-start.1 = (bf16[288,128]{1,0:T(8,128)(2,1)}, bf16[288,128]{1,0:T(8,128)(2,1)S(1)}, u32[]{:S(2)}, u32[]{:S(2)}) collective-permute-start(bf16[288,128]{1,0:T(8,128)(2,1)} %pack.1.refs_0_), channel_id=1, source_target_pairs={{0,1},{1,0},{2,3},{3,2},{4,5},{5,4},{6,7},{7,6},{8,9},{9,8},{10,11... | collective-permute-start | bytes 221192 | tf_op jit(solution)/shard_map/ppermute | solution.py:435
  11.6 10.6 %copy-start.1 = (bf16[288,128]{1,0:T(8,128)(2,1)}, bf16[288,128]{1,0:T(8,128)(2,1)S(1)}, u32[]{:S(2)}) copy-start(bf16[288,128]{1,0:T(8,128)(2,1)S(1)} %collective-permute-done.2.refs_2_) | copy-start | bytes 221188
  11.6 6.8 %collective-permute-start.3 = (bf16[288,128]{1,0:T(8,128)(2,1)S(1)}, bf16[288,128]{1,0:T(8,128)(2,1)S(1)}, u32[]{:S(2)}, u32[]{:S(2)}) collective-permute-start(bf16[288,128]{1,0:T(8,128)(2,1)S(1)} %collective-permute-done.2.refs_2_), channel_id=1, source_target_pairs={{0,1},{1,0},{2,3},{3,2},{4,5},{5,4},{6,7},{7,6},{8,9},{9,8},{10,11... | collective-permute-start | bytes 221192 | tf_op jit(solution)/shard_map/ppermute | solution.py:435
  16.3 5.9 %copy-start.2 = (bf16[288,128]{1,0:T(8,128)(2,1)}, bf16[288,128]{1,0:T(8,128)(2,1)S(1)}, u32[]{:S(2)}) copy-start(bf16[288,128]{1,0:T(8,128)(2,1)S(1)} %collective-permute-done.4.refs_4_) | copy-start | bytes 221188
  16.3 4.4 %collective-permute-start.5 = (bf16[288,128]{1,0:T(8,128)(2,1)S(1)}, bf16[288,128]{1,0:T(8,128)(2,1)S(1)}, u32[]{:S(2)}, u32[]{:S(2)}) collective-permute-start(bf16[288,128]{1,0:T(8,128)(2,1)S(1)} %collective-permute-done.4.refs_4_), channel_id=1, source_target_pairs={{0,1},{1,0},{2,3},{3,2},{4,5},{5,4},{6,7},{7,6},{8,9},{9,8},{10,11... | collective-permute-start | bytes 221192 | tf_op jit(solution)/shard_map/ppermute | solution.py:435
  17.8 4.4 %copy-start.3 = (bf16[288,128]{1,0:T(8,128)(2,1)}, bf16[288,128]{1,0:T(8,128)(2,1)S(1)}, u32[]{:S(2)}) copy-start(bf16[288,128]{1,0:T(8,128)(2,1)S(1)} %collective-permute-done.6.refs_6_) | copy-start | bytes 221188
  17.8 4.4 %collective-permute-start.7 = (bf16[288,128]{1,0:T(8,128)(2,1)S(1)}, bf16[288,128]{1,0:T(8,128)(2,1)S(1)}, u32[]{:S(2)}, u32[]{:S(2)}) collective-permute-start(bf16[288,128]{1,0:T(8,128)(2,1)S(1)} %collective-permute-done.6.refs_6_), channel_id=1, source_target_pairs={{0,1},{1,0},{2,3},{3,2},{4,5},{5,4},{6,7},{7,6},{8,9},{9,8},{10,11... | collective-permute-start | bytes 221192 | tf_op jit(solution)/shard_map/ppermute | solution.py:435
  18.4 3.8 %copy-start.4 = (bf16[288,128]{1,0:T(8,128)(2,1)}, bf16[288,128]{1,0:T(8,128)(2,1)S(1)}, u32[]{:S(2)}) copy-start(bf16[288,128]{1,0:T(8,128)(2,1)S(1)} %collective-permute-done.1.refs_1_) | copy-start | bytes 221188
  18.4 3.8 %copy-start.5 = (bf16[288,128]{1,0:T(8,128)(2,1)}, bf16[288,128]{1,0:T(8,128)(2,1)S(1)}, u32[]{:S(2)}) copy-start(bf16[288,128]{1,0:T(8,128)(2,1)S(1)} %collective-permute-done.3.refs_3_) | copy-start | bytes 221188
  20.7 1.5 %copy-start.6 = (bf16[288,128]{1,0:T(8,128)(2,1)}, bf16[288,128]{1,0:T(8,128)(2,1)S(1)}, u32[]{:S(2)}) copy-start(bf16[288,128]{1,0:T(8,128)(2,1)S(1)} %collective-permute-done.5.refs_5_) | copy-start | bytes 221188
  22.2 0.6 %copy-start.7 = (bf16[288,128]{1,0:T(8,128)(2,1)}, bf16[288,128]{1,0:T(8,128)(2,1)S(1)}, u32[]{:S(2)}) copy-start(bf16[288,128]{1,0:T(8,128)(2,1)S(1)} %collective-permute-done.7.refs_7_) | copy-start | bytes 221188
  22.8 7.4 %copy-start.9 = (bf16[128,64]{0,1:T(8,128)(2,1)S(1)}, bf16[128,64]{0,1:T(8,128)(2,1)}, u32[]{:S(2)}) copy-start(bf16[128,64]{0,1:T(8,128)(2,1)} %param.30) | copy-start | bytes 49156
  30.2 2.1 %collective-permute-start.8 = (bf16[2,32,4,8,128]{4,3,2,1,0:T(8,128)(2,1)}, bf16[2,32,4,8,128]{4,3,2,1,0:T(8,128)(2,1)S(1)}, u32[]{:S(2)}, u32[]{:S(2)}) collective-permute-start(bf16[2,32,4,8,128]{4,3,2,1,0:T(8,128)(2,1)} %get-tuple-element.11.refs_1_), channel_id=1, source_target_pairs={{0,2},{2,0},{4,6},{6,4},{8,10},{10,8},{12,14},{14,12},{1,3},{3,1},... | collective-permute-start | bytes 1572872 | tf_op jit(solution)/shard_map/ppermute | solution.py:435
  32.4 0.8 %copy-start = (bf16[2,32,4,8,128]{4,3,2,1,0:T(8,128)(2,1)}, bf16[2,32,4,8,128]{4,3,2,1,0:T(8,128)(2,1)S(1)}, u32[]{:S(2)}) copy-start(bf16[2,32,4,8,128]{4,3,2,1,0:T(8,128)(2,1)S(1)} %collective-permute-done.8.refs_2_) | copy-start | bytes 1572868
  33.1 11.3 %copy-start.8 = (bf16[384,50]{0,1:T(8,128)(2,1)S(1)}, bf16[384,50]{0,1:T(8,128)(2,1)}, u32[]{:S(2)}) copy-start(bf16[384,50]{0,1:T(8,128)(2,1)} %param.32) | copy-start | bytes 115204
  44.3 0.9 %copy-start.11 = (bf16[128,50]{0,1:T(8,128)(2,1)S(1)}, bf16[128,50]{0,1:T(8,128)(2,1)}, u32[]{:S(2)}) copy-start(bf16[128,50]{0,1:T(8,128)(2,1)} %param.33) | copy-start | bytes 38404
  44.3 1.6 %collective-permute-start.9 = (f32[32,128]{1,0:T(8,128)}, f32[32,128]{1,0:T(8,128)S(1)}, u32[]{:S(2)}, u32[]{:S(2)}) collective-permute-start(f32[32,128]{1,0:T(8,128)} %get-tuple-element.16.mine_ref), channel_id=1, source_target_pairs={{0,2},{2,0},{4,6},{6,4},{8,10},{10,8},{12,14},{14,12},{1,3},{3,1},... | collective-permute-start | bytes 49160 | tf_op jit(solution)/shard_map/ppermute | solution.py:435
  45.9 0.6 %copy-start.10 = (f32[32,128]{1,0:T(8,128)}, f32[32,128]{1,0:T(8,128)S(1)}, u32[]{:S(2)}) copy-start(f32[32,128]{1,0:T(8,128)S(1)} %collective-permute-done.9.other_ref) | copy-start | bytes 49156

commit v2 on v1

--- a/solution.py
+++ b/solution.py
@@ -146,8 +146,37 @@
 
 
 WHOLE_PAIR_BYTES = 4 * 1024 * 1024
+SCOPED_BYTES = 16 * 1024 * 1024
 VMEM = pl.BlockSpec(memory_space=pltpu.VMEM)
-SMEM = pl.BlockSpec(memory_space=pltpu.SMEM)
+
+
+HBM = pl.BlockSpec(memory_space=pltpu.HBM)
+
+
+def run(kernel, name, out_shapes, arguments, held=None, scratch=(), aliases=None):
+    held = len(arguments) if held is None else held
+    spaces = [pltpu.VMEM] * held + [pltpu.HBM] * (len(arguments) - held)
+    return pl.pallas_call(
+        kernel,
+        out_shape=out_shapes,
+        in_specs=[VMEM] * held + [HBM] * (len(arguments) - held),
+        out_specs=(VMEM,) * len(out_shapes) if isinstance(out_shapes, tuple) else VMEM,
+        scratch_shapes=list(scratch),
+        input_output_aliases=aliases or {},
+        compiler_params=pltpu.CompilerParams(vmem_limit_bytes=SCOPED_BYTES),
+        name=name,
+    )(*map(pltpu.with_memory_space_constraint, arguments, spaces))
+
+
+def bring(sources, targets, arrived):
+    copies = [
+        pltpu.make_async_copy(source, target, arrived.at[place])
+        for place, (source, target) in enumerate(zip(sources, targets))
+    ]
+    for copy in copies:
+        copy.start()
+    for copy in copies:
+        copy.wait()
 
 
 def sigmoid(values):
@@ -163,44 +192,73 @@
     return jnp.sum(mask_ref[...].astype(jnp.float32), axis=1, keepdims=True)
 
 
-def pack_kernel(z_ref, mine_ref, other_ref, out_ref):
-    rows, cols, width = z_ref.shape
+def real_pairs(mask_ref, row_start, col_start, shape):
+    limit = token_count(mask_ref).astype(jnp.int32).reshape(1, 1, 1)
+    rows = lax.broadcasted_iota(jnp.int32, shape, 0) + row_start
+    cols = lax.broadcasted_iota(jnp.int32, shape, 1) + col_start
+    return jnp.where((rows < limit) & (cols < limit), 1.0, 0.0)
+
+
+def fetch_kernel(z_ref, coords_ref, out_ref, coords_out_ref, arrived):
+    pairs = z_ref.shape[0]
+    bring((z_ref, coords_ref), (out_ref.at[0:pairs, :], coords_out_ref), arrived)
+    out_ref[pairs:, :] = jnp.zeros_like(out_ref[pairs:, :])
+
+
+def pack_kernel(packed_ref, mine_ref, other_ref, out_ref):
+    del packed_ref
+    width = out_ref.shape[1]
     atoms = mine_ref.shape[1]
-    out_ref[0 : rows * cols, :] = z_ref[...].reshape(rows * cols, width)
-    half = lax.rem(lax.axis_index("row"), 2)
-    for place, ref in ((half, mine_ref), (1 - half, other_ref)):
-        value = ref[...]
-        high = value.astype(jnp.bfloat16).astype(jnp.float32)
-        middle = (value - high).astype(jnp.bfloat16).astype(jnp.float32)
-        low = value - high - middle
-        filler = jnp.zeros((width - 9, atoms), jnp.float32)
-        stacked = jnp.concatenate([high, middle, low, filler], axis=0)
-        start = pl.multiple_of(rows * cols + place * atoms, 16)
-        out_ref[pl.ds(start, atoms), :] = stacked.T.astype(jnp.bfloat16)
-
-
-def edge_kernel(slots, col_count, *refs):
-    packs = refs[: len(slots)]
-    single_ref, rep_ref, mask_ref, w_left_ref, w_right_ref, w_dist_ref, tri_in_ref = refs[
-        len(slots) : len(slots) + 7
+    first = lax.rem(lax.axis_index("row"), 2) == 0
+    mine, other = mine_ref[...], other_ref[...]
+    value = jnp.concatenate(
+        [jnp.where(first, mine, other), jnp.where(first, other, mine)], axis=1
+    )
+    high = value.astype(jnp.bfloat16).astype(jnp.float32)
+    middle = (value - high).astype(jnp.bfloat16).astype(jnp.float32)
+    low = value - high - middle
+    stacked = jnp.concatenate([high, middle, low, jnp.zeros((7, 2 * atoms), jnp.float32)], axis=0)
+    filler = jnp.zeros((16, width - 2 * atoms), jnp.float32)
+    out_ref[out_ref.shape[0] - 16 :, :] = jnp.concatenate([stacked, filler], axis=1).astype(
+        jnp.bfloat16
+    )
+
+
+def prepare_kernel(copied, *refs):
+    raw = refs[1:6]
+    sources = refs[6 : 6 + copied]
+    rows_ref, cols_ref, dist_ref, atom_part_ref = refs[6 + copied : 10 + copied]
+    targets = refs[10 + copied : 10 + 2 * copied]
+    w_left_ref, w_right_ref, w_dist_ref, atom_single_ref, atom_w_ref, arrived = refs[
+        10 + 2 * copied :
     ]
-    pair_ref, gating_ref, left_ref, right_ref = refs[len(slots) + 7 : len(slots) + 11]
-    xyz_ref, rows_ref, cols_ref, dist_ref = refs[len(slots) + 11 :]
-    _, tile_rows, _, tile_cols, width = pair_ref.shape
-    tokens = single_ref.shape[0]
-    pairs = tile_rows * tile_cols
-    atoms = (packs[0].shape[0] - pairs) // 2
-    basis_count = w_dist_ref.shape[0]
-    chip, half, col = place_of()
-    single = single_ref[...]
+    landing = (w_left_ref, w_right_ref, w_dist_ref, atom_single_ref, atom_w_ref)
+    bring((*raw, *sources), (*landing, *targets), arrived)
+    single = targets[0][...]
     rows_ref[...] = jnp.dot(single, w_left_ref[...], preferred_element_type=jnp.float32)
     cols_ref[...] = jnp.dot(single, w_right_ref[...], preferred_element_type=jnp.float32)
     dist_ref[...] = jnp.zeros_like(dist_ref)
-    dist_ref[0:basis_count, :] = w_dist_ref[...].astype(jnp.float32)
+    dist_ref[0 : w_dist_ref.shape[0], :] = w_dist_ref[...].astype(jnp.float32)
+    atom_part_ref[...] = lax.dot_general(
+        atom_w_ref[...],
+        atom_single_ref[...],
+        (((1,), (1,)), ((), ())),
+        preferred_element_type=jnp.float32,
+    )
+
+
+def edge_kernel(slots, col_count, atoms, basis_count, *refs):
+    packs = refs[: len(slots)]
+    rows_ref, cols_ref, dist_ref, rep_ref, mask_ref, tri_in_ref = refs[len(slots) : len(slots) + 6]
+    pair_ref, normed_ref, right_ref, xyz_ref = refs[len(slots) + 6 :]
+    _, tile_rows, _, tile_cols, width = pair_ref.shape
+    tokens = rows_ref.shape[0]
+    pairs = tile_rows * tile_cols
+    chip, half, col = place_of()
     w_dist = dist_ref[...].astype(jnp.bfloat16)
     rep = rep_ref[...]
-    order = lax.broadcasted_iota(jnp.int32, (2 * atoms, tokens), 0)
-    picked = jnp.zeros((tokens, width), jnp.float32)
+    order = lax.broadcasted_iota(jnp.int32, (width, tokens), 0)
+    picked = jnp.zeros((tokens, 16), jnp.float32)
     for pack, (chip_step, col_step) in zip(packs, slots):
         device = 2 * (chip ^ chip_step) * col_count + (col ^ col_step)
         number = jnp.where(
@@ -208,21 +266,18 @@
         )
         chosen = (number == rep).astype(jnp.float32).astype(jnp.bfloat16)
         picked = picked + lax.dot_general(
-            chosen, pack[pairs:, :], (((0,), (0,)), ((), ())), preferred_element_type=jnp.float32
+            chosen, pack[pairs:, :], (((0,), (1,)), ((), ())), preferred_element_type=jnp.float32
         )
     for axis in range(3):
         whole = picked[:, axis : axis + 1] + picked[:, axis + 3 : axis + 4]
         whole = whole + picked[:, axis + 6 : axis + 7]
         xyz_ref[axis] = jnp.broadcast_to(whole, (tokens, width))
-    count = token_count(mask_ref)
     step_size = 18.0 / (basis_count - 1)
     centers = 3.375 + step_size * lax.broadcasted_iota(jnp.int32, (1, 1, width), 2).astype(
         jnp.float32
     )
-    row_order = lax.broadcasted_iota(jnp.int32, (tile_rows, tile_cols, width), 0)
-    col_order = lax.broadcasted_iota(jnp.int32, (tile_rows, tile_cols, width), 1)
-    limit = count.astype(jnp.int32).reshape(1, 1, 1)
-    tri_in = tri_in_ref[...]
+    tile = (tile_rows, tile_cols, width)
+    tri_in = tri_in_ref[:, 2 * width : 4 * width]
     for pack, (chip_step, col_step) in zip(packs, slots):
         at_chip = chip ^ chip_step
         at_col = col ^ col_step
@@ -230,63 +285,69 @@
         col_start = pl.multiple_of(at_col * tile_cols, 8)
         row_slice = pl.ds(row_start, tile_rows)
         col_slice = pl.ds(col_start, tile_cols)
-        square = jnp.zeros((tile_rows, tile_cols, width), jnp.float32)
+        square = jnp.zeros(tile, jnp.float32)
         for axis in range(3):
             gap = xyz_ref[axis, row_slice, :][:, None, :] - xyz_ref[axis, col_slice, :][None]
             square = square + gap * gap
         scaled = (jnp.sqrt(square) - centers) * (1.0 / step_size)
         basis = jnp.exp(-scaled * scaled).astype(jnp.bfloat16)
         pair = (
-            pack[0:pairs, :].astype(jnp.float32).reshape(tile_rows, tile_cols, width)
+            pack[0:pairs, :].astype(jnp.float32).reshape(tile)
             + rows_ref[row_slice, :][:, None, :]
             + cols_ref[col_slice, :][None]
         )
         pair = pair.reshape(pairs, width) + jnp.dot(
             basis.reshape(pairs, width), w_dist, preferred_element_type=jnp.float32
         )
-        tile = (tile_rows, tile_cols, width)
         pair_ref[at_chip, :, at_col] = pair.reshape(tile)
         normed = layer_norm(pair).astype(jnp.bfloat16)
+        normed_ref[at_chip, :, at_col] = normed.reshape(tile)
         projected = jnp.dot(normed, tri_in, preferred_element_type=jnp.float32)
-        real = jnp.where(
-            (row_order + row_start < limit) & (col_order + col_start < limit), 1.0, 0.0
-        )
-        left = sigmoid(projected[:, 0:width]) * projected[:, width : 2 * width]
-        left = (left.reshape(tile) * real).astype(jnp.bfloat16)
-        left_ref[at_chip, :, at_col] = left.astype(jnp.float32)
-        right = sigmoid(projected[:, 2 * width : 3 * width]) * projected[:, 3 * width : 4 * width]
-        right = right.reshape(tile) * real
+        right = sigmoid(projected[:, 0:width]) * projected[:, width : 2 * width]
+        right = right.reshape(tile) * real_pairs(mask_ref, row_start, col_start, tile)
         right_ref[at_col, :, at_chip] = jnp.swapaxes(right, 0, 1).astype(jnp.bfloat16)
-        gating_ref[at_chip, :, at_col] = sigmoid(projected[:, 4 * width :]).reshape(tile)
+
+
+def left_kernel(normed_ref, tri_in_ref, mask_ref, left_ref, gating_ref):
+    chips, tile_rows, col_count, tile_cols, width = normed_ref.shape
+    _, half, _ = place_of()
+    pairs = tile_rows * tile_cols
+    tile = (tile_rows, tile_cols, width)
+    tri_in = jnp.concatenate([tri_in_ref[:, 0 : 2 * width], tri_in_ref[:, 4 * width :]], axis=1)
+    for at_chip in range(chips):
+        for at_col in range(col_count):
+            normed = normed_ref[at_chip, :, at_col].reshape(pairs, width)
+            projected = jnp.dot(normed, tri_in, preferred_element_type=jnp.float32)
+            left = sigmoid(projected[:, 0:width]) * projected[:, width : 2 * width]
+            real = real_pairs(
+                mask_ref, (2 * at_chip + half) * tile_rows, at_col * tile_cols, tile
+            )
+            left = (left.reshape(tile) * real).astype(jnp.bfloat16)
+            left_ref[at_chip, :, at_col] = left.astype(jnp.float32)
+            gating_ref[at_chip, :, at_col] = sigmoid(projected[:, 2 * width :]).reshape(tile)
 
 
 def triangle_kernel(
-    tm_scale,
     left_ref,
     mine_ref,
     other_ref,
     pair_ref,
     gating_ref,
     tri_out_ref,
-    pae_w_ref,
     mask_ref,
-    chain_ref,
-    chain_smem,
-    aligned_ref,
-    interface_ref,
     pooled_ref,
+    own_ref,
     right_ref,
     updated_ref,
 ):
     chips, tile_rows, col_count, tile_cols, width = pair_ref.shape
     tokens = col_count * tile_cols
-    chip, half, col = place_of()
+    chip, half, _ = place_of()
     shape = (tokens, chips, tile_rows, width)
     right_ref[:, :, half] = mine_ref[...].reshape(shape).astype(jnp.float32)
     right_ref[:, :, 1 - half] = other_ref[...].reshape(shape).astype(jnp.float32)
-    count = token_count(mask_ref)
     token_order = lax.broadcasted_iota(jnp.int32, (tokens, width), 0)
-    real = jnp.where(token_order < count.astype(jnp.int32), 1.0, 0.0)
+    real = jnp.where(token_order < token_count(mask_ref).astype(jnp.int32), 1.0, 0.0)
     tri_out = tri_out_ref[...]
     block = 4
     blocks = tile_rows // block
@@ -322,11 +383,20 @@
         return carry
 
     lax.fori_loop(0, chips * blocks, rows_of, 0)
-    bins = pae_w_ref.shape[1]
+    own_ref[...] = updated_ref[chip].reshape(tile_rows * tokens, width)
+
+
+def score_kernel(
+    tm_scale, col_count, own_ref, pae_w_ref, mask_ref, chain_ref, aligned_ref, interface_ref
+):
+    tile_rows, tile_cols = aligned_ref.shape
+    tokens = chain_ref.shape[1]
+    chip, half, col = place_of()
+    bins = pae_w_ref.shape[0]
     logits = lax.dot_general(
         pae_w_ref[...],
-        updated_ref[chip].reshape(tile_rows * tokens, width),
-        (((0,), (1,)), ((), ())),
+        own_ref[...],
+        (((1,), (1,)), ((), ())),
         preferred_element_type=jnp.float32,
     )
     centers = 0.5 * (lax.broadcasted_iota(jnp.int32, (bins, 1), 0).astype(jnp.float32) + 0.5)
@@ -337,7 +407,7 @@
     tm_pair = jnp.sum(weight * (1.0 / (1.0 + ratio * ratio)), axis=0, keepdims=True) / total
     chains = chain_ref[...]
     keys = lax.broadcasted_iota(jnp.int32, (1, tokens), 1)
-    limit = count.astype(jnp.int32)
+    limit = token_count(mask_ref).astype(jnp.int32)
     places = lax.broadcasted_iota(jnp.int32, (1, tile_rows), 1)
     scores = jnp.zeros((1, tile_rows), jnp.float32)
     query = (2 * chip + half) * tile_rows
@@ -349,7 +419,10 @@
                 col == other, span[:, other * tile_cols : (other + 1) * tile_cols], mine
             )
         aligned_ref[i : i + 1, :] = mine
-        face = (keys < limit) & (query + i < limit) & (chains != chain_smem[query + i])
+        own_chain = jnp.sum(
+            jnp.where(keys == query + i, chains, 0).astype(jnp.float32), axis=1, keepdims=True
+        ).astype(jnp.int32)
+        face = (keys < limit) & (query + i < limit) & (chains != own_chain)
         face = jnp.where(face, 1.0, 0.0)
         number = jnp.sum(face, axis=1, keepdims=True)
         score = jnp.sum(face * tm_pair[:, i * tokens : (i + 1) * tokens], axis=1, keepdims=True)
@@ -365,8 +438,7 @@
     pool_w_ref,
     plddt_w_ref,
     atom_token_ref,
-    atom_single_ref,
-    atom_w_ref,
+    atom_part_ref,
     out_ref,
     pooled_ref,
 ):
@@ -386,11 +458,11 @@
     picked = lax.dot_general(
         chosen, single_norm, (((0,), (0,)), ((), ())), preferred_element_type=jnp.float32
     ).astype(jnp.bfloat16)
-    turned = (((0,), (1,)), ((), ()))
-    logits = lax.dot_general(
-        plddt_w_ref[...], picked, turned, preferred_element_type=jnp.float32
-    ) + lax.dot_general(
-        atom_w_ref[...], atom_single_ref[...], turned, preferred_element_type=jnp.float32
+    logits = (
+        lax.dot_general(
+            plddt_w_ref[...], picked, (((1,), (1,)), ((), ())), preferred_element_type=jnp.float32
+        )
+        + atom_part_ref[...]
     )
     bins = logits.shape[0]
     centers = (lax.broadcasted_iota(jnp.int32, (bins, 1), 0).astype(jnp.float32) + 0.5) / bins
@@ -420,7 +492,8 @@
 ):
     tile_rows, tile_cols, width = z_trunk.shape
     tokens = single.shape[0]
-    if tokens * tokens * width * 4 > WHOLE_PAIR_BYTES:
+    atoms = atom_coords.shape[1]
+    if tokens * tokens * width * 4 > WHOLE_PAIR_BYTES or 2 * atoms > width:
         return per_device(
             z_trunk, single, atom_coords, atom_single, rep_atom, atom_token, token_mask, chain_id,
             w_left, w_right, w_dist, tri_in, tri_out, pae_w, pool_w, plddt_w, atom_w,
@@ -428,8 +501,7 @@
     row_count = lax.axis_size("row")
     col_count = lax.axis_size("col")
     chips = row_count // 2
-    atoms = atom_coords.shape[1]
-    float32 = jnp.float32
+    float32, bfloat16 = jnp.float32, jnp.bfloat16
 
     def across(values, axis, count, step):
         return lax.ppermute(values, axis, [(i, i ^ step) for i in range(count)])
@@ -437,61 +509,91 @@
     def partner(values):
         return across(values, "row", row_count, 1)
 
-    packed = pl.pallas_call(
-        pack_kernel,
-        out_shape=jax.ShapeDtypeStruct((tile_rows * tile_cols + 2 * atoms, width), jnp.bfloat16),
-        in_specs=[VMEM] * 3,
-        out_specs=VMEM,
-        name="pack",
-    )(z_trunk, atom_coords, partner(atom_coords))
+    block = pltpu.VMEM((tile_rows * tile_cols + 16, width), bfloat16)
+    fetched, coords = run(
+        fetch_kernel,
+        "fetch",
+        (block, pltpu.VMEM((3, atoms), float32)),
+        (z_trunk.reshape(tile_rows * tile_cols, width), atom_coords),
+        0,
+        scratch=(pltpu.SemaphoreType.DMA((2,)),),
+    )
+    packed = run(
+        pack_kernel, "pack", block, (fetched, coords, partner(atom_coords)), aliases={0: 0}
+    )
     slots = [(i, j) for i in range(chips) for j in range(col_count)]
     along = [packed] + [across(packed, "row", row_count, 2 * i) for i in range(1, chips)]
     packs = [along[i] if j == 0 else across(along[i], "col", col_count, j) for i, j in slots]
-    mask_row = token_mask.reshape(1, tokens)
-    tiles = jax.ShapeDtypeStruct((chips, tile_rows, col_count, tile_cols, width), float32)
-    turned = jax.ShapeDtypeStruct((col_count, tile_cols, chips, tile_rows, width), jnp.bfloat16)
-    pair, gating, left, right = pl.pallas_call(
-        lambda *refs: edge_kernel(slots, col_count, *refs),
-        out_shape=(tiles, tiles, tiles, turned),
-        in_specs=[VMEM] * (len(slots) + 7),
-        out_specs=(VMEM,) * 4,
-        scratch_shapes=[
-            pltpu.VMEM((3, tokens, width), float32),
+    raw = (w_left, w_right, w_dist, atom_single, atom_w.T)
+    kept = (
+        single, tri_in, tri_out, pae_w.T, pool_w, plddt_w.T, rep_atom.reshape(1, tokens),
+        token_mask.reshape(1, tokens), chain_id.reshape(1, tokens), atom_token.reshape(1, atoms),
+    )
+    rows, cols, dist, atom_part, *kept = run(
+        lambda *refs: prepare_kernel(len(kept), *refs),
+        "prepare",
+        (
             pltpu.VMEM((tokens, width), float32),
             pltpu.VMEM((tokens, width), float32),
             pltpu.VMEM((width, width), float32),
-        ],
-        name="edges",
-    )(*packs, single, rep_atom.reshape(1, tokens), mask_row, w_left, w_right, w_dist, tri_in)
+            pltpu.VMEM((plddt_w.shape[1], atoms), float32),
+            *[pltpu.VMEM(value.shape, value.dtype) for value in kept],
+        ),
+        (packed, *raw, *kept),
+        1,
+        scratch=(
+            *[pltpu.VMEM(value.shape, value.dtype) for value in raw],
+            pltpu.SemaphoreType.DMA((len(raw) + len(kept),)),
+        ),
+    )
+    single, tri_in, tri_out, pae_w, pool_w, plddt_w, rep, mask, chain, atom_token = kept
+    full = (chips, tile_rows, col_count, tile_cols, width)
+    pair, normed, right = run(
+        lambda *refs: edge_kernel(slots, col_count, atoms, w_dist.shape[0], *refs),
+        "edges",
+        (
+            pltpu.VMEM(full, float32),
+            pltpu.VMEM(full, bfloat16),
+            pltpu.VMEM((col_count, tile_cols, chips, tile_rows, width), bfloat16),
+        ),
+        (*packs, rows, cols, dist, rep, mask, tri_in),
+        scratch=(pltpu.VMEM((3, tokens, width), float32),),
+    )
+    left, gating = run(
+        left_kernel,
+        "left",
+        (pltpu.VMEM(full, float32), pltpu.VMEM(full, float32)),
+        (normed, tri_in, mask),
+    )
+    pooled, own = run(
+        triangle_kernel,
+        "triangle",
+        (
+            pltpu.VMEM((chips * tile_rows, width), float32),
+            pltpu.VMEM((tile_rows * tokens, width), bfloat16),
+        ),
+        (left, right, partner(right), pair, gating, tri_out, mask),
+        scratch=(
+            pltpu.VMEM((tokens, chips, 2, tile_rows, width), float32),
+            pltpu.VMEM((chips, tile_rows, tokens, width), bfloat16),
+        ),
+    )
     tm_scale = 1.24 * (max(tokens, 19) - 15) ** (1.0 / 3.0) - 1.8
-    aligned_error, interface_score, pooled = pl.pallas_call(
-        lambda *refs: triangle_kernel(tm_scale, *refs),
-        out_shape=(
+    aligned_error, interface_score = run(
+        lambda *refs: score_kernel(tm_scale, col_count, *refs),
+        "scores",
+        (
             jax.ShapeDtypeStruct((tile_rows, tile_cols), float32),
             jax.ShapeDtypeStruct((1, tile_rows), float32),
-            jax.ShapeDtypeStruct((chips * tile_rows, width), float32),
         ),
-        in_specs=[VMEM] * 9 + [SMEM],
-        out_specs=(VMEM,) * 3,
-        scratch_shapes=[
-            pltpu.VMEM((tokens, chips, 2, tile_rows, width), float32),
-            pltpu.VMEM((chips, tile_rows, tokens, width), jnp.bfloat16),
-        ],
-        name="triangle",
-    )(
-        left, right, partner(right), pair, gating, tri_out, pae_w, mask_row,
-        chain_id.reshape(1, tokens), chain_id,
-    )
-    atom_confidence = pl.pallas_call(
+        (own, pae_w, mask, chain),
+    )
+    atom_confidence = run(
         atom_kernel,
-        out_shape=jax.ShapeDtypeStruct((1, atoms), float32),
-        in_specs=[VMEM] * 9,
-        out_specs=VMEM,
-        scratch_shapes=[pltpu.VMEM((chips, 2, tile_rows, width), float32)],
-        name="atoms",
-    )(
-        pooled, partner(pooled), single, mask_row, pool_w, plddt_w,
-        atom_token.reshape(1, atoms), atom_single, atom_w,
+        "atoms",
+        jax.ShapeDtypeStruct((1, atoms), float32),
+        (pooled, partner(pooled), single, mask, pool_w, plddt_w, atom_token, atom_part),
+        scratch=(pltpu.VMEM((chips, 2, tile_rows, width), float32),),
     )
     return (aligned_error, interface_score.reshape(tile_rows), atom_confidence.reshape(atoms))
 

time: 49 us -> 34.3 us (0.70)
  Pallas kernels: 22.3 us -> 16.2 us
  local copies, waits for them, and re-layouts: 4.79 us -> 0 us
  waiting for transfers between devices: 10.7 us -> 6.36 us
  starting transfers between devices: 10.2 us -> 10.8 us
    pallas_call x4 -> x8, Pallas kernels: 22.3 us -> 16.2 us  [run(): pl.pallas_call(kernel, out_shape=out_shapes, in_specs=[VMEM] * held + [HB...]
    unnamed x29 -> x0, local copies, waits for them, and re-layouts: 4.79 us -> none
    ppermute x10, waiting for transfers between devices: 10.7 us -> 6.36 us  [across(): return lax.ppermute(values, axis, [(i, i ^ step) for i in range(count)])]
    ppermute x10, starting transfers between devices: 10.2 us -> 10.8 us  [across(): return lax.ppermute(values, axis, [(i, i ^ step) for i in range(count)])]
  transfers between devices with their start and end apart: 10 -> 10, of which waited for: 5 -> 6; matrix products, arithmetic and copies ran while one was open for 5% -> 0% of each run, Pallas kernels for 0% -> 12%
where the time goes in v2:
time: 34.3 us; the launch traced here: 34.1 us
  Pallas kernels  16.2 us (47%)
  starting transfers between devices  10.8 us (31%)
  waiting for transfers between devices  6.36 us (19%)
  between operations  0.7 us (2%)
    pallas_call x8, Pallas kernels, run(): pl.pallas_call(kernel, out_shape=out_shapes, in_specs=[VMEM] * held + [HB...  16.2 us
    ppermute x10, starting transfers between devices, across(): return lax.ppermute(values, axis, [(i, i ^ step) for i in range(count)])  10.8 us
    ppermute x10, waiting for transfers between devices, across(): return lax.ppermute(values, axis, [(i, i ^ step) for i in range(count)])  6.36 us
  transfers between devices with their start and end apart: 10, of which 6 were waited for; matrix products, arithmetic and copies ran while one was open for 0% of the time, Pallas kernels for 12%

profile of v2, /device:TPU:0, one launch (start us, length us, event | category | flops | bytes accessed | tf_op | source)
XLA Modules:
  0.0 34.1 jit_solution(18362729868217462767)
XLA Ops:
  0.6 0.6 %collective-permute-start = (f32[3,16]{1,0:T(4,128)}, f32[3,16]{1,0:T(4,128)S(1)}, u32[]{:S(2)}, u32[]{:S(2)}) collective-permute-start(f32[3,16]{1,0:T(4,128)} %coords_ref.1), channel_id=1, source_target_pairs={{0,2},{2,0},{4,6},{6,4},{8,10},{10,8},{12,14},{14,12},{1,3},{3,1},... | collective-permute-start | bytes 584 | tf_op jit(solution)/shard_map/ppermute | solution.py:507
  1.2 0.9 %fetch.1 = (bf16[272,128]{1,0:T(8,128)(2,1)S(1)}, f32[3,16]{1,0:T(4,128)S(1)}) custom-call(bf16[256,128]{1,0:T(8,128)(2,1)} %bitcast.10, f32[3,16]{1,0:T(4,128)} %coords_ref.1), custom_call_target="tpu_custom_call" | custom-call | tf_op jit(solution)/shard_map/fetch/pallas_call | solution.py:159
  2.1 0.2 collective-permute-done.other_ref
  2.2 0.1 pack.1.refs_0_
  2.3 2.9 %collective-permute-start.2 = (bf16[272,128]{1,0:T(8,128)(2,1)S(1)}, bf16[272,128]{1,0:T(8,128)(2,1)S(1)}, u32[]{:S(2)}, u32[]{:S(2)}) collective-permute-start(bf16[272,128]{1,0:T(8,128)(2,1)S(1)} %pack.1.refs_0_), channel_id=1, source_target_pairs={{0,4},{2,6},{4,0},{6,2},{8,12},{10,14},{12,8},{14,10},{1,5},{3,7},... | collective-permute-start | bytes 208904 | tf_op jit(solution)/shard_map/ppermute | solution.py:507
  5.2 2.6 %collective-permute-start.4 = (bf16[272,128]{1,0:T(8,128)(2,1)S(1)}, bf16[272,128]{1,0:T(8,128)(2,1)S(1)}, u32[]{:S(2)}, u32[]{:S(2)}) collective-permute-start(bf16[272,128]{1,0:T(8,128)(2,1)S(1)} %pack.1.refs_0_), channel_id=1, source_target_pairs={{0,8},{2,10},{4,12},{6,14},{8,0},{10,2},{12,4},{14,6},{1,9},{3,11}... | collective-permute-start | bytes 208904 | tf_op jit(solution)/shard_map/ppermute | solution.py:507
  7.8 0.0 collective-permute-start.6
  7.8 1.7 %collective-permute-start.1 = (bf16[272,128]{1,0:T(8,128)(2,1)S(1)}, bf16[272,128]{1,0:T(8,128)(2,1)S(1)}, u32[]{:S(2)}, u32[]{:S(2)}) collective-permute-start(bf16[272,128]{1,0:T(8,128)(2,1)S(1)} %pack.1.refs_0_), channel_id=1, source_target_pairs={{0,1},{1,0},{2,3},{3,2},{4,5},{5,4},{6,7},{7,6},{8,9},{9,8},{10,11... | collective-permute-start | bytes 208904 | tf_op jit(solution)/shard_map/ppermute | solution.py:507
  9.5 0.0 collective-permute-done.2.refs_2_
  9.5 0.3 collective-permute-start.3
  9.8 3.2 %collective-permute-done.4.refs_4_ = bf16[272,128]{1,0:T(8,128)(2,1)S(1)} collective-permute-done((bf16[272,128]{1,0:T(8,128)(2,1)S(1)}, bf16[272,128]{1,0:T(8,128)(2,1)S(1)}, u32[]{:S(2)}, u32[]{:S(2)}) %collective-permute-start.4) | collective-permute-done | bytes 69664 | tf_op jit(solution)/shard_map/ppermute | solution.py:507
  13.0 1.5 %collective-permute-start.5 = (bf16[272,128]{1,0:T(8,128)(2,1)S(1)}, bf16[272,128]{1,0:T(8,128)(2,1)S(1)}, u32[]{:S(2)}, u32[]{:S(2)}) collective-permute-start(bf16[272,128]{1,0:T(8,128)(2,1)S(1)} %collective-permute-done.4.refs_4_), channel_id=1, source_target_pairs={{0,1},{1,0},{2,3},{3,2},{4,5},{5,4},{6,7},{7,6},{8,9},{9,8},{10,11... | collective-permute-start | bytes 208904 | tf_op jit(solution)/shard_map/ppermute | solution.py:507
  14.5 0.0 collective-permute-done.6.refs_6_
  14.5 1.0 %collective-permute-start.7 = (bf16[272,128]{1,0:T(8,128)(2,1)S(1)}, bf16[272,128]{1,0:T(8,128)(2,1)S(1)}, u32[]{:S(2)}, u32[]{:S(2)}) collective-permute-start(bf16[272,128]{1,0:T(8,128)(2,1)S(1)} %collective-permute-done.6.refs_6_), channel_id=1, source_target_pairs={{0,1},{1,0},{2,3},{3,2},{4,5},{5,4},{6,7},{7,6},{8,9},{9,8},{10,11... | collective-permute-start | bytes 208904 | tf_op jit(solution)/shard_map/ppermute | solution.py:507
  15.5 1.5 %prepare.1 = (f32[64,128]{1,0:T(8,128)S(1)}, f32[64,128]{1,0:T(8,128)S(1)}, f32[128,128]{1,0:T(8,128)S(1)}, f32[50,16]{1,0:T(8,128)S(1)}, bf16[64,384]{1,0:T(8,1...) custom-call(bf16[272,128]{1,0:T(8,128)(2,1)S(1)} %pack.1.refs_0_, ...), custom_call_target="tpu_custom_call" | custom-call | tf_op jit(solution)/shard_map/prepare/pallas_call | solution.py:159
  17.0 0.0 collective-permute-done.1.refs_1_
  17.0 0.0 collective-permute-done.3.refs_3_
  17.0 0.3 collective-permute-done.5.refs_5_
  17.3 1.5 %collective-permute-done.7.refs_7_ = bf16[272,128]{1,0:T(8,128)(2,1)S(1)} collective-permute-done((bf16[272,128]{1,0:T(8,128)(2,1)S(1)}, bf16[272,128]{1,0:T(8,128)(2,1)S(1)}, u32[]{:S(2)}, u32[]{:S(2)}) %collective-permute-start.7) | collective-permute-done | bytes 69664 | tf_op jit(solution)/shard_map/ppermute | solution.py:507
  18.8 3.0 %edges.1 = (f32[4,8,2,32,128]{4,3,2,1,0:T(8,128)S(1)}, bf16[4,8,2,32,128]{4,3,2,1,0:T(8,128)(2,1)S(1)}, bf16[2,32,4,8,128]{4,3,2,1,0:T(8,128)(2,1)S(1)}) custom-call(bf16[272,128]{1,0:T(8,128)(2,1)S(1)} %pack.1.refs_0_, bf16[272,128]{1,0:T(8,128)(2,1)S(1)} %collective-permute-done.1.refs_1_, bf16[272,128]{1,0:T(8,128)(2,1)S(1)} %collective-permute-done.2.refs_2_, ...), custom_call_target="tpu_custom_call" | custom-call | tf_op jit(solution)/shard_map/edges/pallas_call | solution.py:159
  21.8 0.1 collective-permute-start.8
  21.9 0.7 %left.1 = (f32[4,8,2,32,128]{4,3,2,1,0:T(8,128)S(1)}, f32[4,8,2,32,128]{4,3,2,1,0:T(8,128)S(1)}) custom-call(bf16[4,8,2,32,128]{4,3,2,1,0:T(8,128)(2,1)S(1)} %get-tuple-element.36.normed_ref, bf16[128,640]{1,0:T(8,128)(2,1)S(1)} %get-tuple-element.35.refs_13_.tri_in_ref, s32[1,64]{1,0:T(1,128)S(1)} %get-tuple-element.34.refs_12_.mask_ref.refs_2_), custom_call_target="tpu_custom_call" | custom-call | tf_op jit(solution)/shard_map/left/pallas_call | solution.py:159
  22.6 1.1 %collective-permute-done.8.other_ref = bf16[2,32,4,8,128]{4,3,2,1,0:T(8,128)(2,1)S(1)} collective-permute-done((bf16[2,32,4,8,128]{4,3,2,1,0:T(8,128)(2,1)S(1)}, bf16[2,32,4,8,128]{4,3,2,1,0:T(8,128)(2,1)S(1)}, u32[]{:S(2)}, u32[]{:S(2)}) %collective-permute-start.8) | collective-permute-done | bytes 524320 | tf_op jit(solution)/shard_map/ppermute | solution.py:507
  23.8 7.9 %triangle.1 = (f32[32,128]{1,0:T(8,128)S(1)}, bf16[512,128]{1,0:T(8,128)(2,1)S(1)}) custom-call(f32[4,8,2,32,128]{4,3,2,1,0:T(8,128)S(1)} %get-tuple-element.37.left_ref, bf16[2,32,4,8,128]{4,3,2,1,0:T(8,128)(2,1)S(1)} %get-tuple-element.38.mine_ref, bf16[2,32,4,8,128]{4,3,2,1,0:T(8,128)(2,1)S(1)} %collective-permute-done.8.other_ref, ...), custom_call_target="tpu_custom_call" | custom-call | tf_op jit(solution)/shard_map/triangle/pallas_call | solution.py:159
  31.7 0.2 collective-permute-start.9
  31.9 1.0 %scores.1 = (f32[8,32]{1,0:T(8,128)}, f32[1,8]{1,0:T(1,128)}) custom-call(bf16[512,128]{1,0:T(8,128)(2,1)S(1)} %get-tuple-element.42.refs_0_, bf16[64,128]{1,0:T(8,128)(2,1)S(1)} %get-tuple-element.43.refs_1_, s32[1,64]{1,0:T(1,128)S(1)} %get-tuple-element.34.refs_12_.mask_ref.refs_2_, s32[1,64]{1,0:T(1,128)S(1)} %get-tuple-element.44.refs_3_), custom_call_target="tpu_custom_call" | custom-call | tf_op jit(solution)/shard_map/scores/pallas_call | solution.py:159
  32.9 0.1 collective-permute-done.9.other_ref
  33.0 1.2 %atoms.1 = f32[1,16]{1,0:T(1,128)} custom-call(f32[32,128]{1,0:T(8,128)S(1)} %get-tuple-element.47.mine_ref, f32[32,128]{1,0:T(8,128)S(1)} %collective-permute-done.9.other_ref, bf16[64,384]{1,0:T(8,128)(2,1)S(1)} %get-tuple-element.48.single_ref, s32[1,64]{1,0:T(1,128)S(1)} %get-tuple-element.34.refs_12_.mask_ref.refs_2_, ...), custom_call_target="tpu_custom_call" | custom-call | tf_op jit(solution)/shard_map/atoms/pallas_call | solution.py:159
Async XLA Ops:
  0.6 1.6 %collective-permute-start = (f32[3,16]{1,0:T(4,128)}, f32[3,16]{1,0:T(4,128)S(1)}, u32[]{:S(2)}, u32[]{:S(2)}) collective-permute-start(f32[3,16]{1,0:T(4,128)} %coords_ref.1), channel_id=1, source_target_pairs={{0,2},{2,0},{4,6},{6,4},{8,10},{10,8},{12,14},{14,12},{1,3},{3,1},... | collective-permute-start | bytes 584 | tf_op jit(solution)/shard_map/ppermute | solution.py:507
  2.3 7.2 %collective-permute-start.2 = (bf16[272,128]{1,0:T(8,128)(2,1)S(1)}, bf16[272,128]{1,0:T(8,128)(2,1)S(1)}, u32[]{:S(2)}, u32[]{:S(2)}) collective-permute-start(bf16[272,128]{1,0:T(8,128)(2,1)S(1)} %pack.1.refs_0_), channel_id=1, source_target_pairs={{0,4},{2,6},{4,0},{6,2},{8,12},{10,14},{12,8},{14,10},{1,5},{3,7},... | collective-permute-start | bytes 208904 | tf_op jit(solution)/shard_map/ppermute | solution.py:507
  5.2 7.8 %collective-permute-start.4 = (bf16[272,128]{1,0:T(8,128)(2,1)S(1)}, bf16[272,128]{1,0:T(8,128)(2,1)S(1)}, u32[]{:S(2)}, u32[]{:S(2)}) collective-permute-start(bf16[272,128]{1,0:T(8,128)(2,1)S(1)} %pack.1.refs_0_), channel_id=1, source_target_pairs={{0,8},{2,10},{4,12},{6,14},{8,0},{10,2},{12,4},{14,6},{1,9},{3,11}... | collective-permute-start | bytes 208904 | tf_op jit(solution)/shard_map/ppermute | solution.py:507
  7.8 6.7 %collective-permute-start.6 = (bf16[272,128]{1,0:T(8,128)(2,1)S(1)}, bf16[272,128]{1,0:T(8,128)(2,1)S(1)}, u32[]{:S(2)}, u32[]{:S(2)}) collective-permute-start(bf16[272,128]{1,0:T(8,128)(2,1)S(1)} %pack.1.refs_0_), channel_id=1, source_target_pairs={{0,12},{2,14},{4,8},{6,10},{8,4},{10,6},{12,0},{14,2},{1,13},{3,15... | collective-permute-start | bytes 208904 | tf_op jit(solution)/shard_map/ppermute | solution.py:507
  7.8 9.2 %collective-permute-start.1 = (bf16[272,128]{1,0:T(8,128)(2,1)S(1)}, bf16[272,128]{1,0:T(8,128)(2,1)S(1)}, u32[]{:S(2)}, u32[]{:S(2)}) collective-permute-start(bf16[272,128]{1,0:T(8,128)(2,1)S(1)} %pack.1.refs_0_), channel_id=1, source_target_pairs={{0,1},{1,0},{2,3},{3,2},{4,5},{5,4},{6,7},{7,6},{8,9},{9,8},{10,11... | collective-permute-start | bytes 208904 | tf_op jit(solution)/shard_map/ppermute | solution.py:507
  9.5 7.5 %collective-permute-start.3 = (bf16[272,128]{1,0:T(8,128)(2,1)S(1)}, bf16[272,128]{1,0:T(8,128)(2,1)S(1)}, u32[]{:S(2)}, u32[]{:S(2)}) collective-permute-start(bf16[272,128]{1,0:T(8,128)(2,1)S(1)} %collective-permute-done.2.refs_2_), channel_id=1, source_target_pairs={{0,1},{1,0},{2,3},{3,2},{4,5},{5,4},{6,7},{7,6},{8,9},{9,8},{10,11... | collective-permute-start | bytes 208904 | tf_op jit(solution)/shard_map/ppermute | solution.py:507
  13.0 4.3 %collective-permute-start.5 = (bf16[272,128]{1,0:T(8,128)(2,1)S(1)}, bf16[272,128]{1,0:T(8,128)(2,1)S(1)}, u32[]{:S(2)}, u32[]{:S(2)}) collective-permute-start(bf16[272,128]{1,0:T(8,128)(2,1)S(1)} %collective-permute-done.4.refs_4_), channel_id=1, source_target_pairs={{0,1},{1,0},{2,3},{3,2},{4,5},{5,4},{6,7},{7,6},{8,9},{9,8},{10,11... | collective-permute-start | bytes 208904 | tf_op jit(solution)/shard_map/ppermute | solution.py:507
  14.5 4.3 %collective-permute-start.7 = (bf16[272,128]{1,0:T(8,128)(2,1)S(1)}, bf16[272,128]{1,0:T(8,128)(2,1)S(1)}, u32[]{:S(2)}, u32[]{:S(2)}) collective-permute-start(bf16[272,128]{1,0:T(8,128)(2,1)S(1)} %collective-permute-done.6.refs_6_), channel_id=1, source_target_pairs={{0,1},{1,0},{2,3},{3,2},{4,5},{5,4},{6,7},{7,6},{8,9},{9,8},{10,11... | collective-permute-start | bytes 208904 | tf_op jit(solution)/shard_map/ppermute | solution.py:507
  21.8 2.0 %collective-permute-start.8 = (bf16[2,32,4,8,128]{4,3,2,1,0:T(8,128)(2,1)S(1)}, bf16[2,32,4,8,128]{4,3,2,1,0:T(8,128)(2,1)S(1)}, u32[]{:S(2)}, u32[]{:S(2)}) collective-permute-start(bf16[2,32,4,8,128]{4,3,2,1,0:T(8,128)(2,1)S(1)} %get-tuple-element.38.mine_ref), channel_id=1, source_target_pairs={{0,2},{2,0},{4,6},{6,4},{8,10},{10,8},{12,14},{14,12},{1,3},{3,1},... | collective-permute-start | bytes 1572872 | tf_op jit(solution)/shard_map/ppermute | solution.py:507
  31.7 1.2 %collective-permute-start.9 = (f32[32,128]{1,0:T(8,128)S(1)}, f32[32,128]{1,0:T(8,128)S(1)}, u32[]{:S(2)}, u32[]{:S(2)}) collective-permute-start(f32[32,128]{1,0:T(8,128)S(1)} %get-tuple-element.47.mine_ref), channel_id=1, source_target_pairs={{0,2},{2,0},{4,6},{6,4},{8,10},{10,8},{12,14},{14,12},{1,3},{3,1},... | collective-permute-start | bytes 49160 | tf_op jit(solution)/shard_map/ppermute | solution.py:507

commit v3 on v2

--- a/solution.py
+++ b/solution.py
@@ -146,6 +146,7 @@
 
 
 WHOLE_PAIR_BYTES = 4 * 1024 * 1024
+SPREAD = 1
 SCOPED_BYTES = 16 * 1024 * 1024
 VMEM = pl.BlockSpec(memory_space=pltpu.VMEM)
 
@@ -180,7 +181,11 @@
 
 
 def sigmoid(values):
-    return 1.0 / (1.0 + jnp.exp(-values))
+    return 0.5 * jnp.tanh(0.5 * values) + 0.5
+
+
+def gated(gates, values, half_mask):
+    return (jnp.tanh(0.5 * gates) + 1.0) * values * half_mask
 
 
 def place_of():
@@ -192,11 +197,11 @@
     return jnp.sum(mask_ref[...].astype(jnp.float32), axis=1, keepdims=True)
 
 
-def real_pairs(mask_ref, row_start, col_start, shape):
-    limit = token_count(mask_ref).astype(jnp.int32).reshape(1, 1, 1)
-    rows = lax.broadcasted_iota(jnp.int32, shape, 0) + row_start
-    cols = lax.broadcasted_iota(jnp.int32, shape, 1) + col_start
-    return jnp.where((rows < limit) & (cols < limit), 1.0, 0.0)
+def half_mask(limit, row_start, col_start, shape):
+    rows, cols, width = shape
+    places = lax.broadcasted_iota(jnp.int32, (cols, width), 0) + col_start
+    keys = jnp.where(places < limit, 0.5, 0.0)
+    return jnp.stack([jnp.where(row_start + i < limit, keys, 0.0) for i in range(rows)])
 
 
 def fetch_kernel(z_ref, coords_ref, out_ref, coords_out_ref, arrived):
@@ -250,7 +255,7 @@
 def edge_kernel(slots, col_count, atoms, basis_count, *refs):
     packs = refs[: len(slots)]
     rows_ref, cols_ref, dist_ref, rep_ref, mask_ref, tri_in_ref = refs[len(slots) : len(slots) + 6]
-    pair_ref, normed_ref, right_ref, xyz_ref = refs[len(slots) + 6 :]
+    pair_ref, normed_ref, right_ref, distance_ref = refs[len(slots) + 6 :]
     _, tile_rows, _, tile_cols, width = pair_ref.shape
     tokens = rows_ref.shape[0]
     pairs = tile_rows * tile_cols
@@ -259,23 +264,35 @@
     rep = rep_ref[...]
     order = lax.broadcasted_iota(jnp.int32, (width, tokens), 0)
     picked = jnp.zeros((tokens, 16), jnp.float32)
+    across = jnp.zeros((16, tokens), jnp.float32)
     for pack, (chip_step, col_step) in zip(packs, slots):
         device = 2 * (chip ^ chip_step) * col_count + (col ^ col_step)
         number = jnp.where(
             order < atoms, order + device * atoms, order - atoms + (device + col_count) * atoms
         )
         chosen = (number == rep).astype(jnp.float32).astype(jnp.bfloat16)
+        pieces = pack[pairs:, :]
         picked = picked + lax.dot_general(
-            chosen, pack[pairs:, :], (((0,), (1,)), ((), ())), preferred_element_type=jnp.float32
-        )
+            chosen, pieces, (((0,), (1,)), ((), ())), preferred_element_type=jnp.float32
+        )
+        across = across + jnp.dot(pieces, chosen, preferred_element_type=jnp.float32)
+    square = jnp.zeros((tokens, width), jnp.float32)
     for axis in range(3):
-        whole = picked[:, axis : axis + 1] + picked[:, axis + 3 : axis + 4]
-        whole = whole + picked[:, axis + 6 : axis + 7]
-        xyz_ref[axis] = jnp.broadcast_to(whole, (tokens, width))
+        down = picked[:, axis : axis + 1] + picked[:, axis + 3 : axis + 4]
+        down = down + picked[:, axis + 6 : axis + 7]
+        along = across[axis : axis + 1] + across[axis + 3 : axis + 4] + across[axis + 6 : axis + 7]
+        along = jnp.concatenate([along, jnp.zeros((1, width - tokens), jnp.float32)], axis=1)
+        gap = down - along
+        square = square + gap * gap
+    distance = jnp.sqrt(square)
+    for chip_step in range(pair_ref.shape[0]):
+        first = (2 * (chip ^ chip_step) + half) * tile_rows
+        distance_ref[chip_step] = pltpu.roll(distance, lax.rem(width - first, width), 1)
     step_size = 18.0 / (basis_count - 1)
     centers = 3.375 + step_size * lax.broadcasted_iota(jnp.int32, (1, 1, width), 2).astype(
         jnp.float32
     )
+    limit = token_count(mask_ref).astype(jnp.int32)
     tile = (tile_rows, tile_cols, width)
     tri_in = tri_in_ref[:, 2 * width : 4 * width]
     for pack, (chip_step, col_step) in zip(packs, slots):
@@ -285,11 +302,11 @@
         col_start = pl.multiple_of(at_col * tile_cols, 8)
         row_slice = pl.ds(row_start, tile_rows)
         col_slice = pl.ds(col_start, tile_cols)
-        square = jnp.zeros(tile, jnp.float32)
-        for axis in range(3):
-            gap = xyz_ref[axis, row_slice, :][:, None, :] - xyz_ref[axis, col_slice, :][None]
-            square = square + gap * gap
-        scaled = (jnp.sqrt(square) - centers) * (1.0 / step_size)
+        near = distance_ref[chip_step, col_slice, :]
+        spread = jnp.stack(
+            [jnp.broadcast_to(near[:, i : i + 1], (tile_cols, width)) for i in range(tile_rows)]
+        )
+        scaled = (spread - centers) * (1.0 / step_size)
         basis = jnp.exp(-scaled * scaled).astype(jnp.bfloat16)
         pair = (
             pack[0:pairs, :].astype(jnp.float32).reshape(tile)
@@ -303,14 +320,20 @@
         normed = layer_norm(pair).astype(jnp.bfloat16)
         normed_ref[at_chip, :, at_col] = normed.reshape(tile)
         projected = jnp.dot(normed, tri_in, preferred_element_type=jnp.float32)
-        right = sigmoid(projected[:, 0:width]) * projected[:, width : 2 * width]
-        right = right.reshape(tile) * real_pairs(mask_ref, row_start, col_start, tile)
+        right = gated(
+            projected[:, 0:width].reshape(tile),
+            projected[:, width : 2 * width].reshape(tile),
+            half_mask(limit, row_start, col_start, tile),
+        )
         right_ref[at_col, :, at_chip] = jnp.swapaxes(right, 0, 1).astype(jnp.bfloat16)
 
 
-def left_kernel(normed_ref, tri_in_ref, mask_ref, left_ref, gating_ref):
+def left_kernel(normed_ref, tri_in_ref, mask_ref, turned_ref, gating_ref, left_ref):
     chips, tile_rows, col_count, tile_cols, width = normed_ref.shape
+    tokens = col_count * tile_cols
     _, half, _ = place_of()
+    step = turned_ref.shape[0] // (chips * tile_rows)
+    limit = token_count(mask_ref).astype(jnp.int32)
     pairs = tile_rows * tile_cols
     tile = (tile_rows, tile_cols, width)
     tri_in = jnp.concatenate([tri_in_ref[:, 0 : 2 * width], tri_in_ref[:, 4 * width :]], axis=1)
@@ -318,13 +341,14 @@
         for at_col in range(col_count):
             normed = normed_ref[at_chip, :, at_col].reshape(pairs, width)
             projected = jnp.dot(normed, tri_in, preferred_element_type=jnp.float32)
-            left = sigmoid(projected[:, 0:width]) * projected[:, width : 2 * width]
-            real = real_pairs(
-                mask_ref, (2 * at_chip + half) * tile_rows, at_col * tile_cols, tile
+            left_ref[:, at_col * tile_cols : (at_col + 1) * tile_cols, :] = gated(
+                projected[:, 0:width].reshape(tile),
+                projected[:, width : 2 * width].reshape(tile),
+                half_mask(limit, (2 * at_chip + half) * tile_rows, at_col * tile_cols, tile),
             )
-            left = (left.reshape(tile) * real).astype(jnp.bfloat16)
-            left_ref[at_chip, :, at_col] = left.astype(jnp.float32)
             gating_ref[at_chip, :, at_col] = sigmoid(projected[:, 2 * width :]).reshape(tile)
+        for i in range(tile_rows):
+            turned_ref[pl.ds((at_chip * tile_rows + i) * step, width), :] = left_ref[i].T
 
 
 def triangle_kernel(
@@ -338,36 +362,51 @@
     pooled_ref,
     own_ref,
     right_ref,
+    keys_ref,
+    outer_ref,
     updated_ref,
 ):
     chips, tile_rows, col_count, tile_cols, width = pair_ref.shape
     tokens = col_count * tile_cols
+    queries = chips * tile_rows
+    step = keys_ref.shape[0] // tokens
     chip, half, _ = place_of()
     shape = (tokens, chips, tile_rows, width)
     right_ref[:, :, half] = mine_ref[...].reshape(shape).astype(jnp.float32)
     right_ref[:, :, 1 - half] = other_ref[...].reshape(shape).astype(jnp.float32)
+
+    def turn(token, carry):
+        start = token * step
+        keys_ref[pl.ds(start, width), :] = right_ref[token].reshape(tokens, width).T
+        return carry
+
+    lax.fori_loop(0, tokens, turn, 0, unroll=tokens)
+
+    def multiply(channel, carry):
+        query = left_ref[pl.ds(channel, queries, stride=step), :].astype(jnp.bfloat16)
+        key = keys_ref[pl.ds(channel, tokens, stride=step), :].astype(jnp.bfloat16)
+        outer_ref[pl.ds(channel, queries, stride=step), :] = jnp.dot(
+            query, key, preferred_element_type=jnp.float32
+        )
+        return carry
+
+    lax.fori_loop(0, width, multiply, 0, unroll=width)
     token_order = lax.broadcasted_iota(jnp.int32, (tokens, width), 0)
     real = jnp.where(token_order < token_count(mask_ref).astype(jnp.int32), 1.0, 0.0)
     tri_out = tri_out_ref[...]
-    block = 4
+    block = tile_rows
     blocks = tile_rows // block
 
-    def rows_of(step, carry):
-        at_chip = lax.div(step, blocks)
-        first = lax.rem(step, blocks) * block
-
-        def add_token(token, sums):
-            key = right_ref[token].reshape(tokens, width)
-            key_col = lax.div(token, tile_cols)
-            key_place = lax.rem(token, tile_cols)
-            return tuple(
-                sums[i] + left_ref[at_chip, first + i, key_col, pl.ds(key_place, 1), :] * key
+    def rows_of(group, carry):
+        at_chip = lax.div(group, blocks)
+        first = lax.rem(group, blocks) * block
+        outer = jnp.concatenate(
+            [
+                outer_ref[pl.ds((group * block + i) * step, width), :].T
                 for i in range(block)
-            )
-
-        zero = jnp.zeros((tokens, width), jnp.float32)
-        sums = lax.fori_loop(0, tokens, add_token, (zero,) * block, unroll=8)
-        outer = jnp.concatenate(sums, axis=0)
+            ],
+            axis=0,
+        )
         change = jnp.dot(
             layer_norm(outer).astype(jnp.bfloat16), tri_out, preferred_element_type=jnp.float32
         )
@@ -382,7 +421,7 @@
             )
         return carry
 
-    lax.fori_loop(0, chips * blocks, rows_of, 0)
+    lax.fori_loop(0, chips * blocks, rows_of, 0, unroll=2)
     own_ref[...] = updated_ref[chip].reshape(tile_rows * tokens, width)
 
 
@@ -448,15 +487,19 @@
     pooled_ref[:, half] = mine_ref[...].reshape(chips, tile_rows, width)
     pooled_ref[:, 1 - half] = other_ref[...].reshape(chips, tile_rows, width)
     pooled = pooled_ref[...].reshape(tokens, width) / token_count(mask_ref)
-    single_new = single_ref[...].astype(jnp.float32) + jnp.dot(
-        pooled.astype(jnp.bfloat16), pool_w_ref[...], preferred_element_type=jnp.float32
-    )
-    single_norm = layer_norm(single_new).astype(jnp.bfloat16)
     atoms = atom_token_ref.shape[1]
     order = lax.broadcasted_iota(jnp.int32, (tokens, atoms), 0)
     chosen = (order == atom_token_ref[...]).astype(jnp.float32).astype(jnp.bfloat16)
-    picked = lax.dot_general(
-        chosen, single_norm, (((0,), (0,)), ((), ())), preferred_element_type=jnp.float32
+    turned = (((0,), (0,)), ((), ()))
+    pooled = lax.dot_general(
+        chosen, pooled.astype(jnp.bfloat16), turned, preferred_element_type=jnp.float32
+    )
+    picked = lax.dot_general(chosen, single_ref[...], turned, preferred_element_type=jnp.float32)
+    picked = layer_norm(
+        picked
+        + jnp.dot(
+            pooled.astype(jnp.bfloat16), pool_w_ref[...], preferred_element_type=jnp.float32
+        )
     ).astype(jnp.bfloat16)
     logits = (
         lax.dot_general(
@@ -523,7 +566,16 @@
     )
     slots = [(i, j) for i in range(chips) for j in range(col_count)]
     along = [packed] + [across(packed, "row", row_count, 2 * i) for i in range(1, chips)]
-    packs = [along[i] if j == 0 else across(along[i], "col", col_count, j) for i, j in slots]
+    beside = [packed] + [across(packed, "col", col_count, j) for j in range(1, col_count)]
+
+    def pack_of(i, j):
+        if i == 0 or j == 0:
+            return beside[j] if i == 0 else along[i]
+        if i < chips - 1:
+            return across(beside[j], "row", row_count, 2 * i)
+        return across(along[i], "col", col_count, j)
+
+    packs = [pack_of(i, j) for i, j in slots]
     raw = (w_left, w_right, w_dist, atom_single, atom_w.T)
     kept = (
         single, tri_in, tri_out, pae_w.T, pool_w, plddt_w.T, rep_atom.reshape(1, tokens),
@@ -557,13 +609,15 @@
             pltpu.VMEM((col_count, tile_cols, chips, tile_rows, width), bfloat16),
         ),
         (*packs, rows, cols, dist, rep, mask, tri_in),
-        scratch=(pltpu.VMEM((3, tokens, width), float32),),
-    )
+        scratch=(pltpu.VMEM((chips, tokens, width), float32),),
+    )
+    step = width + SPREAD
     left, gating = run(
         left_kernel,
         "left",
-        (pltpu.VMEM(full, float32), pltpu.VMEM(full, float32)),
+        (pltpu.VMEM((chips * tile_rows * step, tokens), float32), pltpu.VMEM(full, float32)),
         (normed, tri_in, mask),
+        scratch=(pltpu.VMEM((tile_rows, tokens, width), float32),),
     )
     pooled, own = run(
         triangle_kernel,
@@ -575,6 +629,8 @@
         (left, right, partner(right), pair, gating, tri_out, mask),
         scratch=(
             pltpu.VMEM((tokens, chips, 2, tile_rows, width), float32),
+            pltpu.VMEM((tokens * step, tokens), float32),
+            pltpu.VMEM((chips * tile_rows * step, tokens), float32),
             pltpu.VMEM((chips, tile_rows, tokens, width), bfloat16),
         ),
     )

time: 34.3 us -> 29.4 us (0.86)
  Pallas kernels: 16.2 us -> 12 us
  waiting for transfers between devices: 6.36 us -> 3.81 us
  starting transfers between devices: 10.8 us -> 12.7 us
    pallas_call x8, Pallas kernels: 16.2 us -> 12 us  [run(): pl.pallas_call(kernel, out_shape=out_shapes, in_specs=[VMEM] * held + [HB...]
    ppermute x10, waiting for transfers between devices: 6.36 us -> 3.81 us  [across(): return lax.ppermute(values, axis, [(i, i ^ step) for i in range(count)])]
    ppermute x10, starting transfers between devices: 10.8 us -> 12.7 us  [across(): return lax.ppermute(values, axis, [(i, i ^ step) for i in range(count)])]
  transfers between devices with their start and end apart: 10 -> 10, of which waited for: 6 -> 5; matrix products, arithmetic and copies ran while one was open for 0% -> 0% of each run, Pallas kernels for 12% -> 14%
where the time goes in v3:
time: 29.4 us; the launch traced here: 29.3 us
  starting transfers between devices  12.7 us (43%)
  Pallas kernels  12 us (41%)
  waiting for transfers between devices  3.81 us (13%)
  between operations  0.69 us (2%)
    ppermute x10, starting transfers between devices, across(): return lax.ppermute(values, axis, [(i, i ^ step) for i in range(count)])  12.7 us
    pallas_call x8, Pallas kernels, run(): pl.pallas_call(kernel, out_shape=out_shapes, in_specs=[VMEM] * held + [HB...  12 us
    ppermute x10, waiting for transfers between devices, across(): return lax.ppermute(values, axis, [(i, i ^ step) for i in range(count)])  3.81 us
  transfers between devices with their start and end apart: 10, of which 5 were waited for; matrix products, arithmetic and copies ran while one was open for 0% of the time, Pallas kernels for 14%

profile of v3, /device:TPU:0, one launch (start us, length us, event | category | flops | bytes accessed | tf_op | source)
XLA Modules:
  0.0 29.3 jit_solution(14129064173936214147)
XLA Ops:
  0.6 0.6 %collective-permute-start = (f32[3,16]{1,0:T(4,128)}, f32[3,16]{1,0:T(4,128)S(1)}, u32[]{:S(2)}, u32[]{:S(2)}) collective-permute-start(f32[3,16]{1,0:T(4,128)} %coords_ref.1), channel_id=1, source_target_pairs={{0,2},{2,0},{4,6},{6,4},{8,10},{10,8},{12,14},{14,12},{1,3},{3,1},... | collective-permute-start | bytes 584 | tf_op jit(solution)/shard_map/ppermute | solution.py:550
  1.2 0.9 %fetch.1 = (bf16[272,128]{1,0:T(8,128)(2,1)S(1)}, f32[3,16]{1,0:T(4,128)S(1)}) custom-call(bf16[256,128]{1,0:T(8,128)(2,1)} %bitcast.10, f32[3,16]{1,0:T(4,128)} %coords_ref.1), custom_call_target="tpu_custom_call" | custom-call | tf_op jit(solution)/shard_map/fetch/pallas_call | solution.py:160
  2.1 0.2 collective-permute-done.other_ref
  2.2 0.1 pack.1.refs_0_
  2.3 2.8 %collective-permute-start.1 = (bf16[272,128]{1,0:T(8,128)(2,1)S(1)}, bf16[272,128]{1,0:T(8,128)(2,1)S(1)}, u32[]{:S(2)}, u32[]{:S(2)}) collective-permute-start(bf16[272,128]{1,0:T(8,128)(2,1)S(1)} %pack.1.refs_0_), channel_id=1, source_target_pairs={{0,1},{1,0},{2,3},{3,2},{4,5},{5,4},{6,7},{7,6},{8,9},{9,8},{10,11... | collective-permute-start | bytes 208904 | tf_op jit(solution)/shard_map/ppermute | solution.py:550
  5.1 3.6 %collective-permute-start.6 = (bf16[272,128]{1,0:T(8,128)(2,1)S(1)}, bf16[272,128]{1,0:T(8,128)(2,1)S(1)}, u32[]{:S(2)}, u32[]{:S(2)}) collective-permute-start(bf16[272,128]{1,0:T(8,128)(2,1)S(1)} %pack.1.refs_0_), channel_id=1, source_target_pairs={{0,12},{2,14},{4,8},{6,10},{8,4},{10,6},{12,0},{14,2},{1,13},{3,15... | collective-permute-start | bytes 208904 | tf_op jit(solution)/shard_map/ppermute | solution.py:550
  8.7 0.0 collective-permute-start.2
  8.7 0.8 %collective-permute-start.4 = (bf16[272,128]{1,0:T(8,128)(2,1)S(1)}, bf16[272,128]{1,0:T(8,128)(2,1)S(1)}, u32[]{:S(2)}, u32[]{:S(2)}) collective-permute-start(bf16[272,128]{1,0:T(8,128)(2,1)S(1)} %pack.1.refs_0_), channel_id=1, source_target_pairs={{0,8},{2,10},{4,12},{6,14},{8,0},{10,2},{12,4},{14,6},{1,9},{3,11}... | collective-permute-start | bytes 208904 | tf_op jit(solution)/shard_map/ppermute | solution.py:550
  9.5 0.0 collective-permute-done.1.refs_1_
  9.5 1.2 %collective-permute-start.3 = (bf16[272,128]{1,0:T(8,128)(2,1)S(1)}, bf16[272,128]{1,0:T(8,128)(2,1)S(1)}, u32[]{:S(2)}, u32[]{:S(2)}) collective-permute-start(bf16[272,128]{1,0:T(8,128)(2,1)S(1)} %collective-permute-done.1.refs_1_), channel_id=1, source_target_pairs={{0,4},{2,6},{4,0},{6,2},{8,12},{10,14},{12,8},{14,10},{1,5},{3,7},... | collective-permute-start | bytes 208904 | tf_op jit(solution)/shard_map/ppermute | solution.py:550
  10.8 2.9 %collective-permute-start.5 = (bf16[272,128]{1,0:T(8,128)(2,1)S(1)}, bf16[272,128]{1,0:T(8,128)(2,1)S(1)}, u32[]{:S(2)}, u32[]{:S(2)}) collective-permute-start(bf16[272,128]{1,0:T(8,128)(2,1)S(1)} %collective-permute-done.1.refs_1_), channel_id=1, source_target_pairs={{0,8},{2,10},{4,12},{6,14},{8,0},{10,2},{12,4},{14,6},{1,9},{3,11}... | collective-permute-start | bytes 208904 | tf_op jit(solution)/shard_map/ppermute | solution.py:550
  13.7 0.0 collective-permute-done.6.refs_6_
  13.7 0.5 %collective-permute-start.7 = (bf16[272,128]{1,0:T(8,128)(2,1)S(1)}, bf16[272,128]{1,0:T(8,128)(2,1)S(1)}, u32[]{:S(2)}, u32[]{:S(2)}) collective-permute-start(bf16[272,128]{1,0:T(8,128)(2,1)S(1)} %collective-permute-done.6.refs_6_), channel_id=1, source_target_pairs={{0,1},{1,0},{2,3},{3,2},{4,5},{5,4},{6,7},{7,6},{8,9},{9,8},{10,11... | collective-permute-start | bytes 208904 | tf_op jit(solution)/shard_map/ppermute | solution.py:550
  14.2 1.5 %prepare.1 = (f32[64,128]{1,0:T(8,128)S(1)}, f32[64,128]{1,0:T(8,128)S(1)}, f32[128,128]{1,0:T(8,128)S(1)}, f32[50,16]{1,0:T(8,128)S(1)}, bf16[64,384]{1,0:T(8,1...) custom-call(bf16[272,128]{1,0:T(8,128)(2,1)S(1)} %pack.1.refs_0_, ...), custom_call_target="tpu_custom_call" | custom-call | tf_op jit(solution)/shard_map/prepare/pallas_call | solution.py:160
  15.7 0.0 collective-permute-done.2.refs_2_
  15.7 1.0 %collective-permute-done.4.refs_4_ = bf16[272,128]{1,0:T(8,128)(2,1)S(1)} collective-permute-done((bf16[272,128]{1,0:T(8,128)(2,1)S(1)}, bf16[272,128]{1,0:T(8,128)(2,1)S(1)}, u32[]{:S(2)}, u32[]{:S(2)}) %collective-permute-start.4) | collective-permute-done | bytes 69664 | tf_op jit(solution)/shard_map/ppermute | solution.py:550
  16.7 0.0 collective-permute-done.3.refs_3_
  16.7 1.5 %collective-permute-done.5.refs_5_ = bf16[272,128]{1,0:T(8,128)(2,1)S(1)} collective-permute-done((bf16[272,128]{1,0:T(8,128)(2,1)S(1)}, bf16[272,128]{1,0:T(8,128)(2,1)S(1)}, u32[]{:S(2)}, u32[]{:S(2)}) %collective-permute-start.5) | collective-permute-done | bytes 69664 | tf_op jit(solution)/shard_map/ppermute | solution.py:550
  18.2 0.0 collective-permute-done.7.refs_7_
  18.2 2.8 %edges.1 = (f32[4,8,2,32,128]{4,3,2,1,0:T(8,128)S(1)}, bf16[4,8,2,32,128]{4,3,2,1,0:T(8,128)(2,1)S(1)}, bf16[2,32,4,8,128]{4,3,2,1,0:T(8,128)(2,1)S(1)}) custom-call(bf16[272,128]{1,0:T(8,128)(2,1)S(1)} %pack.1.refs_0_, bf16[272,128]{1,0:T(8,128)(2,1)S(1)} %collective-permute-done.1.refs_1_, bf16[272,128]{1,0:T(8,128)(2,1)S(1)} %collective-permute-done.2.refs_2_, ...), custom_call_target="tpu_custom_call" | custom-call | tf_op jit(solution)/shard_map/edges/pallas_call | solution.py:160
  21.1 0.1 collective-permute-start.8
  21.1 0.8 %left.1 = (f32[4128,64]{1,0:T(8,128)S(1)}, f32[4,8,2,32,128]{4,3,2,1,0:T(8,128)S(1)}) custom-call(bf16[4,8,2,32,128]{4,3,2,1,0:T(8,128)(2,1)S(1)} %get-tuple-element.36.normed_ref, bf16[128,640]{1,0:T(8,128)(2,1)S(1)} %get-tuple-element.35.refs_13_.tri_in_ref, s32[1,64]{1,0:T(1,128)S(1)} %get-tuple-element.34.refs_12_.mask_ref.refs_2_), custom_call_target="tpu_custom_call" | custom-call | tf_op jit(solution)/shard_map/left/pallas_call | solution.py:160
  22.0 1.1 %collective-permute-done.8.other_ref = bf16[2,32,4,8,128]{4,3,2,1,0:T(8,128)(2,1)S(1)} collective-permute-done((bf16[2,32,4,8,128]{4,3,2,1,0:T(8,128)(2,1)S(1)}, bf16[2,32,4,8,128]{4,3,2,1,0:T(8,128)(2,1)S(1)}, u32[]{:S(2)}, u32[]{:S(2)}) %collective-permute-start.8) | collective-permute-done | bytes 524320 | tf_op jit(solution)/shard_map/ppermute | solution.py:550
  23.0 3.8 %triangle.1 = (f32[32,128]{1,0:T(8,128)S(1)}, bf16[512,128]{1,0:T(8,128)(2,1)S(1)}) custom-call(f32[4128,64]{1,0:T(8,128)S(1)} %get-tuple-element.37.left_ref, bf16[2,32,4,8,128]{4,3,2,1,0:T(8,128)(2,1)S(1)} %get-tuple-element.38.mine_ref, bf16[2,32,4,8,128]{4,3,2,1,0:T(8,128)(2,1)S(1)} %collective-permute-done.8.other_ref, ...), custom_call_target="tpu_custom_call" | custom-call | tf_op jit(solution)/shard_map/triangle/pallas_call | solution.py:160
  26.8 0.2 collective-permute-start.9
  27.0 1.0 %scores.1 = (f32[8,32]{1,0:T(8,128)}, f32[1,8]{1,0:T(1,128)}) custom-call(bf16[512,128]{1,0:T(8,128)(2,1)S(1)} %get-tuple-element.42.refs_0_, bf16[64,128]{1,0:T(8,128)(2,1)S(1)} %get-tuple-element.43.refs_1_, s32[1,64]{1,0:T(1,128)S(1)} %get-tuple-element.34.refs_12_.mask_ref.refs_2_, s32[1,64]{1,0:T(1,128)S(1)} %get-tuple-element.44.refs_3_), custom_call_target="tpu_custom_call" | custom-call | tf_op jit(solution)/shard_map/scores/pallas_call | solution.py:160
  28.0 0.1 collective-permute-done.9.other_ref
  28.1 1.2 %atoms.1 = f32[1,16]{1,0:T(1,128)} custom-call(f32[32,128]{1,0:T(8,128)S(1)} %get-tuple-element.47.mine_ref, f32[32,128]{1,0:T(8,128)S(1)} %collective-permute-done.9.other_ref, bf16[64,384]{1,0:T(8,128)(2,1)S(1)} %get-tuple-element.48.single_ref, s32[1,64]{1,0:T(1,128)S(1)} %get-tuple-element.34.refs_12_.mask_ref.refs_2_, ...), custom_call_target="tpu_custom_call" | custom-call | tf_op jit(solution)/shard_map/atoms/pallas_call | solution.py:160
Async XLA Ops:
  0.6 1.6 %collective-permute-start = (f32[3,16]{1,0:T(4,128)}, f32[3,16]{1,0:T(4,128)S(1)}, u32[]{:S(2)}, u32[]{:S(2)}) collective-permute-start(f32[3,16]{1,0:T(4,128)} %coords_ref.1), channel_id=1, source_target_pairs={{0,2},{2,0},{4,6},{6,4},{8,10},{10,8},{12,14},{14,12},{1,3},{3,1},... | collective-permute-start | bytes 584 | tf_op jit(solution)/shard_map/ppermute | solution.py:550
  2.3 7.2 %collective-permute-start.1 = (bf16[272,128]{1,0:T(8,128)(2,1)S(1)}, bf16[272,128]{1,0:T(8,128)(2,1)S(1)}, u32[]{:S(2)}, u32[]{:S(2)}) collective-permute-start(bf16[272,128]{1,0:T(8,128)(2,1)S(1)} %pack.1.refs_0_), channel_id=1, source_target_pairs={{0,1},{1,0},{2,3},{3,2},{4,5},{5,4},{6,7},{7,6},{8,9},{9,8},{10,11... | collective-permute-start | bytes 208904 | tf_op jit(solution)/shard_map/ppermute | solution.py:550
  5.1 8.6 %collective-permute-start.6 = (bf16[272,128]{1,0:T(8,128)(2,1)S(1)}, bf16[272,128]{1,0:T(8,128)(2,1)S(1)}, u32[]{:S(2)}, u32[]{:S(2)}) collective-permute-start(bf16[272,128]{1,0:T(8,128)(2,1)S(1)} %pack.1.refs_0_), channel_id=1, source_target_pairs={{0,12},{2,14},{4,8},{6,10},{8,4},{10,6},{12,0},{14,2},{1,13},{3,15... | collective-permute-start | bytes 208904 | tf_op jit(solution)/shard_map/ppermute | solution.py:550
  8.7 7.0 %collective-permute-start.2 = (bf16[272,128]{1,0:T(8,128)(2,1)S(1)}, bf16[272,128]{1,0:T(8,128)(2,1)S(1)}, u32[]{:S(2)}, u32[]{:S(2)}) collective-permute-start(bf16[272,128]{1,0:T(8,128)(2,1)S(1)} %pack.1.refs_0_), channel_id=1, source_target_pairs={{0,4},{2,6},{4,0},{6,2},{8,12},{10,14},{12,8},{14,10},{1,5},{3,7},... | collective-permute-start | bytes 208904 | tf_op jit(solution)/shard_map/ppermute | solution.py:550
  8.7 8.0 %collective-permute-start.4 = (bf16[272,128]{1,0:T(8,128)(2,1)S(1)}, bf16[272,128]{1,0:T(8,128)(2,1)S(1)}, u32[]{:S(2)}, u32[]{:S(2)}) collective-permute-start(bf16[272,128]{1,0:T(8,128)(2,1)S(1)} %pack.1.refs_0_), channel_id=1, source_target_pairs={{0,8},{2,10},{4,12},{6,14},{8,0},{10,2},{12,4},{14,6},{1,9},{3,11}... | collective-permute-start | bytes 208904 | tf_op jit(solution)/shard_map/ppermute | solution.py:550
  9.5 7.2 %collective-permute-start.3 = (bf16[272,128]{1,0:T(8,128)(2,1)S(1)}, bf16[272,128]{1,0:T(8,128)(2,1)S(1)}, u32[]{:S(2)}, u32[]{:S(2)}) collective-permute-start(bf16[272,128]{1,0:T(8,128)(2,1)S(1)} %collective-permute-done.1.refs_1_), channel_id=1, source_target_pairs={{0,4},{2,6},{4,0},{6,2},{8,12},{10,14},{12,8},{14,10},{1,5},{3,7},... | collective-permute-start | bytes 208904 | tf_op jit(solution)/shard_map/ppermute | solution.py:550
  10.8 7.5 %collective-permute-start.5 = (bf16[272,128]{1,0:T(8,128)(2,1)S(1)}, bf16[272,128]{1,0:T(8,128)(2,1)S(1)}, u32[]{:S(2)}, u32[]{:S(2)}) collective-permute-start(bf16[272,128]{1,0:T(8,128)(2,1)S(1)} %collective-permute-done.1.refs_1_), channel_id=1, source_target_pairs={{0,8},{2,10},{4,12},{6,14},{8,0},{10,2},{12,4},{14,6},{1,9},{3,11}... | collective-permute-start | bytes 208904 | tf_op jit(solution)/shard_map/ppermute | solution.py:550
  13.7 4.5 %collective-permute-start.7 = (bf16[272,128]{1,0:T(8,128)(2,1)S(1)}, bf16[272,128]{1,0:T(8,128)(2,1)S(1)}, u32[]{:S(2)}, u32[]{:S(2)}) collective-permute-start(bf16[272,128]{1,0:T(8,128)(2,1)S(1)} %collective-permute-done.6.refs_6_), channel_id=1, source_target_pairs={{0,1},{1,0},{2,3},{3,2},{4,5},{5,4},{6,7},{7,6},{8,9},{9,8},{10,11... | collective-permute-start | bytes 208904 | tf_op jit(solution)/shard_map/ppermute | solution.py:550
  21.1 2.0 %collective-permute-start.8 = (bf16[2,32,4,8,128]{4,3,2,1,0:T(8,128)(2,1)S(1)}, bf16[2,32,4,8,128]{4,3,2,1,0:T(8,128)(2,1)S(1)}, u32[]{:S(2)}, u32[]{:S(2)}) collective-permute-start(bf16[2,32,4,8,128]{4,3,2,1,0:T(8,128)(2,1)S(1)} %get-tuple-element.38.mine_ref), channel_id=1, source_target_pairs={{0,2},{2,0},{4,6},{6,4},{8,10},{10,8},{12,14},{14,12},{1,3},{3,1},... | collective-permute-start | bytes 1572872 | tf_op jit(solution)/shard_map/ppermute | solution.py:550
  26.8 1.2 %collective-permute-start.9 = (f32[32,128]{1,0:T(8,128)S(1)}, f32[32,128]{1,0:T(8,128)S(1)}, u32[]{:S(2)}, u32[]{:S(2)}) collective-permute-start(f32[32,128]{1,0:T(8,128)S(1)} %get-tuple-element.47.mine_ref), channel_id=1, source_target_pairs={{0,2},{2,0},{4,6},{6,4},{8,10},{10,8},{12,14},{14,12},{1,3},{3,1},... | collective-permute-start | bytes 49160 | tf_op jit(solution)/shard_map/ppermute | solution.py:550

commit v4 on v3

--- a/solution.py
+++ b/solution.py
@@ -204,6 +204,13 @@
     return jnp.stack([jnp.where(row_start + i < limit, keys, 0.0) for i in range(rows)])
 
 
+def spread_keys(target, at_chip, at_col, half, tile):
+    rows, cols, _ = tile.shape
+    for group in range(cols // rows):
+        chip = at_col * (cols // (2 * rows)) + group // 2
+        target[at_chip, :, (group % 2) ^ half, chip] = tile[:, group * rows : (group + 1) * rows]
+
+
 def fetch_kernel(z_ref, coords_ref, out_ref, coords_out_ref, arrived):
     pairs = z_ref.shape[0]
     bring((z_ref, coords_ref), (out_ref.at[0:pairs, :], coords_out_ref), arrived)
@@ -256,7 +263,7 @@
     packs = refs[: len(slots)]
     rows_ref, cols_ref, dist_ref, rep_ref, mask_ref, tri_in_ref = refs[len(slots) : len(slots) + 6]
     pair_ref, normed_ref, right_ref, distance_ref = refs[len(slots) + 6 :]
-    _, tile_rows, _, tile_cols, width = pair_ref.shape
+    _, tile_rows, _, tile_cols, width = normed_ref.shape
     tokens = rows_ref.shape[0]
     pairs = tile_rows * tile_cols
     chip, half, col = place_of()
@@ -316,7 +323,7 @@
         pair = pair.reshape(pairs, width) + jnp.dot(
             basis.reshape(pairs, width), w_dist, preferred_element_type=jnp.float32
         )
-        pair_ref[at_chip, :, at_col] = pair.reshape(tile)
+        spread_keys(pair_ref, at_chip, at_col, half, pair.reshape(tile))
         normed = layer_norm(pair).astype(jnp.bfloat16)
         normed_ref[at_chip, :, at_col] = normed.reshape(tile)
         projected = jnp.dot(normed, tri_in, preferred_element_type=jnp.float32)
@@ -325,10 +332,12 @@
             projected[:, width : 2 * width].reshape(tile),
             half_mask(limit, row_start, col_start, tile),
         )
-        right_ref[at_col, :, at_chip] = jnp.swapaxes(right, 0, 1).astype(jnp.bfloat16)
-
-
-def left_kernel(normed_ref, tri_in_ref, mask_ref, turned_ref, gating_ref, left_ref):
+        right_ref[at_chip, :, at_col] = right.astype(jnp.bfloat16)
+
+
+def left_kernel(
+    normed_ref, right_ref, tri_in_ref, mask_ref, turned_ref, keys_ref, gating_ref, left_ref
+):
     chips, tile_rows, col_count, tile_cols, width = normed_ref.shape
     tokens = col_count * tile_cols
     _, half, _ = place_of()
@@ -346,9 +355,14 @@
                 projected[:, width : 2 * width].reshape(tile),
                 half_mask(limit, (2 * at_chip + half) * tile_rows, at_col * tile_cols, tile),
             )
-            gating_ref[at_chip, :, at_col] = sigmoid(projected[:, 2 * width :]).reshape(tile)
+            spread_keys(
+                gating_ref, at_chip, at_col, half, sigmoid(projected[:, 2 * width :]).reshape(tile)
+            )
         for i in range(tile_rows):
-            turned_ref[pl.ds((at_chip * tile_rows + i) * step, width), :] = left_ref[i].T
+            rows = pl.ds((at_chip * tile_rows + i) * step, width)
+            turned_ref[rows, :] = left_ref[i].T
+            key = right_ref[at_chip, i].reshape(tokens, width).astype(jnp.float32)
+            keys_ref[rows, :] = key.T
 
 
 def triangle_kernel(
@@ -361,68 +375,56 @@
     mask_ref,
     pooled_ref,
     own_ref,
-    right_ref,
     keys_ref,
     outer_ref,
     updated_ref,
 ):
-    chips, tile_rows, col_count, tile_cols, width = pair_ref.shape
-    tokens = col_count * tile_cols
+    chips, tile_rows, _, _, _, width = pair_ref.shape
+    tokens = 2 * chips * tile_rows
     queries = chips * tile_rows
-    step = keys_ref.shape[0] // tokens
+    step = keys_ref.shape[0] // queries
     chip, half, _ = place_of()
-    shape = (tokens, chips, tile_rows, width)
-    right_ref[:, :, half] = mine_ref[...].reshape(shape).astype(jnp.float32)
-    right_ref[:, :, 1 - half] = other_ref[...].reshape(shape).astype(jnp.float32)
-
-    def turn(token, carry):
-        start = token * step
-        keys_ref[pl.ds(start, width), :] = right_ref[token].reshape(tokens, width).T
-        return carry
-
-    lax.fori_loop(0, tokens, turn, 0, unroll=tokens)
-
-    def multiply(channel, carry):
-        query = left_ref[pl.ds(channel, queries, stride=step), :].astype(jnp.bfloat16)
-        key = keys_ref[pl.ds(channel, tokens, stride=step), :].astype(jnp.bfloat16)
-        outer_ref[pl.ds(channel, queries, stride=step), :] = jnp.dot(
-            query, key, preferred_element_type=jnp.float32
-        )
-        return carry
-
-    lax.fori_loop(0, width, multiply, 0, unroll=width)
-    token_order = lax.broadcasted_iota(jnp.int32, (tokens, width), 0)
-    real = jnp.where(token_order < token_count(mask_ref).astype(jnp.int32), 1.0, 0.0)
+    for at_chip in range(chips):
+        for i in range(tile_rows):
+            key = other_ref[at_chip, i].reshape(tokens, width).astype(jnp.float32)
+            keys_ref[pl.ds((at_chip * tile_rows + i) * step, width), :] = key.T
+    for channel in range(width):
+        rows = pl.ds(channel, queries, stride=step)
+        query = left_ref[rows, :].astype(jnp.bfloat16)
+        key = jnp.concatenate([mine_ref[rows, :], keys_ref[rows, :]], axis=0)
+        outer_ref[rows, :] = lax.dot_general(
+            query,
+            key.astype(jnp.bfloat16),
+            (((1,), (1,)), ((), ())),
+            preferred_element_type=jnp.float32,
+        )
+    place = lax.broadcasted_iota(jnp.int32, (tokens, width), 0)
+    key_half = jnp.where(place < queries, half, 1 - half)
+    place = jnp.where(place < queries, place, place - queries)
+    token = 2 * place - lax.rem(place, tile_rows) + key_half * tile_rows
+    real = jnp.where(token < token_count(mask_ref).astype(jnp.int32), 1.0, 0.0)
     tri_out = tri_out_ref[...]
-    block = tile_rows
-    blocks = tile_rows // block
-
-    def rows_of(group, carry):
-        at_chip = lax.div(group, blocks)
-        first = lax.rem(group, blocks) * block
+    for at_chip in range(chips):
         outer = jnp.concatenate(
             [
-                outer_ref[pl.ds((group * block + i) * step, width), :].T
-                for i in range(block)
+                outer_ref[pl.ds((at_chip * tile_rows + i) * step, width), :].T
+                for i in range(tile_rows)
             ],
             axis=0,
         )
         change = jnp.dot(
             layer_norm(outer).astype(jnp.bfloat16), tri_out, preferred_element_type=jnp.float32
         )
-        for i in range(block):
-            gating = gating_ref[at_chip, first + i].reshape(tokens, width)
-            updated = pair_ref[at_chip, first + i].reshape(tokens, width) + gating * (
+        for i in range(tile_rows):
+            gating = gating_ref[at_chip, i].reshape(tokens, width)
+            updated = pair_ref[at_chip, i].reshape(tokens, width) + gating * (
                 change[i * tokens : (i + 1) * tokens]
             )
-            updated_ref[at_chip, first + i] = updated.astype(jnp.bfloat16)
-            pooled_ref[pl.ds(at_chip * tile_rows + first + i, 1), :] = jnp.sum(
-                updated * real, axis=0, keepdims=True
-            )
-        return carry
-
-    lax.fori_loop(0, chips * blocks, rows_of, 0, unroll=2)
-    own_ref[...] = updated_ref[chip].reshape(tile_rows * tokens, width)
+            updated_ref[at_chip, i] = updated.reshape(2, chips, tile_rows, width)
+            row = at_chip * tile_rows + i
+            pooled_ref[row : row + 1, :] = jnp.sum(updated * real, axis=0, keepdims=True)
+    own_ref[:, :, half] = updated_ref[chip, :, 0]
+    own_ref[:, :, 1 - half] = updated_ref[chip, :, 1]
 
 
 def score_kernel(
@@ -434,7 +436,7 @@
     bins = pae_w_ref.shape[0]
     logits = lax.dot_general(
         pae_w_ref[...],
-        own_ref[...],
+        own_ref[...].reshape(tile_rows * tokens, own_ref.shape[-1]).astype(jnp.bfloat16),
         (((1,), (1,)), ((), ())),
         preferred_element_type=jnp.float32,
     )
@@ -536,7 +538,8 @@
     tile_rows, tile_cols, width = z_trunk.shape
     tokens = single.shape[0]
     atoms = atom_coords.shape[1]
-    if tokens * tokens * width * 4 > WHOLE_PAIR_BYTES or 2 * atoms > width:
+    fits = 2 * atoms <= width and tile_cols % (2 * tile_rows) == 0 and tile_rows % 8 == 0
+    if tokens * tokens * width * 4 > WHOLE_PAIR_BYTES or not fits:
         return per_device(
             z_trunk, single, atom_coords, atom_single, rep_atom, atom_token, token_mask, chain_id,
             w_left, w_right, w_dist, tri_in, tri_out, pae_w, pool_w, plddt_w, atom_w,
@@ -600,23 +603,20 @@
     )
     single, tri_in, tri_out, pae_w, pool_w, plddt_w, rep, mask, chain, atom_token = kept
     full = (chips, tile_rows, col_count, tile_cols, width)
+    by_half = pltpu.VMEM((chips, tile_rows, 2, chips, tile_rows, width), float32)
     pair, normed, right = run(
         lambda *refs: edge_kernel(slots, col_count, atoms, w_dist.shape[0], *refs),
         "edges",
-        (
-            pltpu.VMEM(full, float32),
-            pltpu.VMEM(full, bfloat16),
-            pltpu.VMEM((col_count, tile_cols, chips, tile_rows, width), bfloat16),
-        ),
+        (by_half, pltpu.VMEM(full, bfloat16), pltpu.VMEM(full, bfloat16)),
         (*packs, rows, cols, dist, rep, mask, tri_in),
         scratch=(pltpu.VMEM((chips, tokens, width), float32),),
     )
-    step = width + SPREAD
-    left, gating = run(
+    turned = pltpu.VMEM((chips * tile_rows * (width + SPREAD), tokens), float32)
+    left, keys, gating = run(
         left_kernel,
         "left",
-        (pltpu.VMEM((chips * tile_rows * step, tokens), float32), pltpu.VMEM(full, float32)),
-        (normed, tri_in, mask),
+        (turned, turned, by_half),
+        (normed, right, tri_in, mask),
         scratch=(pltpu.VMEM((tile_rows, tokens, width), float32),),
     )
     pooled, own = run(
@@ -624,15 +624,10 @@
         "triangle",
         (
             pltpu.VMEM((chips * tile_rows, width), float32),
-            pltpu.VMEM((tile_rows * tokens, width), bfloat16),
+            pltpu.VMEM((tile_rows, chips, 2, tile_rows, width), float32),
         ),
-        (left, right, partner(right), pair, gating, tri_out, mask),
-        scratch=(
-            pltpu.VMEM((tokens, chips, 2, tile_rows, width), float32),
-            pltpu.VMEM((tokens * step, tokens), float32),
-            pltpu.VMEM((chips * tile_rows * step, tokens), float32),
-            pltpu.VMEM((chips, tile_rows, tokens, width), bfloat16),
-        ),
+        (left, keys, partner(right), pair, gating, tri_out, mask),
+        scratch=(turned, turned, by_half),
     )
     tm_scale = 1.24 * (max(tokens, 19) - 15) ** (1.0 / 3.0) - 1.8
     aligned_error, interface_score = run(

time: 29.4 us -> 28.7 us (0.976)
  Pallas kernels: 12 us -> 11.5 us
    pallas_call x8, Pallas kernels: 12 us -> 11.5 us  [run(): pl.pallas_call(kernel, out_shape=out_shapes, in_specs=[VMEM] * held + [HB...]
  transfers between devices with their start and end apart: 10 -> 10, of which waited for: 5 -> 5; matrix products, arithmetic and copies ran while one was open for 0% -> 0% of each run, Pallas kernels for 14% -> 15%
where the time goes in v4:
time: 28.7 us; the launch traced here: 28.5 us
  starting transfers between devices  12.7 us (44%)
  Pallas kernels  11.5 us (40%)
  waiting for transfers between devices  3.57 us (12%)
  between operations  0.69 us (2%)
    ppermute x10, starting transfers between devices, across(): return lax.ppermute(values, axis, [(i, i ^ step) for i in range(count)])  12.7 us
    pallas_call x8, Pallas kernels, run(): pl.pallas_call(kernel, out_shape=out_shapes, in_specs=[VMEM] * held + [HB...  11.5 us
    ppermute x10, waiting for transfers between devices, across(): return lax.ppermute(values, axis, [(i, i ^ step) for i in range(count)])  3.57 us
  transfers between devices with their start and end apart: 10, of which 5 were waited for; matrix products, arithmetic and copies ran while one was open for 0% of the time, Pallas kernels for 15%

profile of v4, /device:TPU:0, one launch (start us, length us, event | category | flops | bytes accessed | tf_op | source)
XLA Modules:
  0.0 28.5 jit_solution(3847011373074458522)
XLA Ops:
  0.6 0.6 %collective-permute-start = (f32[3,16]{1,0:T(4,128)}, f32[3,16]{1,0:T(4,128)S(1)}, u32[]{:S(2)}, u32[]{:S(2)}) collective-permute-start(f32[3,16]{1,0:T(4,128)} %coords_ref.1), channel_id=1, source_target_pairs={{0,2},{2,0},{4,6},{6,4},{8,10},{10,8},{12,14},{14,12},{1,3},{3,1},... | collective-permute-start | bytes 584 | tf_op jit(solution)/shard_map/ppermute | solution.py:553
  1.2 0.9 %fetch.1 = (bf16[272,128]{1,0:T(8,128)(2,1)S(1)}, f32[3,16]{1,0:T(4,128)S(1)}) custom-call(bf16[256,128]{1,0:T(8,128)(2,1)} %bitcast.10, f32[3,16]{1,0:T(4,128)} %coords_ref.1), custom_call_target="tpu_custom_call" | custom-call | tf_op jit(solution)/shard_map/fetch/pallas_call | solution.py:160
  2.1 0.2 collective-permute-done.other_ref
  2.2 0.1 pack.1.refs_0_
  2.3 2.8 %collective-permute-start.1 = (bf16[272,128]{1,0:T(8,128)(2,1)S(1)}, bf16[272,128]{1,0:T(8,128)(2,1)S(1)}, u32[]{:S(2)}, u32[]{:S(2)}) collective-permute-start(bf16[272,128]{1,0:T(8,128)(2,1)S(1)} %pack.1.refs_0_), channel_id=1, source_target_pairs={{0,1},{1,0},{2,3},{3,2},{4,5},{5,4},{6,7},{7,6},{8,9},{9,8},{10,11... | collective-permute-start | bytes 208904 | tf_op jit(solution)/shard_map/ppermute | solution.py:553
  5.1 3.6 %collective-permute-start.6 = (bf16[272,128]{1,0:T(8,128)(2,1)S(1)}, bf16[272,128]{1,0:T(8,128)(2,1)S(1)}, u32[]{:S(2)}, u32[]{:S(2)}) collective-permute-start(bf16[272,128]{1,0:T(8,128)(2,1)S(1)} %pack.1.refs_0_), channel_id=1, source_target_pairs={{0,12},{2,14},{4,8},{6,10},{8,4},{10,6},{12,0},{14,2},{1,13},{3,15... | collective-permute-start | bytes 208904 | tf_op jit(solution)/shard_map/ppermute | solution.py:553
  8.7 0.0 collective-permute-start.2
  8.7 0.8 %collective-permute-start.4 = (bf16[272,128]{1,0:T(8,128)(2,1)S(1)}, bf16[272,128]{1,0:T(8,128)(2,1)S(1)}, u32[]{:S(2)}, u32[]{:S(2)}) collective-permute-start(bf16[272,128]{1,0:T(8,128)(2,1)S(1)} %pack.1.refs_0_), channel_id=1, source_target_pairs={{0,8},{2,10},{4,12},{6,14},{8,0},{10,2},{12,4},{14,6},{1,9},{3,11}... | collective-permute-start | bytes 208904 | tf_op jit(solution)/shard_map/ppermute | solution.py:553
  9.5 0.0 collective-permute-done.1.refs_1_
  9.5 1.2 %collective-permute-start.3 = (bf16[272,128]{1,0:T(8,128)(2,1)S(1)}, bf16[272,128]{1,0:T(8,128)(2,1)S(1)}, u32[]{:S(2)}, u32[]{:S(2)}) collective-permute-start(bf16[272,128]{1,0:T(8,128)(2,1)S(1)} %collective-permute-done.1.refs_1_), channel_id=1, source_target_pairs={{0,4},{2,6},{4,0},{6,2},{8,12},{10,14},{12,8},{14,10},{1,5},{3,7},... | collective-permute-start | bytes 208904 | tf_op jit(solution)/shard_map/ppermute | solution.py:553
  10.8 2.9 %collective-permute-start.5 = (bf16[272,128]{1,0:T(8,128)(2,1)S(1)}, bf16[272,128]{1,0:T(8,128)(2,1)S(1)}, u32[]{:S(2)}, u32[]{:S(2)}) collective-permute-start(bf16[272,128]{1,0:T(8,128)(2,1)S(1)} %collective-permute-done.1.refs_1_), channel_id=1, source_target_pairs={{0,8},{2,10},{4,12},{6,14},{8,0},{10,2},{12,4},{14,6},{1,9},{3,11}... | collective-permute-start | bytes 208904 | tf_op jit(solution)/shard_map/ppermute | solution.py:553
  13.7 0.0 collective-permute-done.6.refs_6_
  13.7 0.5 %collective-permute-start.7 = (bf16[272,128]{1,0:T(8,128)(2,1)S(1)}, bf16[272,128]{1,0:T(8,128)(2,1)S(1)}, u32[]{:S(2)}, u32[]{:S(2)}) collective-permute-start(bf16[272,128]{1,0:T(8,128)(2,1)S(1)} %collective-permute-done.6.refs_6_), channel_id=1, source_target_pairs={{0,1},{1,0},{2,3},{3,2},{4,5},{5,4},{6,7},{7,6},{8,9},{9,8},{10,11... | collective-permute-start | bytes 208904 | tf_op jit(solution)/shard_map/ppermute | solution.py:553
  14.2 1.5 %prepare.1 = (f32[64,128]{1,0:T(8,128)S(1)}, f32[64,128]{1,0:T(8,128)S(1)}, f32[128,128]{1,0:T(8,128)S(1)}, f32[50,16]{1,0:T(8,128)S(1)}, bf16[64,384]{1,0:T(8,1...) custom-call(bf16[272,128]{1,0:T(8,128)(2,1)S(1)} %pack.1.refs_0_, ...), custom_call_target="tpu_custom_call" | custom-call | tf_op jit(solution)/shard_map/prepare/pallas_call | solution.py:160
  15.7 0.0 collective-permute-done.2.refs_2_
  15.7 1.0 %collective-permute-done.4.refs_4_ = bf16[272,128]{1,0:T(8,128)(2,1)S(1)} collective-permute-done((bf16[272,128]{1,0:T(8,128)(2,1)S(1)}, bf16[272,128]{1,0:T(8,128)(2,1)S(1)}, u32[]{:S(2)}, u32[]{:S(2)}) %collective-permute-start.4) | collective-permute-done | bytes 69664 | tf_op jit(solution)/shard_map/ppermute | solution.py:553
  16.7 0.0 collective-permute-done.3.refs_3_
  16.7 1.5 %collective-permute-done.5.refs_5_ = bf16[272,128]{1,0:T(8,128)(2,1)S(1)} collective-permute-done((bf16[272,128]{1,0:T(8,128)(2,1)S(1)}, bf16[272,128]{1,0:T(8,128)(2,1)S(1)}, u32[]{:S(2)}, u32[]{:S(2)}) %collective-permute-start.5) | collective-permute-done | bytes 69664 | tf_op jit(solution)/shard_map/ppermute | solution.py:553
  18.2 0.0 collective-permute-done.7.refs_7_
  18.2 2.6 %edges.1 = (f32[4,8,2,4,8,128]{5,4,3,2,1,0:T(8,128)S(1)}, bf16[4,8,2,32,128]{4,3,2,1,0:T(8,128)(2,1)S(1)}, bf16[4,8,2,32,128]{4,3,2,1,0:T(8,128)(2,1)S(1)}) custom-call(bf16[272,128]{1,0:T(8,128)(2,1)S(1)} %pack.1.refs_0_, bf16[272,128]{1,0:T(8,128)(2,1)S(1)} %collective-permute-done.1.refs_1_, bf16[272,128]{1,0:T(8,128)(2,1)S(1)} %collective-permute-done.2.refs_2_, ...), custom_call_target="tpu_custom_call" | custom-call | tf_op jit(solution)/shard_map/edges/pallas_call | solution.py:160
  20.9 0.1 collective-permute-start.8
  21.0 1.1 %left.1 = (f32[4128,64]{1,0:T(8,128)S(1)}, f32[4128,64]{1,0:T(8,128)S(1)}, f32[4,8,2,4,8,128]{5,4,3,2,1,0:T(8,128)S(1)}) custom-call(bf16[4,8,2,32,128]{4,3,2,1,0:T(8,128)(2,1)S(1)} %get-tuple-element.37.normed_ref, bf16[4,8,2,32,128]{4,3,2,1,0:T(8,128)(2,1)S(1)} %get-tuple-element.38.right_ref, bf16[128,640]{1,0:T(8,128)(2,1)S(1)} %get-tuple-element.36.refs_13_.tri_in_ref, ...), custom_call_target="tpu_custom_call" | custom-call | tf_op jit(solution)/shard_map/left/pallas_call | solution.py:160
  22.0 0.8 %collective-permute-done.8.other_ref = bf16[4,8,2,32,128]{4,3,2,1,0:T(8,128)(2,1)S(1)} collective-permute-done((bf16[4,8,2,32,128]{4,3,2,1,0:T(8,128)(2,1)S(1)}, bf16[4,8,2,32,128]{4,3,2,1,0:T(8,128)(2,1)S(1)}, u32[]{:S(2)}, u32[]{:S(2)}) %collective-permute-start.8) | collective-permute-done | bytes 524320 | tf_op jit(solution)/shard_map/ppermute | solution.py:553
  22.9 3.2 %triangle.1 = (f32[32,128]{1,0:T(8,128)S(1)}, f32[8,4,2,8,128]{4,3,2,1,0:T(8,128)S(1)}) custom-call(f32[4128,64]{1,0:T(8,128)S(1)} %get-tuple-element.39.left_ref, f32[4128,64]{1,0:T(8,128)S(1)} %get-tuple-element.40.mine_ref, bf16[4,8,2,32,128]{4,3,2,1,0:T(8,128)(2,1)S(1)} %collective-permute-done.8.other_ref, ...), custom_call_target="tpu_custom_call" | custom-call | tf_op jit(solution)/shard_map/triangle/pallas_call | solution.py:160
  26.0 0.2 collective-permute-start.9
  26.2 1.0 %scores.1 = (f32[8,32]{1,0:T(8,128)}, f32[1,8]{1,0:T(1,128)}) custom-call(f32[8,4,2,8,128]{4,3,2,1,0:T(8,128)S(1)} %get-tuple-element.44.refs_0_, bf16[64,128]{1,0:T(8,128)(2,1)S(1)} %get-tuple-element.45.refs_1_, s32[1,64]{1,0:T(1,128)S(1)} %get-tuple-element.35.refs_12_.mask_ref.refs_2_, s32[1,64]{1,0:T(1,128)S(1)} %get-tuple-element.46.refs_3_), custom_call_target="tpu_custom_call" | custom-call | tf_op jit(solution)/shard_map/scores/pallas_call | solution.py:160
  27.2 0.1 collective-permute-done.9.other_ref
  27.3 1.2 %atoms.1 = f32[1,16]{1,0:T(1,128)} custom-call(f32[32,128]{1,0:T(8,128)S(1)} %get-tuple-element.49.mine_ref, f32[32,128]{1,0:T(8,128)S(1)} %collective-permute-done.9.other_ref, bf16[64,384]{1,0:T(8,128)(2,1)S(1)} %get-tuple-element.50.single_ref, s32[1,64]{1,0:T(1,128)S(1)} %get-tuple-element.35.refs_12_.mask_ref.refs_2_, ...), custom_call_target="tpu_custom_call" | custom-call | tf_op jit(solution)/shard_map/atoms/pallas_call | solution.py:160
Async XLA Ops:
  0.6 1.6 %collective-permute-start = (f32[3,16]{1,0:T(4,128)}, f32[3,16]{1,0:T(4,128)S(1)}, u32[]{:S(2)}, u32[]{:S(2)}) collective-permute-start(f32[3,16]{1,0:T(4,128)} %coords_ref.1), channel_id=1, source_target_pairs={{0,2},{2,0},{4,6},{6,4},{8,10},{10,8},{12,14},{14,12},{1,3},{3,1},... | collective-permute-start | bytes 584 | tf_op jit(solution)/shard_map/ppermute | solution.py:553
  2.3 7.2 %collective-permute-start.1 = (bf16[272,128]{1,0:T(8,128)(2,1)S(1)}, bf16[272,128]{1,0:T(8,128)(2,1)S(1)}, u32[]{:S(2)}, u32[]{:S(2)}) collective-permute-start(bf16[272,128]{1,0:T(8,128)(2,1)S(1)} %pack.1.refs_0_), channel_id=1, source_target_pairs={{0,1},{1,0},{2,3},{3,2},{4,5},{5,4},{6,7},{7,6},{8,9},{9,8},{10,11... | collective-permute-start | bytes 208904 | tf_op jit(solution)/shard_map/ppermute | solution.py:553
  5.1 8.6 %collective-permute-start.6 = (bf16[272,128]{1,0:T(8,128)(2,1)S(1)}, bf16[272,128]{1,0:T(8,128)(2,1)S(1)}, u32[]{:S(2)}, u32[]{:S(2)}) collective-permute-start(bf16[272,128]{1,0:T(8,128)(2,1)S(1)} %pack.1.refs_0_), channel_id=1, source_target_pairs={{0,12},{2,14},{4,8},{6,10},{8,4},{10,6},{12,0},{14,2},{1,13},{3,15... | collective-permute-start | bytes 208904 | tf_op jit(solution)/shard_map/ppermute | solution.py:553
  8.7 7.0 %collective-permute-start.2 = (bf16[272,128]{1,0:T(8,128)(2,1)S(1)}, bf16[272,128]{1,0:T(8,128)(2,1)S(1)}, u32[]{:S(2)}, u32[]{:S(2)}) collective-permute-start(bf16[272,128]{1,0:T(8,128)(2,1)S(1)} %pack.1.refs_0_), channel_id=1, source_target_pairs={{0,4},{2,6},{4,0},{6,2},{8,12},{10,14},{12,8},{14,10},{1,5},{3,7},... | collective-permute-start | bytes 208904 | tf_op jit(solution)/shard_map/ppermute | solution.py:553
  8.7 8.0 %collective-permute-start.4 = (bf16[272,128]{1,0:T(8,128)(2,1)S(1)}, bf16[272,128]{1,0:T(8,128)(2,1)S(1)}, u32[]{:S(2)}, u32[]{:S(2)}) collective-permute-start(bf16[272,128]{1,0:T(8,128)(2,1)S(1)} %pack.1.refs_0_), channel_id=1, source_target_pairs={{0,8},{2,10},{4,12},{6,14},{8,0},{10,2},{12,4},{14,6},{1,9},{3,11}... | collective-permute-start | bytes 208904 | tf_op jit(solution)/shard_map/ppermute | solution.py:553
  9.5 7.2 %collective-permute-start.3 = (bf16[272,128]{1,0:T(8,128)(2,1)S(1)}, bf16[272,128]{1,0:T(8,128)(2,1)S(1)}, u32[]{:S(2)}, u32[]{:S(2)}) collective-permute-start(bf16[272,128]{1,0:T(8,128)(2,1)S(1)} %collective-permute-done.1.refs_1_), channel_id=1, source_target_pairs={{0,4},{2,6},{4,0},{6,2},{8,12},{10,14},{12,8},{14,10},{1,5},{3,7},... | collective-permute-start | bytes 208904 | tf_op jit(solution)/shard_map/ppermute | solution.py:553
  10.8 7.5 %collective-permute-start.5 = (bf16[272,128]{1,0:T(8,128)(2,1)S(1)}, bf16[272,128]{1,0:T(8,128)(2,1)S(1)}, u32[]{:S(2)}, u32[]{:S(2)}) collective-permute-start(bf16[272,128]{1,0:T(8,128)(2,1)S(1)} %collective-permute-done.1.refs_1_), channel_id=1, source_target_pairs={{0,8},{2,10},{4,12},{6,14},{8,0},{10,2},{12,4},{14,6},{1,9},{3,11}... | collective-permute-start | bytes 208904 | tf_op jit(solution)/shard_map/ppermute | solution.py:553
  13.7 4.5 %collective-permute-start.7 = (bf16[272,128]{1,0:T(8,128)(2,1)S(1)}, bf16[272,128]{1,0:T(8,128)(2,1)S(1)}, u32[]{:S(2)}, u32[]{:S(2)}) collective-permute-start(bf16[272,128]{1,0:T(8,128)(2,1)S(1)} %collective-permute-done.6.refs_6_), channel_id=1, source_target_pairs={{0,1},{1,0},{2,3},{3,2},{4,5},{5,4},{6,7},{7,6},{8,9},{9,8},{10,11... | collective-permute-start | bytes 208904 | tf_op jit(solution)/shard_map/ppermute | solution.py:553
  20.9 2.0 %collective-permute-start.8 = (bf16[4,8,2,32,128]{4,3,2,1,0:T(8,128)(2,1)S(1)}, bf16[4,8,2,32,128]{4,3,2,1,0:T(8,128)(2,1)S(1)}, u32[]{:S(2)}, u32[]{:S(2)}) collective-permute-start(bf16[4,8,2,32,128]{4,3,2,1,0:T(8,128)(2,1)S(1)} %get-tuple-element.38.right_ref), channel_id=1, source_target_pairs={{0,2},{2,0},{4,6},{6,4},{8,10},{10,8},{12,14},{14,12},{1,3},{3,1},... | collective-permute-start | bytes 1572872 | tf_op jit(solution)/shard_map/ppermute | solution.py:553
  26.0 1.2 %collective-permute-start.9 = (f32[32,128]{1,0:T(8,128)S(1)}, f32[32,128]{1,0:T(8,128)S(1)}, u32[]{:S(2)}, u32[]{:S(2)}) collective-permute-start(f32[32,128]{1,0:T(8,128)S(1)} %get-tuple-element.49.mine_ref), channel_id=1, source_target_pairs={{0,2},{2,0},{4,6},{6,4},{8,10},{10,8},{12,14},{14,12},{1,3},{3,1},... | collective-permute-start | bytes 49160 | tf_op jit(solution)/shard_map/ppermute | solution.py:553

commit v5 on v4

--- a/solution.py
+++ b/solution.py
@@ -236,17 +236,29 @@
     )
 
 
-def prepare_kernel(copied, *refs):
+def prepare_kernel(slots, col_count, atoms, copied, *refs):
     raw = refs[1:6]
     sources = refs[6 : 6 + copied]
-    rows_ref, cols_ref, dist_ref, atom_part_ref = refs[6 + copied : 10 + copied]
-    targets = refs[10 + copied : 10 + 2 * copied]
+    rows_ref, cols_ref, dist_ref, atom_part_ref, chosen_ref, turned_ref = refs[
+        6 + copied : 12 + copied
+    ]
+    targets = refs[12 + copied : 12 + 2 * copied]
     w_left_ref, w_right_ref, w_dist_ref, atom_single_ref, atom_w_ref, arrived = refs[
-        10 + 2 * copied :
+        12 + 2 * copied :
     ]
     landing = (w_left_ref, w_right_ref, w_dist_ref, atom_single_ref, atom_w_ref)
     bring((*raw, *sources), (*landing, *targets), arrived)
-    single = targets[0][...]
+    single, rep = targets[0][...], targets[-1][...]
+    chip, _, col = place_of()
+    order = lax.broadcasted_iota(jnp.int32, chosen_ref.shape[1:], 0)
+    for place, (chip_step, col_step) in enumerate(slots):
+        device = 2 * (chip ^ chip_step) * col_count + (col ^ col_step)
+        number = jnp.where(
+            order < atoms, order + device * atoms, order - atoms + (device + col_count) * atoms
+        )
+        chosen = (number == rep).astype(jnp.float32)
+        chosen_ref[place] = chosen.astype(jnp.bfloat16)
+        turned_ref[place] = chosen.T.astype(jnp.bfloat16)
     rows_ref[...] = jnp.dot(single, w_left_ref[...], preferred_element_type=jnp.float32)
     cols_ref[...] = jnp.dot(single, w_right_ref[...], preferred_element_type=jnp.float32)
     dist_ref[...] = jnp.zeros_like(dist_ref)
@@ -259,30 +271,27 @@
     )
 
 
-def edge_kernel(slots, col_count, atoms, basis_count, *refs):
+def edge_kernel(slots, basis_count, *refs):
     packs = refs[: len(slots)]
-    rows_ref, cols_ref, dist_ref, rep_ref, mask_ref, tri_in_ref = refs[len(slots) : len(slots) + 6]
-    pair_ref, normed_ref, right_ref, distance_ref = refs[len(slots) + 6 :]
+    rows_ref, cols_ref, dist_ref, chosen_ref, turned_ref, mask_ref, tri_in_ref = refs[
+        len(slots) : len(slots) + 7
+    ]
+    pair_ref, normed_ref, right_ref, distance_ref = refs[len(slots) + 7 :]
     _, tile_rows, _, tile_cols, width = normed_ref.shape
     tokens = rows_ref.shape[0]
     pairs = tile_rows * tile_cols
     chip, half, col = place_of()
     w_dist = dist_ref[...].astype(jnp.bfloat16)
-    rep = rep_ref[...]
-    order = lax.broadcasted_iota(jnp.int32, (width, tokens), 0)
+    across = jnp.zeros((16, tokens), jnp.float32)
     picked = jnp.zeros((tokens, 16), jnp.float32)
-    across = jnp.zeros((16, tokens), jnp.float32)
-    for pack, (chip_step, col_step) in zip(packs, slots):
-        device = 2 * (chip ^ chip_step) * col_count + (col ^ col_step)
-        number = jnp.where(
-            order < atoms, order + device * atoms, order - atoms + (device + col_count) * atoms
-        )
-        chosen = (number == rep).astype(jnp.float32).astype(jnp.bfloat16)
+    for place, pack in enumerate(packs):
         pieces = pack[pairs:, :]
+        across = across + jnp.dot(
+            pieces, chosen_ref[place], preferred_element_type=jnp.float32
+        )
         picked = picked + lax.dot_general(
-            chosen, pieces, (((0,), (1,)), ((), ())), preferred_element_type=jnp.float32
-        )
-        across = across + jnp.dot(pieces, chosen, preferred_element_type=jnp.float32)
+            turned_ref[place], pieces, (((1,), (1,)), ((), ())), preferred_element_type=jnp.float32
+        )
     square = jnp.zeros((tokens, width), jnp.float32)
     for axis in range(3):
         down = picked[:, axis : axis + 1] + picked[:, axis + 3 : axis + 4]
@@ -363,6 +372,12 @@
             turned_ref[rows, :] = left_ref[i].T
             key = right_ref[at_chip, i].reshape(tokens, width).astype(jnp.float32)
             keys_ref[rows, :] = key.T
+
+
+def normed_columns(values):
+    center = values - jnp.mean(values, axis=0, keepdims=True)
+    spread = jnp.mean(center * center, axis=0, keepdims=True)
+    return (center * lax.rsqrt(spread + EPSILON)).astype(jnp.bfloat16)
 
 
 def triangle_kernel(
@@ -405,15 +420,18 @@
     real = jnp.where(token < token_count(mask_ref).astype(jnp.int32), 1.0, 0.0)
     tri_out = tri_out_ref[...]
     for at_chip in range(chips):
-        outer = jnp.concatenate(
-            [
-                outer_ref[pl.ds((at_chip * tile_rows + i) * step, width), :].T
-                for i in range(tile_rows)
-            ],
-            axis=0,
-        )
         change = jnp.dot(
-            layer_norm(outer).astype(jnp.bfloat16), tri_out, preferred_element_type=jnp.float32
+            jnp.concatenate(
+                [
+                    normed_columns(
+                        outer_ref[pl.ds((at_chip * tile_rows + i) * step, width), :]
+                    ).T
+                    for i in range(tile_rows)
+                ],
+                axis=0,
+            ),
+            tri_out,
+            preferred_element_type=jnp.float32,
         )
         for i in range(tile_rows):
             gating = gating_ref[at_chip, i].reshape(tokens, width)
@@ -574,24 +592,27 @@
     def pack_of(i, j):
         if i == 0 or j == 0:
             return beside[j] if i == 0 else along[i]
-        if i < chips - 1:
-            return across(beside[j], "row", row_count, 2 * i)
+        if i == 1:
+            step = 2 * i * col_count + j
+            return across(packed, ("row", "col"), row_count * col_count, step)
         return across(along[i], "col", col_count, j)
 
     packs = [pack_of(i, j) for i, j in slots]
     raw = (w_left, w_right, w_dist, atom_single, atom_w.T)
     kept = (
-        single, tri_in, tri_out, pae_w.T, pool_w, plddt_w.T, rep_atom.reshape(1, tokens),
-        token_mask.reshape(1, tokens), chain_id.reshape(1, tokens), atom_token.reshape(1, atoms),
-    )
-    rows, cols, dist, atom_part, *kept = run(
-        lambda *refs: prepare_kernel(len(kept), *refs),
+        single, tri_in, tri_out, pae_w.T, pool_w, plddt_w.T, token_mask.reshape(1, tokens),
+        chain_id.reshape(1, tokens), atom_token.reshape(1, atoms), rep_atom.reshape(1, tokens),
+    )
+    rows, cols, dist, atom_part, chosen, turned, *kept = run(
+        lambda *refs: prepare_kernel(slots, col_count, atoms, len(kept), *refs),
         "prepare",
         (
             pltpu.VMEM((tokens, width), float32),
             pltpu.VMEM((tokens, width), float32),
             pltpu.VMEM((width, width), float32),
             pltpu.VMEM((plddt_w.shape[1], atoms), float32),
+            pltpu.VMEM((len(slots), width, tokens), bfloat16),
+            pltpu.VMEM((len(slots), tokens, width), bfloat16),
             *[pltpu.VMEM(value.shape, value.dtype) for value in kept],
         ),
         (packed, *raw, *kept),
@@ -601,14 +622,14 @@
             pltpu.SemaphoreType.DMA((len(raw) + len(kept),)),
         ),
     )
-    single, tri_in, tri_out, pae_w, pool_w, plddt_w, rep, mask, chain, atom_token = kept
+    single, tri_in, tri_out, pae_w, pool_w, plddt_w, mask, chain, atom_token, _ = kept
     full = (chips, tile_rows, col_count, tile_cols, width)
     by_half = pltpu.VMEM((chips, tile_rows, 2, chips, tile_rows, width), float32)
     pair, normed, right = run(
-        lambda *refs: edge_kernel(slots, col_count, atoms, w_dist.shape[0], *refs),
+        lambda *refs: edge_kernel(slots, w_dist.shape[0], *refs),
         "edges",
         (by_half, pltpu.VMEM(full, bfloat16), pltpu.VMEM(full, bfloat16)),
-        (*packs, rows, cols, dist, rep, mask, tri_in),
+        (*packs, rows, cols, dist, chosen, turned, mask, tri_in),
         scratch=(pltpu.VMEM((chips, tokens, width), float32),),
     )
     turned = pltpu.VMEM((chips * tile_rows * (width + SPREAD), tokens), float32)

time: 28.7 us -> 27.1 us (0.944)
  waiting for transfers between devices: 3.57 us -> 2.49 us
  Pallas kernels: 11.5 us -> 11 us
    ppermute x10, waiting for transfers between devices: 3.57 us -> 2.49 us  [across(): return lax.ppermute(values, axis, [(i, i ^ step) for i in range(count)])]
    pallas_call x8, Pallas kernels: 11.5 us -> 11 us  [run(): pl.pallas_call(kernel, out_shape=out_shapes, in_specs=[VMEM] * held + [HB...]
  transfers between devices with their start and end apart: 10 -> 10, of which waited for: 5 -> 4; matrix products, arithmetic and copies ran while one was open for 0% -> 0% of each run, Pallas kernels for 15% -> 18%
where the time goes in v5:
time: 27.1 us; the launch traced here: 26.9 us
  starting transfers between devices  12.8 us (47%)
  Pallas kernels  11 us (41%)
  waiting for transfers between devices  2.49 us (9%)
  between operations  0.7 us (3%)
    ppermute x10, starting transfers between devices, across(): return lax.ppermute(values, axis, [(i, i ^ step) for i in range(count)])  12.8 us
    pallas_call x8, Pallas kernels, run(): pl.pallas_call(kernel, out_shape=out_shapes, in_specs=[VMEM] * held + [HB...  11 us
    ppermute x10, waiting for transfers between devices, across(): return lax.ppermute(values, axis, [(i, i ^ step) for i in range(count)])  2.49 us
  transfers between devices with their start and end apart: 10, of which 4 were waited for; matrix products, arithmetic and copies ran while one was open for 0% of the time, Pallas kernels for 18%

profile of v5, /device:TPU:0, one launch (start us, length us, event | category | flops | bytes accessed | tf_op | source)
XLA Modules:
  0.0 26.9 jit_solution(4921823604982076866)
XLA Ops:
  0.6 0.6 %collective-permute-start = (f32[3,16]{1,0:T(4,128)}, f32[3,16]{1,0:T(4,128)S(1)}, u32[]{:S(2)}, u32[]{:S(2)}) collective-permute-start(f32[3,16]{1,0:T(4,128)} %coords_ref.1), channel_id=1, source_target_pairs={{0,2},{2,0},{4,6},{6,4},{8,10},{10,8},{12,14},{14,12},{1,3},{3,1},... | collective-permute-start | bytes 584 | tf_op jit(solution)/shard_map/ppermute | solution.py:571
  1.2 0.9 %fetch.1 = (bf16[272,128]{1,0:T(8,128)(2,1)S(1)}, f32[3,16]{1,0:T(4,128)S(1)}) custom-call(bf16[256,128]{1,0:T(8,128)(2,1)} %bitcast.10, f32[3,16]{1,0:T(4,128)} %coords_ref.1), custom_call_target="tpu_custom_call" | custom-call | tf_op jit(solution)/shard_map/fetch/pallas_call | solution.py:160
  2.1 0.2 collective-permute-done.other_ref
  2.2 0.1 pack.1.refs_0_
  2.3 3.9 %collective-permute-start.4 = (bf16[272,128]{1,0:T(8,128)(2,1)S(1)}, bf16[272,128]{1,0:T(8,128)(2,1)S(1)}, u32[]{:S(2)}, u32[]{:S(2)}) collective-permute-start(bf16[272,128]{1,0:T(8,128)(2,1)S(1)} %pack.1.refs_0_), channel_id=1, source_target_pairs={{0,8},{2,10},{4,12},{6,14},{8,0},{10,2},{12,4},{14,6},{1,9},{3,11}... | collective-permute-start | bytes 208904 | tf_op jit(solution)/shard_map/ppermute | solution.py:571
  6.2 1.3 %collective-permute-start.6 = (bf16[272,128]{1,0:T(8,128)(2,1)S(1)}, bf16[272,128]{1,0:T(8,128)(2,1)S(1)}, u32[]{:S(2)}, u32[]{:S(2)}) collective-permute-start(bf16[272,128]{1,0:T(8,128)(2,1)S(1)} %pack.1.refs_0_), channel_id=1, source_target_pairs={{0,12},{2,14},{4,8},{6,10},{8,4},{10,6},{12,0},{14,2},{1,13},{3,15... | collective-permute-start | bytes 208904 | tf_op jit(solution)/shard_map/ppermute | solution.py:571
  7.6 1.5 %collective-permute-start.1 = (bf16[272,128]{1,0:T(8,128)(2,1)S(1)}, bf16[272,128]{1,0:T(8,128)(2,1)S(1)}, u32[]{:S(2)}, u32[]{:S(2)}) collective-permute-start(bf16[272,128]{1,0:T(8,128)(2,1)S(1)} %pack.1.refs_0_), channel_id=1, source_target_pairs={{0,1},{1,0},{2,3},{3,2},{4,5},{5,4},{6,7},{7,6},{8,9},{9,8},{10,11... | collective-permute-start | bytes 208904 | tf_op jit(solution)/shard_map/ppermute | solution.py:571
  9.1 0.2 collective-permute-start.2
  9.3 1.8 %collective-permute-start.3 = (bf16[272,128]{1,0:T(8,128)(2,1)S(1)}, bf16[272,128]{1,0:T(8,128)(2,1)S(1)}, u32[]{:S(2)}, u32[]{:S(2)}) collective-permute-start(bf16[272,128]{1,0:T(8,128)(2,1)S(1)} %pack.1.refs_0_), channel_id=1, source_target_pairs={{0,5},{1,4},{2,7},{3,6},{4,1},{5,0},{6,3},{7,2},{8,13},{9,12},{10,... | collective-permute-start | bytes 208904 | tf_op jit(solution)/shard_map/ppermute | solution.py:571
  11.1 0.0 collective-permute-done.4.refs_4_
  11.1 1.9 %collective-permute-start.5 = (bf16[272,128]{1,0:T(8,128)(2,1)S(1)}, bf16[272,128]{1,0:T(8,128)(2,1)S(1)}, u32[]{:S(2)}, u32[]{:S(2)}) collective-permute-start(bf16[272,128]{1,0:T(8,128)(2,1)S(1)} %collective-permute-done.4.refs_4_), channel_id=1, source_target_pairs={{0,1},{1,0},{2,3},{3,2},{4,5},{5,4},{6,7},{7,6},{8,9},{9,8},{10,11... | collective-permute-start | bytes 208904 | tf_op jit(solution)/shard_map/ppermute | solution.py:571
  13.0 0.0 collective-permute-done.6.refs_6_
  13.0 1.2 %collective-permute-start.7 = (bf16[272,128]{1,0:T(8,128)(2,1)S(1)}, bf16[272,128]{1,0:T(8,128)(2,1)S(1)}, u32[]{:S(2)}, u32[]{:S(2)}) collective-permute-start(bf16[272,128]{1,0:T(8,128)(2,1)S(1)} %collective-permute-done.6.refs_6_), channel_id=1, source_target_pairs={{0,1},{1,0},{2,3},{3,2},{4,5},{5,4},{6,7},{7,6},{8,9},{9,8},{10,11... | collective-permute-start | bytes 208904 | tf_op jit(solution)/shard_map/ppermute | solution.py:571
  14.2 1.8 %prepare.1 = (f32[64,128]{1,0:T(8,128)S(1)}, f32[64,128]{1,0:T(8,128)S(1)}, f32[128,128]{1,0:T(8,128)S(1)}, f32[50,16]{1,0:T(8,128)S(1)}, bf16[8,128,64]{2,1,0:T...) custom-call(bf16[272,128]{1,0:T(8,128)(2,1)S(1)} %pack.1.refs_0_, ...), custom_call_target="tpu_custom_call" | custom-call | tf_op jit(solution)/shard_map/prepare/pallas_call | solution.py:160
  16.1 0.0 collective-permute-done.1.refs_1_
  16.1 0.0 collective-permute-done.2.refs_2_
  16.1 0.0 collective-permute-done.3.refs_3_
  16.1 0.7 %collective-permute-done.5.refs_5_ = bf16[272,128]{1,0:T(8,128)(2,1)S(1)} collective-permute-done((bf16[272,128]{1,0:T(8,128)(2,1)S(1)}, bf16[272,128]{1,0:T(8,128)(2,1)S(1)}, u32[]{:S(2)}, u32[]{:S(2)}) %collective-permute-start.5) | collective-permute-done | bytes 69664 | tf_op jit(solution)/shard_map/ppermute | solution.py:571
  16.8 0.7 %collective-permute-done.7.refs_7_ = bf16[272,128]{1,0:T(8,128)(2,1)S(1)} collective-permute-done((bf16[272,128]{1,0:T(8,128)(2,1)S(1)}, bf16[272,128]{1,0:T(8,128)(2,1)S(1)}, u32[]{:S(2)}, u32[]{:S(2)}) %collective-permute-start.7) | collective-permute-done | bytes 69664 | tf_op jit(solution)/shard_map/ppermute | solution.py:571
  17.5 2.6 %edges.1 = (f32[4,8,2,4,8,128]{5,4,3,2,1,0:T(8,128)S(1)}, bf16[4,8,2,32,128]{4,3,2,1,0:T(8,128)(2,1)S(1)}, bf16[4,8,2,32,128]{4,3,2,1,0:T(8,128)(2,1)S(1)}) custom-call(bf16[272,128]{1,0:T(8,128)(2,1)S(1)} %pack.1.refs_0_, bf16[272,128]{1,0:T(8,128)(2,1)S(1)} %collective-permute-done.1.refs_1_, bf16[272,128]{1,0:T(8,128)(2,1)S(1)} %collective-permute-done.2.refs_2_, ...), custom_call_target="tpu_custom_call" | custom-call | tf_op jit(solution)/shard_map/edges/pallas_call | solution.py:160
  20.1 0.1 collective-permute-start.8
  20.2 1.1 %left.1 = (f32[4128,64]{1,0:T(8,128)S(1)}, f32[4128,64]{1,0:T(8,128)S(1)}, f32[4,8,2,4,8,128]{5,4,3,2,1,0:T(8,128)S(1)}) custom-call(bf16[4,8,2,32,128]{4,3,2,1,0:T(8,128)(2,1)S(1)} %get-tuple-element.39.normed_ref, bf16[4,8,2,32,128]{4,3,2,1,0:T(8,128)(2,1)S(1)} %get-tuple-element.40.right_ref, bf16[128,640]{1,0:T(8,128)(2,1)S(1)} %get-tuple-element.38.refs_14_.tri_in_ref, ...), custom_call_target="tpu_custom_call" | custom-call | tf_op jit(solution)/shard_map/left/pallas_call | solution.py:160
  21.2 0.8 %collective-permute-done.8.other_ref = bf16[4,8,2,32,128]{4,3,2,1,0:T(8,128)(2,1)S(1)} collective-permute-done((bf16[4,8,2,32,128]{4,3,2,1,0:T(8,128)(2,1)S(1)}, bf16[4,8,2,32,128]{4,3,2,1,0:T(8,128)(2,1)S(1)}, u32[]{:S(2)}, u32[]{:S(2)}) %collective-permute-start.8) | collective-permute-done | bytes 524320 | tf_op jit(solution)/shard_map/ppermute | solution.py:571
  22.1 2.4 %triangle.1 = (f32[32,128]{1,0:T(8,128)S(1)}, f32[8,4,2,8,128]{4,3,2,1,0:T(8,128)S(1)}) custom-call(f32[4128,64]{1,0:T(8,128)S(1)} %get-tuple-element.41.left_ref, f32[4128,64]{1,0:T(8,128)S(1)} %get-tuple-element.42.mine_ref, bf16[4,8,2,32,128]{4,3,2,1,0:T(8,128)(2,1)S(1)} %collective-permute-done.8.other_ref, ...), custom_call_target="tpu_custom_call" | custom-call | tf_op jit(solution)/shard_map/triangle/pallas_call | solution.py:160
  24.5 0.2 collective-permute-start.9
  24.7 1.0 %scores.1 = (f32[8,32]{1,0:T(8,128)}, f32[1,8]{1,0:T(1,128)}) custom-call(f32[8,4,2,8,128]{4,3,2,1,0:T(8,128)S(1)} %get-tuple-element.46.refs_0_, bf16[64,128]{1,0:T(8,128)(2,1)S(1)} %get-tuple-element.47.refs_1_, s32[1,64]{1,0:T(1,128)S(1)} %get-tuple-element.37.refs_13_.mask_ref.refs_2_, s32[1,64]{1,0:T(1,128)S(1)} %get-tuple-element.48.refs_3_), custom_call_target="tpu_custom_call" | custom-call | tf_op jit(solution)/shard_map/scores/pallas_call | solution.py:160
  25.7 0.1 collective-permute-done.9.other_ref
  25.7 1.2 %atoms.1 = f32[1,16]{1,0:T(1,128)} custom-call(f32[32,128]{1,0:T(8,128)S(1)} %get-tuple-element.51.mine_ref, f32[32,128]{1,0:T(8,128)S(1)} %collective-permute-done.9.other_ref, bf16[64,384]{1,0:T(8,128)(2,1)S(1)} %get-tuple-element.52.single_ref, s32[1,64]{1,0:T(1,128)S(1)} %get-tuple-element.37.refs_13_.mask_ref.refs_2_, ...), custom_call_target="tpu_custom_call" | custom-call | tf_op jit(solution)/shard_map/atoms/pallas_call | solution.py:160
Async XLA Ops:
  0.6 1.6 %collective-permute-start = (f32[3,16]{1,0:T(4,128)}, f32[3,16]{1,0:T(4,128)S(1)}, u32[]{:S(2)}, u32[]{:S(2)}) collective-permute-start(f32[3,16]{1,0:T(4,128)} %coords_ref.1), channel_id=1, source_target_pairs={{0,2},{2,0},{4,6},{6,4},{8,10},{10,8},{12,14},{14,12},{1,3},{3,1},... | collective-permute-start | bytes 584 | tf_op jit(solution)/shard_map/ppermute | solution.py:571
  2.3 8.8 %collective-permute-start.4 = (bf16[272,128]{1,0:T(8,128)(2,1)S(1)}, bf16[272,128]{1,0:T(8,128)(2,1)S(1)}, u32[]{:S(2)}, u32[]{:S(2)}) collective-permute-start(bf16[272,128]{1,0:T(8,128)(2,1)S(1)} %pack.1.refs_0_), channel_id=1, source_target_pairs={{0,8},{2,10},{4,12},{6,14},{8,0},{10,2},{12,4},{14,6},{1,9},{3,11}... | collective-permute-start | bytes 208904 | tf_op jit(solution)/shard_map/ppermute | solution.py:571
  6.2 6.8 %collective-permute-start.6 = (bf16[272,128]{1,0:T(8,128)(2,1)S(1)}, bf16[272,128]{1,0:T(8,128)(2,1)S(1)}, u32[]{:S(2)}, u32[]{:S(2)}) collective-permute-start(bf16[272,128]{1,0:T(8,128)(2,1)S(1)} %pack.1.refs_0_), channel_id=1, source_target_pairs={{0,12},{2,14},{4,8},{6,10},{8,4},{10,6},{12,0},{14,2},{1,13},{3,15... | collective-permute-start | bytes 208904 | tf_op jit(solution)/shard_map/ppermute | solution.py:571
  7.6 8.5 %collective-permute-start.1 = (bf16[272,128]{1,0:T(8,128)(2,1)S(1)}, bf16[272,128]{1,0:T(8,128)(2,1)S(1)}, u32[]{:S(2)}, u32[]{:S(2)}) collective-permute-start(bf16[272,128]{1,0:T(8,128)(2,1)S(1)} %pack.1.refs_0_), channel_id=1, source_target_pairs={{0,1},{1,0},{2,3},{3,2},{4,5},{5,4},{6,7},{7,6},{8,9},{9,8},{10,11... | collective-permute-start | bytes 208904 | tf_op jit(solution)/shard_map/ppermute | solution.py:571
  9.1 7.0 %collective-permute-start.2 = (bf16[272,128]{1,0:T(8,128)(2,1)S(1)}, bf16[272,128]{1,0:T(8,128)(2,1)S(1)}, u32[]{:S(2)}, u32[]{:S(2)}) collective-permute-start(bf16[272,128]{1,0:T(8,128)(2,1)S(1)} %pack.1.refs_0_), channel_id=1, source_target_pairs={{0,4},{2,6},{4,0},{6,2},{8,12},{10,14},{12,8},{14,10},{1,5},{3,7},... | collective-permute-start | bytes 208904 | tf_op jit(solution)/shard_map/ppermute | solution.py:571
  9.3 6.8 %collective-permute-start.3 = (bf16[272,128]{1,0:T(8,128)(2,1)S(1)}, bf16[272,128]{1,0:T(8,128)(2,1)S(1)}, u32[]{:S(2)}, u32[]{:S(2)}) collective-permute-start(bf16[272,128]{1,0:T(8,128)(2,1)S(1)} %pack.1.refs_0_), channel_id=1, source_target_pairs={{0,5},{1,4},{2,7},{3,6},{4,1},{5,0},{6,3},{7,2},{8,13},{9,12},{10,... | collective-permute-start | bytes 208904 | tf_op jit(solution)/shard_map/ppermute | solution.py:571
  11.1 5.7 %collective-permute-start.5 = (bf16[272,128]{1,0:T(8,128)(2,1)S(1)}, bf16[272,128]{1,0:T(8,128)(2,1)S(1)}, u32[]{:S(2)}, u32[]{:S(2)}) collective-permute-start(bf16[272,128]{1,0:T(8,128)(2,1)S(1)} %collective-permute-done.4.refs_4_), channel_id=1, source_target_pairs={{0,1},{1,0},{2,3},{3,2},{4,5},{5,4},{6,7},{7,6},{8,9},{9,8},{10,11... | collective-permute-start | bytes 208904 | tf_op jit(solution)/shard_map/ppermute | solution.py:571
  13.0 4.5 %collective-permute-start.7 = (bf16[272,128]{1,0:T(8,128)(2,1)S(1)}, bf16[272,128]{1,0:T(8,128)(2,1)S(1)}, u32[]{:S(2)}, u32[]{:S(2)}) collective-permute-start(bf16[272,128]{1,0:T(8,128)(2,1)S(1)} %collective-permute-done.6.refs_6_), channel_id=1, source_target_pairs={{0,1},{1,0},{2,3},{3,2},{4,5},{5,4},{6,7},{7,6},{8,9},{9,8},{10,11... | collective-permute-start | bytes 208904 | tf_op jit(solution)/shard_map/ppermute | solution.py:571
  20.1 2.0 %collective-permute-start.8 = (bf16[4,8,2,32,128]{4,3,2,1,0:T(8,128)(2,1)S(1)}, bf16[4,8,2,32,128]{4,3,2,1,0:T(8,128)(2,1)S(1)}, u32[]{:S(2)}, u32[]{:S(2)}) collective-permute-start(bf16[4,8,2,32,128]{4,3,2,1,0:T(8,128)(2,1)S(1)} %get-tuple-element.40.right_ref), channel_id=1, source_target_pairs={{0,2},{2,0},{4,6},{6,4},{8,10},{10,8},{12,14},{14,12},{1,3},{3,1},... | collective-permute-start | bytes 1572872 | tf_op jit(solution)/shard_map/ppermute | solution.py:571
  24.5 1.2 %collective-permute-start.9 = (f32[32,128]{1,0:T(8,128)S(1)}, f32[32,128]{1,0:T(8,128)S(1)}, u32[]{:S(2)}, u32[]{:S(2)}) collective-permute-start(f32[32,128]{1,0:T(8,128)S(1)} %get-tuple-element.51.mine_ref), channel_id=1, source_target_pairs={{0,2},{2,0},{4,6},{6,4},{8,10},{10,8},{12,14},{14,12},{1,3},{3,1},... | collective-permute-start | bytes 49160 | tf_op jit(solution)/shard_map/ppermute | solution.py:571

commit v6 on v5

--- a/solution.py
+++ b/solution.py
@@ -344,8 +344,17 @@
         right_ref[at_chip, :, at_col] = right.astype(jnp.bfloat16)
 
 
+def over_keys(query, key):
+    return lax.dot_general(
+        query.astype(jnp.bfloat16),
+        key.astype(jnp.bfloat16),
+        (((1,), (1,)), ((), ())),
+        preferred_element_type=jnp.float32,
+    )
+
+
 def left_kernel(
-    normed_ref, right_ref, tri_in_ref, mask_ref, turned_ref, keys_ref, gating_ref, left_ref
+    normed_ref, right_ref, tri_in_ref, mask_ref, turned_ref, keys_ref, mine_ref, gating_ref, left_ref
 ):
     chips, tile_rows, col_count, tile_cols, width = normed_ref.shape
     tokens = col_count * tile_cols
@@ -372,6 +381,9 @@
             turned_ref[rows, :] = left_ref[i].T
             key = right_ref[at_chip, i].reshape(tokens, width).astype(jnp.float32)
             keys_ref[rows, :] = key.T
+    for channel in range(width // 2):
+        rows = pl.ds(channel, chips * tile_rows, stride=step)
+        mine_ref[rows, :] = over_keys(turned_ref[rows, :], keys_ref[rows, :])
 
 
 def normed_columns(values):
@@ -382,6 +394,7 @@
 
 def triangle_kernel(
     left_ref,
+    mine_keys_ref,
     mine_ref,
     other_ref,
     pair_ref,
@@ -405,14 +418,12 @@
             keys_ref[pl.ds((at_chip * tile_rows + i) * step, width), :] = key.T
     for channel in range(width):
         rows = pl.ds(channel, queries, stride=step)
-        query = left_ref[rows, :].astype(jnp.bfloat16)
-        key = jnp.concatenate([mine_ref[rows, :], keys_ref[rows, :]], axis=0)
-        outer_ref[rows, :] = lax.dot_general(
-            query,
-            key.astype(jnp.bfloat16),
-            (((1,), (1,)), ((), ())),
-            preferred_element_type=jnp.float32,
-        )
+        query, other = left_ref[rows, :], keys_ref[rows, :]
+        if channel < width // 2:
+            outer = jnp.concatenate([mine_ref[rows, :], over_keys(query, other)], axis=1)
+        else:
+            outer = over_keys(query, jnp.concatenate([mine_keys_ref[rows, :], other], axis=0))
+        outer_ref[rows, :] = outer
     place = lax.broadcasted_iota(jnp.int32, (tokens, width), 0)
     key_half = jnp.where(place < queries, half, 1 - half)
     place = jnp.where(place < queries, place, place - queries)
@@ -633,10 +644,11 @@
         scratch=(pltpu.VMEM((chips, tokens, width), float32),),
     )
     turned = pltpu.VMEM((chips * tile_rows * (width + SPREAD), tokens), float32)
-    left, keys, gating = run(
+    mine = pltpu.VMEM((chips * tile_rows * (width + SPREAD), chips * tile_rows), float32)
+    left, keys, mine, gating = run(
         left_kernel,
         "left",
-        (turned, turned, by_half),
+        (turned, turned, mine, by_half),
         (normed, right, tri_in, mask),
         scratch=(pltpu.VMEM((tile_rows, tokens, width), float32),),
     )
@@ -647,7 +659,7 @@
             pltpu.VMEM((chips * tile_rows, width), float32),
             pltpu.VMEM((tile_rows, chips, 2, tile_rows, width), float32),
         ),
-        (left, keys, partner(right), pair, gating, tri_out, mask),
+        (left, keys, mine, partner(right), pair, gating, tri_out, mask),
         scratch=(turned, turned, by_half),
     )
     tm_scale = 1.24 * (max(tokens, 19) - 15) ** (1.0 / 3.0) - 1.8

time: 27.1 us -> 26.9 us (level)
  waiting for transfers between devices: 2.49 us -> 2.12 us
    ppermute x10, waiting for transfers between devices: 2.49 us -> 2.12 us  [across(): return lax.ppermute(values, axis, [(i, i ^ step) for i in range(count)])]
  transfers between devices with their start and end apart: 10 -> 10, of which waited for: 4 -> 5; matrix products, arithmetic and copies ran while one was open for 0% -> 0% of each run, Pallas kernels for 18% -> 19%
where the time goes in v6:
time: 26.9 us; the launch traced here: 26.7 us
  starting transfers between devices  12.8 us (48%)
  Pallas kernels  11.1 us (41%)
  waiting for transfers between devices  2.12 us (8%)
  between operations  0.7 us (3%)
    ppermute x10, starting transfers between devices, across(): return lax.ppermute(values, axis, [(i, i ^ step) for i in range(count)])  12.8 us
    pallas_call x8, Pallas kernels, run(): pl.pallas_call(kernel, out_shape=out_shapes, in_specs=[VMEM] * held + [HB...  11.1 us
    ppermute x10, waiting for transfers between devices, across(): return lax.ppermute(values, axis, [(i, i ^ step) for i in range(count)])  2.12 us
  transfers between devices with their start and end apart: 10, of which 5 were waited for; matrix products, arithmetic and copies ran while one was open for 0% of the time, Pallas kernels for 19%

profile of v6, /device:TPU:0, one launch (start us, length us, event | category | flops | bytes accessed | tf_op | source)
XLA Modules:
  0.0 26.7 jit_solution(15562070755909460424)
XLA Ops:
  0.6 0.6 %collective-permute-start = (f32[3,16]{1,0:T(4,128)}, f32[3,16]{1,0:T(4,128)S(1)}, u32[]{:S(2)}, u32[]{:S(2)}) collective-permute-start(f32[3,16]{1,0:T(4,128)} %coords_ref.1), channel_id=1, source_target_pairs={{0,2},{2,0},{4,6},{6,4},{8,10},{10,8},{12,14},{14,12},{1,3},{3,1},... | collective-permute-start | bytes 584 | tf_op jit(solution)/shard_map/ppermute | solution.py:582
  1.2 0.9 %fetch.1 = (bf16[272,128]{1,0:T(8,128)(2,1)S(1)}, f32[3,16]{1,0:T(4,128)S(1)}) custom-call(bf16[256,128]{1,0:T(8,128)(2,1)} %bitcast.10, f32[3,16]{1,0:T(4,128)} %coords_ref.1), custom_call_target="tpu_custom_call" | custom-call | tf_op jit(solution)/shard_map/fetch/pallas_call | solution.py:160
  2.1 0.2 collective-permute-done.other_ref
  2.2 0.1 pack.1.refs_0_
  2.3 3.9 %collective-permute-start.4 = (bf16[272,128]{1,0:T(8,128)(2,1)S(1)}, bf16[272,128]{1,0:T(8,128)(2,1)S(1)}, u32[]{:S(2)}, u32[]{:S(2)}) collective-permute-start(bf16[272,128]{1,0:T(8,128)(2,1)S(1)} %pack.1.refs_0_), channel_id=1, source_target_pairs={{0,8},{2,10},{4,12},{6,14},{8,0},{10,2},{12,4},{14,6},{1,9},{3,11}... | collective-permute-start | bytes 208904 | tf_op jit(solution)/shard_map/ppermute | solution.py:582
  6.2 1.3 %collective-permute-start.6 = (bf16[272,128]{1,0:T(8,128)(2,1)S(1)}, bf16[272,128]{1,0:T(8,128)(2,1)S(1)}, u32[]{:S(2)}, u32[]{:S(2)}) collective-permute-start(bf16[272,128]{1,0:T(8,128)(2,1)S(1)} %pack.1.refs_0_), channel_id=1, source_target_pairs={{0,12},{2,14},{4,8},{6,10},{8,4},{10,6},{12,0},{14,2},{1,13},{3,15... | collective-permute-start | bytes 208904 | tf_op jit(solution)/shard_map/ppermute | solution.py:582
  7.6 1.5 %collective-permute-start.1 = (bf16[272,128]{1,0:T(8,128)(2,1)S(1)}, bf16[272,128]{1,0:T(8,128)(2,1)S(1)}, u32[]{:S(2)}, u32[]{:S(2)}) collective-permute-start(bf16[272,128]{1,0:T(8,128)(2,1)S(1)} %pack.1.refs_0_), channel_id=1, source_target_pairs={{0,1},{1,0},{2,3},{3,2},{4,5},{5,4},{6,7},{7,6},{8,9},{9,8},{10,11... | collective-permute-start | bytes 208904 | tf_op jit(solution)/shard_map/ppermute | solution.py:582
  9.1 0.2 collective-permute-start.2
  9.3 1.8 %collective-permute-start.3 = (bf16[272,128]{1,0:T(8,128)(2,1)S(1)}, bf16[272,128]{1,0:T(8,128)(2,1)S(1)}, u32[]{:S(2)}, u32[]{:S(2)}) collective-permute-start(bf16[272,128]{1,0:T(8,128)(2,1)S(1)} %pack.1.refs_0_), channel_id=1, source_target_pairs={{0,5},{1,4},{2,7},{3,6},{4,1},{5,0},{6,3},{7,2},{8,13},{9,12},{10,... | collective-permute-start | bytes 208904 | tf_op jit(solution)/shard_map/ppermute | solution.py:582
  11.1 0.0 collective-permute-done.4.refs_4_
  11.1 1.9 %collective-permute-start.5 = (bf16[272,128]{1,0:T(8,128)(2,1)S(1)}, bf16[272,128]{1,0:T(8,128)(2,1)S(1)}, u32[]{:S(2)}, u32[]{:S(2)}) collective-permute-start(bf16[272,128]{1,0:T(8,128)(2,1)S(1)} %collective-permute-done.4.refs_4_), channel_id=1, source_target_pairs={{0,1},{1,0},{2,3},{3,2},{4,5},{5,4},{6,7},{7,6},{8,9},{9,8},{10,11... | collective-permute-start | bytes 208904 | tf_op jit(solution)/shard_map/ppermute | solution.py:582
  13.0 0.0 collective-permute-done.6.refs_6_
  13.0 1.2 %collective-permute-start.7 = (bf16[272,128]{1,0:T(8,128)(2,1)S(1)}, bf16[272,128]{1,0:T(8,128)(2,1)S(1)}, u32[]{:S(2)}, u32[]{:S(2)}) collective-permute-start(bf16[272,128]{1,0:T(8,128)(2,1)S(1)} %collective-permute-done.6.refs_6_), channel_id=1, source_target_pairs={{0,1},{1,0},{2,3},{3,2},{4,5},{5,4},{6,7},{7,6},{8,9},{9,8},{10,11... | collective-permute-start | bytes 208904 | tf_op jit(solution)/shard_map/ppermute | solution.py:582
  14.2 1.8 %prepare.1 = (f32[64,128]{1,0:T(8,128)S(1)}, f32[64,128]{1,0:T(8,128)S(1)}, f32[128,128]{1,0:T(8,128)S(1)}, f32[50,16]{1,0:T(8,128)S(1)}, bf16[8,128,64]{2,1,0:T...) custom-call(bf16[272,128]{1,0:T(8,128)(2,1)S(1)} %pack.1.refs_0_, ...), custom_call_target="tpu_custom_call" | custom-call | tf_op jit(solution)/shard_map/prepare/pallas_call | solution.py:160
  16.1 0.0 collective-permute-done.1.refs_1_
  16.1 0.0 collective-permute-done.2.refs_2_
  16.1 0.0 collective-permute-done.3.refs_3_
  16.1 0.7 %collective-permute-done.5.refs_5_ = bf16[272,128]{1,0:T(8,128)(2,1)S(1)} collective-permute-done((bf16[272,128]{1,0:T(8,128)(2,1)S(1)}, bf16[272,128]{1,0:T(8,128)(2,1)S(1)}, u32[]{:S(2)}, u32[]{:S(2)}) %collective-permute-start.5) | collective-permute-done | bytes 69664 | tf_op jit(solution)/shard_map/ppermute | solution.py:582
  16.8 0.7 %collective-permute-done.7.refs_7_ = bf16[272,128]{1,0:T(8,128)(2,1)S(1)} collective-permute-done((bf16[272,128]{1,0:T(8,128)(2,1)S(1)}, bf16[272,128]{1,0:T(8,128)(2,1)S(1)}, u32[]{:S(2)}, u32[]{:S(2)}) %collective-permute-start.7) | collective-permute-done | bytes 69664 | tf_op jit(solution)/shard_map/ppermute | solution.py:582
  17.5 2.6 %edges.1 = (f32[4,8,2,4,8,128]{5,4,3,2,1,0:T(8,128)S(1)}, bf16[4,8,2,32,128]{4,3,2,1,0:T(8,128)(2,1)S(1)}, bf16[4,8,2,32,128]{4,3,2,1,0:T(8,128)(2,1)S(1)}) custom-call(bf16[272,128]{1,0:T(8,128)(2,1)S(1)} %pack.1.refs_0_, bf16[272,128]{1,0:T(8,128)(2,1)S(1)} %collective-permute-done.1.refs_1_, bf16[272,128]{1,0:T(8,128)(2,1)S(1)} %collective-permute-done.2.refs_2_, ...), custom_call_target="tpu_custom_call" | custom-call | tf_op jit(solution)/shard_map/edges/pallas_call | solution.py:160
  20.1 0.1 collective-permute-start.8
  20.2 1.4 %left.1 = (f32[4128,64]{1,0:T(8,128)S(1)}, f32[4128,64]{1,0:T(8,128)S(1)}, f32[4128,32]{1,0:T(8,128)S(1)}, f32[4,8,2,4,8,128]{5,4,3,2,1,0:T(8,128)S(1)}) custom-call(bf16[4,8,2,32,128]{4,3,2,1,0:T(8,128)(2,1)S(1)} %get-tuple-element.40.normed_ref, bf16[4,8,2,32,128]{4,3,2,1,0:T(8,128)(2,1)S(1)} %get-tuple-element.41.right_ref, ...), custom_call_target="tpu_custom_call" | custom-call | tf_op jit(solution)/shard_map/left/pallas_call | solution.py:160
  21.6 0.5 %collective-permute-done.8.other_ref = bf16[4,8,2,32,128]{4,3,2,1,0:T(8,128)(2,1)S(1)} collective-permute-done((bf16[4,8,2,32,128]{4,3,2,1,0:T(8,128)(2,1)S(1)}, bf16[4,8,2,32,128]{4,3,2,1,0:T(8,128)(2,1)S(1)}, u32[]{:S(2)}, u32[]{:S(2)}) %collective-permute-start.8) | collective-permute-done | bytes 524320 | tf_op jit(solution)/shard_map/ppermute | solution.py:582
  22.1 2.2 %triangle.1 = (f32[32,128]{1,0:T(8,128)S(1)}, f32[8,4,2,8,128]{4,3,2,1,0:T(8,128)S(1)}) custom-call(f32[4128,64]{1,0:T(8,128)S(1)} %get-tuple-element.42.left_ref, f32[4128,64]{1,0:T(8,128)S(1)} %get-tuple-element.43.mine_keys_ref, f32[4128,32]{1,0:T(8,128)S(1)} %get-tuple-element.44.mine_ref, ...), custom_call_target="tpu_custom_call" | custom-call | tf_op jit(solution)/shard_map/triangle/pallas_call | solution.py:160
  24.3 0.2 collective-permute-start.9
  24.5 1.0 %scores.1 = (f32[8,32]{1,0:T(8,128)}, f32[1,8]{1,0:T(1,128)}) custom-call(f32[8,4,2,8,128]{4,3,2,1,0:T(8,128)S(1)} %get-tuple-element.48.refs_0_, bf16[64,128]{1,0:T(8,128)(2,1)S(1)} %get-tuple-element.49.refs_1_, s32[1,64]{1,0:T(1,128)S(1)} %get-tuple-element.38.refs_13_.mask_ref.refs_2_, s32[1,64]{1,0:T(1,128)S(1)} %get-tuple-element.50.refs_3_), custom_call_target="tpu_custom_call" | custom-call | tf_op jit(solution)/shard_map/scores/pallas_call | solution.py:160
  25.5 0.1 collective-permute-done.9.other_ref
  25.5 1.2 %atoms.1 = f32[1,16]{1,0:T(1,128)} custom-call(f32[32,128]{1,0:T(8,128)S(1)} %get-tuple-element.53.mine_ref, f32[32,128]{1,0:T(8,128)S(1)} %collective-permute-done.9.other_ref, bf16[64,384]{1,0:T(8,128)(2,1)S(1)} %get-tuple-element.54.single_ref, s32[1,64]{1,0:T(1,128)S(1)} %get-tuple-element.38.refs_13_.mask_ref.refs_2_, ...), custom_call_target="tpu_custom_call" | custom-call | tf_op jit(solution)/shard_map/atoms/pallas_call | solution.py:160
Async XLA Ops:
  0.6 1.6 %collective-permute-start = (f32[3,16]{1,0:T(4,128)}, f32[3,16]{1,0:T(4,128)S(1)}, u32[]{:S(2)}, u32[]{:S(2)}) collective-permute-start(f32[3,16]{1,0:T(4,128)} %coords_ref.1), channel_id=1, source_target_pairs={{0,2},{2,0},{4,6},{6,4},{8,10},{10,8},{12,14},{14,12},{1,3},{3,1},... | collective-permute-start | bytes 584 | tf_op jit(solution)/shard_map/ppermute | solution.py:582
  2.3 8.8 %collective-permute-start.4 = (bf16[272,128]{1,0:T(8,128)(2,1)S(1)}, bf16[272,128]{1,0:T(8,128)(2,1)S(1)}, u32[]{:S(2)}, u32[]{:S(2)}) collective-permute-start(bf16[272,128]{1,0:T(8,128)(2,1)S(1)} %pack.1.refs_0_), channel_id=1, source_target_pairs={{0,8},{2,10},{4,12},{6,14},{8,0},{10,2},{12,4},{14,6},{1,9},{3,11}... | collective-permute-start | bytes 208904 | tf_op jit(solution)/shard_map/ppermute | solution.py:582
  6.2 6.8 %collective-permute-start.6 = (bf16[272,128]{1,0:T(8,128)(2,1)S(1)}, bf16[272,128]{1,0:T(8,128)(2,1)S(1)}, u32[]{:S(2)}, u32[]{:S(2)}) collective-permute-start(bf16[272,128]{1,0:T(8,128)(2,1)S(1)} %pack.1.refs_0_), channel_id=1, source_target_pairs={{0,12},{2,14},{4,8},{6,10},{8,4},{10,6},{12,0},{14,2},{1,13},{3,15... | collective-permute-start | bytes 208904 | tf_op jit(solution)/shard_map/ppermute | solution.py:582
  7.6 8.5 %collective-permute-start.1 = (bf16[272,128]{1,0:T(8,128)(2,1)S(1)}, bf16[272,128]{1,0:T(8,128)(2,1)S(1)}, u32[]{:S(2)}, u32[]{:S(2)}) collective-permute-start(bf16[272,128]{1,0:T(8,128)(2,1)S(1)} %pack.1.refs_0_), channel_id=1, source_target_pairs={{0,1},{1,0},{2,3},{3,2},{4,5},{5,4},{6,7},{7,6},{8,9},{9,8},{10,11... | collective-permute-start | bytes 208904 | tf_op jit(solution)/shard_map/ppermute | solution.py:582
  9.1 7.0 %collective-permute-start.2 = (bf16[272,128]{1,0:T(8,128)(2,1)S(1)}, bf16[272,128]{1,0:T(8,128)(2,1)S(1)}, u32[]{:S(2)}, u32[]{:S(2)}) collective-permute-start(bf16[272,128]{1,0:T(8,128)(2,1)S(1)} %pack.1.refs_0_), channel_id=1, source_target_pairs={{0,4},{2,6},{4,0},{6,2},{8,12},{10,14},{12,8},{14,10},{1,5},{3,7},... | collective-permute-start | bytes 208904 | tf_op jit(solution)/shard_map/ppermute | solution.py:582
  9.3 6.8 %collective-permute-start.3 = (bf16[272,128]{1,0:T(8,128)(2,1)S(1)}, bf16[272,128]{1,0:T(8,128)(2,1)S(1)}, u32[]{:S(2)}, u32[]{:S(2)}) collective-permute-start(bf16[272,128]{1,0:T(8,128)(2,1)S(1)} %pack.1.refs_0_), channel_id=1, source_target_pairs={{0,5},{1,4},{2,7},{3,6},{4,1},{5,0},{6,3},{7,2},{8,13},{9,12},{10,... | collective-permute-start | bytes 208904 | tf_op jit(solution)/shard_map/ppermute | solution.py:582
  11.1 5.7 %collective-permute-start.5 = (bf16[272,128]{1,0:T(8,128)(2,1)S(1)}, bf16[272,128]{1,0:T(8,128)(2,1)S(1)}, u32[]{:S(2)}, u32[]{:S(2)}) collective-permute-start(bf16[272,128]{1,0:T(8,128)(2,1)S(1)} %collective-permute-done.4.refs_4_), channel_id=1, source_target_pairs={{0,1},{1,0},{2,3},{3,2},{4,5},{5,4},{6,7},{7,6},{8,9},{9,8},{10,11... | collective-permute-start | bytes 208904 | tf_op jit(solution)/shard_map/ppermute | solution.py:582
  13.0 4.5 %collective-permute-start.7 = (bf16[272,128]{1,0:T(8,128)(2,1)S(1)}, bf16[272,128]{1,0:T(8,128)(2,1)S(1)}, u32[]{:S(2)}, u32[]{:S(2)}) collective-permute-start(bf16[272,128]{1,0:T(8,128)(2,1)S(1)} %collective-permute-done.6.refs_6_), channel_id=1, source_target_pairs={{0,1},{1,0},{2,3},{3,2},{4,5},{5,4},{6,7},{7,6},{8,9},{9,8},{10,11... | collective-permute-start | bytes 208904 | tf_op jit(solution)/shard_map/ppermute | solution.py:582
  20.1 2.0 %collective-permute-start.8 = (bf16[4,8,2,32,128]{4,3,2,1,0:T(8,128)(2,1)S(1)}, bf16[4,8,2,32,128]{4,3,2,1,0:T(8,128)(2,1)S(1)}, u32[]{:S(2)}, u32[]{:S(2)}) collective-permute-start(bf16[4,8,2,32,128]{4,3,2,1,0:T(8,128)(2,1)S(1)} %get-tuple-element.41.right_ref), channel_id=1, source_target_pairs={{0,2},{2,0},{4,6},{6,4},{8,10},{10,8},{12,14},{14,12},{1,3},{3,1},... | collective-permute-start | bytes 1572872 | tf_op jit(solution)/shard_map/ppermute | solution.py:582
  24.3 1.2 %collective-permute-start.9 = (f32[32,128]{1,0:T(8,128)S(1)}, f32[32,128]{1,0:T(8,128)S(1)}, u32[]{:S(2)}, u32[]{:S(2)}) collective-permute-start(f32[32,128]{1,0:T(8,128)S(1)} %get-tuple-element.53.mine_ref), channel_id=1, source_target_pairs={{0,2},{2,0},{4,6},{6,4},{8,10},{10,8},{12,14},{14,12},{1,3},{3,1},... | collective-permute-start | bytes 49160 | tf_op jit(solution)/shard_map/ppermute | solution.py:582

commit v7 on v6

--- a/solution.py
+++ b/solution.py
@@ -147,6 +147,7 @@
 
 WHOLE_PAIR_BYTES = 4 * 1024 * 1024
 SPREAD = 1
+GROUP = 4
 SCOPED_BYTES = 16 * 1024 * 1024
 VMEM = pl.BlockSpec(memory_space=pltpu.VMEM)
 
@@ -430,28 +431,28 @@
     token = 2 * place - lax.rem(place, tile_rows) + key_half * tile_rows
     real = jnp.where(token < token_count(mask_ref).astype(jnp.int32), 1.0, 0.0)
     tri_out = tri_out_ref[...]
-    for at_chip in range(chips):
+    for first in range(0, queries, GROUP):
         change = jnp.dot(
             jnp.concatenate(
                 [
-                    normed_columns(
-                        outer_ref[pl.ds((at_chip * tile_rows + i) * step, width), :]
-                    ).T
-                    for i in range(tile_rows)
+                    normed_columns(outer_ref[pl.ds(row * step, width), :]).T
+                    for row in range(first, first + GROUP)
                 ],
                 axis=0,
             ),
             tri_out,
             preferred_element_type=jnp.float32,
         )
-        for i in range(tile_rows):
-            gating = gating_ref[at_chip, i].reshape(tokens, width)
-            updated = pair_ref[at_chip, i].reshape(tokens, width) + gating * (
+        for i in range(GROUP):
+            at_chip, at_row = divmod(first + i, tile_rows)
+            gating = gating_ref[at_chip, at_row].reshape(tokens, width)
+            updated = pair_ref[at_chip, at_row].reshape(tokens, width) + gating * (
                 change[i * tokens : (i + 1) * tokens]
             )
-            updated_ref[at_chip, i] = updated.reshape(2, chips, tile_rows, width)
-            row = at_chip * tile_rows + i
-            pooled_ref[row : row + 1, :] = jnp.sum(updated * real, axis=0, keepdims=True)
+            updated_ref[at_chip, at_row] = updated.reshape(2, chips, tile_rows, width)
+            pooled_ref[first + i : first + i + 1, :] = jnp.sum(
+                updated * real, axis=0, keepdims=True
+            )
     own_ref[:, :, half] = updated_ref[chip, :, 0]
     own_ref[:, :, 1 - half] = updated_ref[chip, :, 1]
 

time: 26.9 us -> 26.9 us (level)
  no operation moved by 1% of the time
where the time goes in v7:
time: 26.9 us; the launch traced here: 26.7 us
  starting transfers between devices  12.8 us (48%)
  Pallas kernels  11.1 us (41%)
  waiting for transfers between devices  2.12 us (8%)
  between operations  0.7 us (3%)
    ppermute x10, starting transfers between devices, across(): return lax.ppermute(values, axis, [(i, i ^ step) for i in range(count)])  12.8 us
    pallas_call x8, Pallas kernels, run(): pl.pallas_call(kernel, out_shape=out_shapes, in_specs=[VMEM] * held + [HB...  11.1 us
    ppermute x10, waiting for transfers between devices, across(): return lax.ppermute(values, axis, [(i, i ^ step) for i in range(count)])  2.12 us
  transfers between devices with their start and end apart: 10, of which 5 were waited for; matrix products, arithmetic and copies ran while one was open for 0% of the time, Pallas kernels for 19%

profile of v7, /device:TPU:0, one launch (start us, length us, event | category | flops | bytes accessed | tf_op | source)
XLA Modules:
  0.0 26.7 jit_solution(3174739155547773428)
XLA Ops:
  0.6 0.6 %collective-permute-start = (f32[3,16]{1,0:T(4,128)}, f32[3,16]{1,0:T(4,128)S(1)}, u32[]{:S(2)}, u32[]{:S(2)}) collective-permute-start(f32[3,16]{1,0:T(4,128)} %coords_ref.1), channel_id=1, source_target_pairs={{0,2},{2,0},{4,6},{6,4},{8,10},{10,8},{12,14},{14,12},{1,3},{3,1},... | collective-permute-start | bytes 584 | tf_op jit(solution)/shard_map/ppermute | solution.py:583
  1.2 0.9 %fetch.1 = (bf16[272,128]{1,0:T(8,128)(2,1)S(1)}, f32[3,16]{1,0:T(4,128)S(1)}) custom-call(bf16[256,128]{1,0:T(8,128)(2,1)} %bitcast.10, f32[3,16]{1,0:T(4,128)} %coords_ref.1), custom_call_target="tpu_custom_call" | custom-call | tf_op jit(solution)/shard_map/fetch/pallas_call | solution.py:161
  2.1 0.2 collective-permute-done.other_ref
  2.2 0.1 pack.1.refs_0_
  2.3 3.9 %collective-permute-start.4 = (bf16[272,128]{1,0:T(8,128)(2,1)S(1)}, bf16[272,128]{1,0:T(8,128)(2,1)S(1)}, u32[]{:S(2)}, u32[]{:S(2)}) collective-permute-start(bf16[272,128]{1,0:T(8,128)(2,1)S(1)} %pack.1.refs_0_), channel_id=1, source_target_pairs={{0,8},{2,10},{4,12},{6,14},{8,0},{10,2},{12,4},{14,6},{1,9},{3,11}... | collective-permute-start | bytes 208904 | tf_op jit(solution)/shard_map/ppermute | solution.py:583
  6.2 1.3 %collective-permute-start.6 = (bf16[272,128]{1,0:T(8,128)(2,1)S(1)}, bf16[272,128]{1,0:T(8,128)(2,1)S(1)}, u32[]{:S(2)}, u32[]{:S(2)}) collective-permute-start(bf16[272,128]{1,0:T(8,128)(2,1)S(1)} %pack.1.refs_0_), channel_id=1, source_target_pairs={{0,12},{2,14},{4,8},{6,10},{8,4},{10,6},{12,0},{14,2},{1,13},{3,15... | collective-permute-start | bytes 208904 | tf_op jit(solution)/shard_map/ppermute | solution.py:583
  7.6 1.5 %collective-permute-start.1 = (bf16[272,128]{1,0:T(8,128)(2,1)S(1)}, bf16[272,128]{1,0:T(8,128)(2,1)S(1)}, u32[]{:S(2)}, u32[]{:S(2)}) collective-permute-start(bf16[272,128]{1,0:T(8,128)(2,1)S(1)} %pack.1.refs_0_), channel_id=1, source_target_pairs={{0,1},{1,0},{2,3},{3,2},{4,5},{5,4},{6,7},{7,6},{8,9},{9,8},{10,11... | collective-permute-start | bytes 208904 | tf_op jit(solution)/shard_map/ppermute | solution.py:583
  9.1 0.2 collective-permute-start.2
  9.3 1.8 %collective-permute-start.3 = (bf16[272,128]{1,0:T(8,128)(2,1)S(1)}, bf16[272,128]{1,0:T(8,128)(2,1)S(1)}, u32[]{:S(2)}, u32[]{:S(2)}) collective-permute-start(bf16[272,128]{1,0:T(8,128)(2,1)S(1)} %pack.1.refs_0_), channel_id=1, source_target_pairs={{0,5},{1,4},{2,7},{3,6},{4,1},{5,0},{6,3},{7,2},{8,13},{9,12},{10,... | collective-permute-start | bytes 208904 | tf_op jit(solution)/shard_map/ppermute | solution.py:583
  11.1 0.0 collective-permute-done.4.refs_4_
  11.1 1.9 %collective-permute-start.5 = (bf16[272,128]{1,0:T(8,128)(2,1)S(1)}, bf16[272,128]{1,0:T(8,128)(2,1)S(1)}, u32[]{:S(2)}, u32[]{:S(2)}) collective-permute-start(bf16[272,128]{1,0:T(8,128)(2,1)S(1)} %collective-permute-done.4.refs_4_), channel_id=1, source_target_pairs={{0,1},{1,0},{2,3},{3,2},{4,5},{5,4},{6,7},{7,6},{8,9},{9,8},{10,11... | collective-permute-start | bytes 208904 | tf_op jit(solution)/shard_map/ppermute | solution.py:583
  13.0 0.0 collective-permute-done.6.refs_6_
  13.0 1.2 %collective-permute-start.7 = (bf16[272,128]{1,0:T(8,128)(2,1)S(1)}, bf16[272,128]{1,0:T(8,128)(2,1)S(1)}, u32[]{:S(2)}, u32[]{:S(2)}) collective-permute-start(bf16[272,128]{1,0:T(8,128)(2,1)S(1)} %collective-permute-done.6.refs_6_), channel_id=1, source_target_pairs={{0,1},{1,0},{2,3},{3,2},{4,5},{5,4},{6,7},{7,6},{8,9},{9,8},{10,11... | collective-permute-start | bytes 208904 | tf_op jit(solution)/shard_map/ppermute | solution.py:583
  14.2 1.8 %prepare.1 = (f32[64,128]{1,0:T(8,128)S(1)}, f32[64,128]{1,0:T(8,128)S(1)}, f32[128,128]{1,0:T(8,128)S(1)}, f32[50,16]{1,0:T(8,128)S(1)}, bf16[8,128,64]{2,1,0:T...) custom-call(bf16[272,128]{1,0:T(8,128)(2,1)S(1)} %pack.1.refs_0_, ...), custom_call_target="tpu_custom_call" | custom-call | tf_op jit(solution)/shard_map/prepare/pallas_call | solution.py:161
  16.1 0.0 collective-permute-done.1.refs_1_
  16.1 0.0 collective-permute-done.2.refs_2_
  16.1 0.0 collective-permute-done.3.refs_3_
  16.1 0.7 %collective-permute-done.5.refs_5_ = bf16[272,128]{1,0:T(8,128)(2,1)S(1)} collective-permute-done((bf16[272,128]{1,0:T(8,128)(2,1)S(1)}, bf16[272,128]{1,0:T(8,128)(2,1)S(1)}, u32[]{:S(2)}, u32[]{:S(2)}) %collective-permute-start.5) | collective-permute-done | bytes 69664 | tf_op jit(solution)/shard_map/ppermute | solution.py:583
  16.8 0.7 %collective-permute-done.7.refs_7_ = bf16[272,128]{1,0:T(8,128)(2,1)S(1)} collective-permute-done((bf16[272,128]{1,0:T(8,128)(2,1)S(1)}, bf16[272,128]{1,0:T(8,128)(2,1)S(1)}, u32[]{:S(2)}, u32[]{:S(2)}) %collective-permute-start.7) | collective-permute-done | bytes 69664 | tf_op jit(solution)/shard_map/ppermute | solution.py:583
  17.5 2.6 %edges.1 = (f32[4,8,2,4,8,128]{5,4,3,2,1,0:T(8,128)S(1)}, bf16[4,8,2,32,128]{4,3,2,1,0:T(8,128)(2,1)S(1)}, bf16[4,8,2,32,128]{4,3,2,1,0:T(8,128)(2,1)S(1)}) custom-call(bf16[272,128]{1,0:T(8,128)(2,1)S(1)} %pack.1.refs_0_, bf16[272,128]{1,0:T(8,128)(2,1)S(1)} %collective-permute-done.1.refs_1_, bf16[272,128]{1,0:T(8,128)(2,1)S(1)} %collective-permute-done.2.refs_2_, ...), custom_call_target="tpu_custom_call" | custom-call | tf_op jit(solution)/shard_map/edges/pallas_call | solution.py:161
  20.1 0.1 collective-permute-start.8
  20.2 1.4 %left.1 = (f32[4128,64]{1,0:T(8,128)S(1)}, f32[4128,64]{1,0:T(8,128)S(1)}, f32[4128,32]{1,0:T(8,128)S(1)}, f32[4,8,2,4,8,128]{5,4,3,2,1,0:T(8,128)S(1)}) custom-call(bf16[4,8,2,32,128]{4,3,2,1,0:T(8,128)(2,1)S(1)} %get-tuple-element.40.normed_ref, bf16[4,8,2,32,128]{4,3,2,1,0:T(8,128)(2,1)S(1)} %get-tuple-element.41.right_ref, ...), custom_call_target="tpu_custom_call" | custom-call | tf_op jit(solution)/shard_map/left/pallas_call | solution.py:161
  21.6 0.5 %collective-permute-done.8.other_ref = bf16[4,8,2,32,128]{4,3,2,1,0:T(8,128)(2,1)S(1)} collective-permute-done((bf16[4,8,2,32,128]{4,3,2,1,0:T(8,128)(2,1)S(1)}, bf16[4,8,2,32,128]{4,3,2,1,0:T(8,128)(2,1)S(1)}, u32[]{:S(2)}, u32[]{:S(2)}) %collective-permute-start.8) | collective-permute-done | bytes 524320 | tf_op jit(solution)/shard_map/ppermute | solution.py:583
  22.1 2.2 %triangle.1 = (f32[32,128]{1,0:T(8,128)S(1)}, f32[8,4,2,8,128]{4,3,2,1,0:T(8,128)S(1)}) custom-call(f32[4128,64]{1,0:T(8,128)S(1)} %get-tuple-element.42.left_ref, f32[4128,64]{1,0:T(8,128)S(1)} %get-tuple-element.43.mine_keys_ref, f32[4128,32]{1,0:T(8,128)S(1)} %get-tuple-element.44.mine_ref, ...), custom_call_target="tpu_custom_call" | custom-call | tf_op jit(solution)/shard_map/triangle/pallas_call | solution.py:161
  24.2 0.2 collective-permute-start.9
  24.4 1.0 %scores.1 = (f32[8,32]{1,0:T(8,128)}, f32[1,8]{1,0:T(1,128)}) custom-call(f32[8,4,2,8,128]{4,3,2,1,0:T(8,128)S(1)} %get-tuple-element.48.refs_0_, bf16[64,128]{1,0:T(8,128)(2,1)S(1)} %get-tuple-element.49.refs_1_, s32[1,64]{1,0:T(1,128)S(1)} %get-tuple-element.38.refs_13_.mask_ref.refs_2_, s32[1,64]{1,0:T(1,128)S(1)} %get-tuple-element.50.refs_3_), custom_call_target="tpu_custom_call" | custom-call | tf_op jit(solution)/shard_map/scores/pallas_call | solution.py:161
  25.4 0.1 collective-permute-done.9.other_ref
  25.5 1.2 %atoms.1 = f32[1,16]{1,0:T(1,128)} custom-call(f32[32,128]{1,0:T(8,128)S(1)} %get-tuple-element.53.mine_ref, f32[32,128]{1,0:T(8,128)S(1)} %collective-permute-done.9.other_ref, bf16[64,384]{1,0:T(8,128)(2,1)S(1)} %get-tuple-element.54.single_ref, s32[1,64]{1,0:T(1,128)S(1)} %get-tuple-element.38.refs_13_.mask_ref.refs_2_, ...), custom_call_target="tpu_custom_call" | custom-call | tf_op jit(solution)/shard_map/atoms/pallas_call | solution.py:161
Async XLA Ops:
  0.6 1.6 %collective-permute-start = (f32[3,16]{1,0:T(4,128)}, f32[3,16]{1,0:T(4,128)S(1)}, u32[]{:S(2)}, u32[]{:S(2)}) collective-permute-start(f32[3,16]{1,0:T(4,128)} %coords_ref.1), channel_id=1, source_target_pairs={{0,2},{2,0},{4,6},{6,4},{8,10},{10,8},{12,14},{14,12},{1,3},{3,1},... | collective-permute-start | bytes 584 | tf_op jit(solution)/shard_map/ppermute | solution.py:583
  2.3 8.8 %collective-permute-start.4 = (bf16[272,128]{1,0:T(8,128)(2,1)S(1)}, bf16[272,128]{1,0:T(8,128)(2,1)S(1)}, u32[]{:S(2)}, u32[]{:S(2)}) collective-permute-start(bf16[272,128]{1,0:T(8,128)(2,1)S(1)} %pack.1.refs_0_), channel_id=1, source_target_pairs={{0,8},{2,10},{4,12},{6,14},{8,0},{10,2},{12,4},{14,6},{1,9},{3,11}... | collective-permute-start | bytes 208904 | tf_op jit(solution)/shard_map/ppermute | solution.py:583
  6.2 6.8 %collective-permute-start.6 = (bf16[272,128]{1,0:T(8,128)(2,1)S(1)}, bf16[272,128]{1,0:T(8,128)(2,1)S(1)}, u32[]{:S(2)}, u32[]{:S(2)}) collective-permute-start(bf16[272,128]{1,0:T(8,128)(2,1)S(1)} %pack.1.refs_0_), channel_id=1, source_target_pairs={{0,12},{2,14},{4,8},{6,10},{8,4},{10,6},{12,0},{14,2},{1,13},{3,15... | collective-permute-start | bytes 208904 | tf_op jit(solution)/shard_map/ppermute | solution.py:583
  7.6 8.5 %collective-permute-start.1 = (bf16[272,128]{1,0:T(8,128)(2,1)S(1)}, bf16[272,128]{1,0:T(8,128)(2,1)S(1)}, u32[]{:S(2)}, u32[]{:S(2)}) collective-permute-start(bf16[272,128]{1,0:T(8,128)(2,1)S(1)} %pack.1.refs_0_), channel_id=1, source_target_pairs={{0,1},{1,0},{2,3},{3,2},{4,5},{5,4},{6,7},{7,6},{8,9},{9,8},{10,11... | collective-permute-start | bytes 208904 | tf_op jit(solution)/shard_map/ppermute | solution.py:583
  9.1 7.0 %collective-permute-start.2 = (bf16[272,128]{1,0:T(8,128)(2,1)S(1)}, bf16[272,128]{1,0:T(8,128)(2,1)S(1)}, u32[]{:S(2)}, u32[]{:S(2)}) collective-permute-start(bf16[272,128]{1,0:T(8,128)(2,1)S(1)} %pack.1.refs_0_), channel_id=1, source_target_pairs={{0,4},{2,6},{4,0},{6,2},{8,12},{10,14},{12,8},{14,10},{1,5},{3,7},... | collective-permute-start | bytes 208904 | tf_op jit(solution)/shard_map/ppermute | solution.py:583
  9.3 6.8 %collective-permute-start.3 = (bf16[272,128]{1,0:T(8,128)(2,1)S(1)}, bf16[272,128]{1,0:T(8,128)(2,1)S(1)}, u32[]{:S(2)}, u32[]{:S(2)}) collective-permute-start(bf16[272,128]{1,0:T(8,128)(2,1)S(1)} %pack.1.refs_0_), channel_id=1, source_target_pairs={{0,5},{1,4},{2,7},{3,6},{4,1},{5,0},{6,3},{7,2},{8,13},{9,12},{10,... | collective-permute-start | bytes 208904 | tf_op jit(solution)/shard_map/ppermute | solution.py:583
  11.1 5.7 %collective-permute-start.5 = (bf16[272,128]{1,0:T(8,128)(2,1)S(1)}, bf16[272,128]{1,0:T(8,128)(2,1)S(1)}, u32[]{:S(2)}, u32[]{:S(2)}) collective-permute-start(bf16[272,128]{1,0:T(8,128)(2,1)S(1)} %collective-permute-done.4.refs_4_), channel_id=1, source_target_pairs={{0,1},{1,0},{2,3},{3,2},{4,5},{5,4},{6,7},{7,6},{8,9},{9,8},{10,11... | collective-permute-start | bytes 208904 | tf_op jit(solution)/shard_map/ppermute | solution.py:583
  13.0 4.5 %collective-permute-start.7 = (bf16[272,128]{1,0:T(8,128)(2,1)S(1)}, bf16[272,128]{1,0:T(8,128)(2,1)S(1)}, u32[]{:S(2)}, u32[]{:S(2)}) collective-permute-start(bf16[272,128]{1,0:T(8,128)(2,1)S(1)} %collective-permute-done.6.refs_6_), channel_id=1, source_target_pairs={{0,1},{1,0},{2,3},{3,2},{4,5},{5,4},{6,7},{7,6},{8,9},{9,8},{10,11... | collective-permute-start | bytes 208904 | tf_op jit(solution)/shard_map/ppermute | solution.py:583
  20.1 2.0 %collective-permute-start.8 = (bf16[4,8,2,32,128]{4,3,2,1,0:T(8,128)(2,1)S(1)}, bf16[4,8,2,32,128]{4,3,2,1,0:T(8,128)(2,1)S(1)}, u32[]{:S(2)}, u32[]{:S(2)}) collective-permute-start(bf16[4,8,2,32,128]{4,3,2,1,0:T(8,128)(2,1)S(1)} %get-tuple-element.41.right_ref), channel_id=1, source_target_pairs={{0,2},{2,0},{4,6},{6,4},{8,10},{10,8},{12,14},{14,12},{1,3},{3,1},... | collective-permute-start | bytes 1572872 | tf_op jit(solution)/shard_map/ppermute | solution.py:583
  24.2 1.2 %collective-permute-start.9 = (f32[32,128]{1,0:T(8,128)S(1)}, f32[32,128]{1,0:T(8,128)S(1)}, u32[]{:S(2)}, u32[]{:S(2)}) collective-permute-start(f32[32,128]{1,0:T(8,128)S(1)} %get-tuple-element.53.mine_ref), channel_id=1, source_target_pairs={{0,2},{2,0},{4,6},{6,4},{8,10},{10,8},{12,14},{14,12},{1,3},{3,1},... | collective-permute-start | bytes 49160 | tf_op jit(solution)/shard_map/ppermute | solution.py:583
